TPU v7x, 256 devices: a whole 4x4x8 slice. The times are simulated.
256 devices in a mesh: grid: 128 (over y_lo, x, z, core), batch: 2 (over y_hi).
Axes of the slice: x: 4, y: 4 (y_hi: 2, y_lo: 2; y = y_hi * 2 + y_lo), z: 8, core: 2. Of those that a mesh axis runs over, the one named last changes fastest.
Arguments:
- orbitals: bfloat16 [1024, 262144], P(None, 'grid'), may hold values from -0.1875 to 0.1875
- points: int32 [2, 256], P('batch'), may hold values from 0 to 262143, as said below
Outputs:
- kernel: float32 [512, 512], P('batch', 'grid')
Inputs may be any that keep to these rules, and one draw needn't show every extreme that they name: `points`: each entry is a cell index (x * 64 + y) * 64 + z.
All inputs are finite; a program needn't handle non-finite values.
Results may differ from a plain program's by a relative error of at most 0.0006.
The roundings to bfloat16 on the way count: a program that leaves them out, or rounds other values in their place, can miss the bound.
Values may be sent and summed in bfloat16 or wider, within the bound.
No kernel may reach another device: no remote copies, remote signals or barrier semaphores. Data moves between devices by JAX's collectives and lax.ppermute only.
A program may use at most 64 MiB of HBM per device.

v0:
```python
import math

import jax
import jax.numpy as jnp
from jax import lax
from jax.sharding import PartitionSpec as P

NX = 64
NY = 64
NZ = 64


screen_rate = 0.05
kernel_scale = 16.0


def partner_2(block, axis, apart):
    count = lax.axis_size(axis)
    route = []
    for low in range(count):
        high = low | 1 << apart
        if high != low and high < count:
            route += [(low, high), (high, low)]
    return lax.ppermute(block, axis, route)


def make_tables(length):
    rows = jnp.arange(length, dtype=jnp.int32)[:, None]
    columns = jnp.arange(length, dtype=jnp.int32)[None, :]
    angles = (rows * columns % length).astype(jnp.float32) * jnp.float32(2.0 * math.pi / length)
    cosine = (jnp.cos(angles) / math.sqrt(length)).astype(jnp.bfloat16)
    sine = (jnp.sin(angles) / math.sqrt(length)).astype(jnp.bfloat16)
    return (cosine, sine)


def signed_freq(values, length):
    return jnp.where(values < length // 2, values, values - length).astype(jnp.float32)


def screen_weights(z_modes):
    mode_z = signed_freq(z_modes, NZ)[:, None, None]
    mode_x = signed_freq(jnp.arange(NX, dtype=jnp.int32), NX)[None, :, None]
    mode_y = signed_freq(jnp.arange(NY, dtype=jnp.int32), NY)[None, None, :]
    scaled = screen_rate * (mode_x * mode_x + mode_y * mode_y + mode_z * mode_z)
    positive = scaled > 0
    safe_scaled = jnp.where(positive, scaled, jnp.float32(1.0))
    return jnp.where(positive, -jnp.expm1(-safe_scaled) / safe_scaled, jnp.float32(0.0))


def plane_transform(planes):
    count = planes.shape[0]
    items = planes.shape[2]
    cos_y, sin_y = make_tables(NY)
    cos_x, sin_x = make_tables(NX)
    y_table = jnp.stack([cos_y, -sin_y])
    x_table = jnp.concatenate(
        [jnp.concatenate([cos_x, sin_x], 1), jnp.concatenate([-sin_x, cos_x], 1)], 0
    )
    layout = planes.reshape(count, NX, NY, items)
    half_y = jnp.einsum(
        "dky,cxyp->cdxkp", y_table, layout, preferred_element_type=jnp.float32
    ).astype(jnp.bfloat16)
    flat = half_y.reshape(count, 2 * NX, NY * items)
    spectra = jnp.einsum("ab,cbm->cam", x_table, flat, preferred_element_type=jnp.float32).astype(
        jnp.bfloat16
    )
    return spectra.reshape(count, 2, NX, NY, items)


def combine_parts(real_half, received, parity_sign):
    return (real_half + parity_sign * received.astype(jnp.float32)).astype(jnp.bfloat16)


def coefficient_swap(orbitals, point_values, position, batch_index, grid_count):
    contract_first = (((0,), (0,)), ((), ()))
    cells = orbitals.shape[1]
    fit_count = point_values.shape[1]
    density = lax.dot_general(
        orbitals, point_values, contract_first, preferred_element_type=jnp.float32
    )
    fitted = (density * density).astype(jnp.bfloat16).reshape(cells // NZ, NZ, fit_count)
    cos_z, sin_z = make_tables(NZ)
    z_table = jnp.concatenate([cos_z, -sin_z], 0)
    planes = jnp.einsum("kz,azp->kap", z_table, fitted, preferred_element_type=jnp.float32).astype(
        jnp.bfloat16
    )
    spectra = plane_transform(
        lax.all_to_all(planes, "grid", split_axis=0, concat_axis=1, tiled=True)
    )
    local_modes = spectra.shape[0]
    modes = position * local_modes + jnp.arange(local_modes, dtype=jnp.int32)
    real_half = spectra[:, 0].astype(jnp.float32)
    received = partner_2(spectra[:, 1], "grid", grid_count.bit_length() - 2)
    parity_sign = jnp.where(position >= grid_count // 2, jnp.float32(1.0), jnp.float32(-1.0))
    coeffs = combine_parts(real_half, received, parity_sign)
    z_modes = modes % NZ
    screen = screen_weights(z_modes)
    weighted = (coeffs.astype(jnp.float32) * screen[:, :, :, None]).astype(jnp.bfloat16)
    flat_coeffs = coeffs.reshape(-1, fit_count)
    flat_weighted = weighted.reshape(-1, fit_count)
    partner = partner_2(flat_coeffs, "batch", 0)
    own_block = (
        lax.dot_general(
            flat_weighted, flat_coeffs, contract_first, preferred_element_type=jnp.float32
        )
        * kernel_scale
    )
    cross_block = (
        lax.dot_general(flat_weighted, partner, contract_first, preferred_element_type=jnp.float32)
        * kernel_scale
    )
    leading = jnp.where(batch_index == 0, own_block, cross_block)
    trailing = jnp.where(batch_index == 0, cross_block, own_block)
    summands = jnp.concatenate([leading, trailing], 1)
    return lax.psum_scatter(summands, "grid", scatter_dimension=1, tiled=True)


def on_device(orbitals, points):
    grid_count = lax.axis_size("grid")
    position = lax.axis_index("grid")
    batch_index = lax.axis_index("batch")
    cells = orbitals.shape[1]
    offsets = points[0] - position * cells
    inside = (offsets >= 0) & (offsets < cells)
    picked = jnp.take(orbitals, jnp.clip(offsets, 0, cells - 1), axis=1).astype(jnp.float32)
    picked = picked * inside.astype(jnp.float32)[None, :]
    point_values = lax.psum(picked, "grid").astype(jnp.bfloat16)
    return coefficient_swap(orbitals, point_values, position, batch_index, grid_count)


def solution(mesh):
    return jax.shard_map(
        on_device,
        mesh=mesh,
        in_specs=(P(None, "grid"), P("batch", None)),
        out_specs=P("batch", "grid"),
        check_vma=False,
    )
```

profile of v0, /device:TPU:1, one launch (start us, length us, event | category | flops | bytes accessed | tf_op | source)
XLA Modules:
  0.0 1786.9 jit_solution(10447819909346194401)
XLA Ops:
  6.5 0.7 compare_select_fusion.2
  7.2 0.7 and_convert_fusion
  7.9 0.2 multiply_convert_fusion.4
  8.1 0.1 fusion.42
  8.2 6.4 copy.12
  14.6 4.3 gather_fusion
  18.9 0.2 multiply_bitcast_fusion
  19.1 557.5 %all-reduce.5 = bf16[1024,256]{0,1:T(8,128)(2,1)S(1)} all-reduce(f32[1024,256]{0,1:T(8,128)S(1)} %multiply_bitcast_fusion), channel_id=1, replica_groups=mesh['grid'=128,'batch'=2] {'grid'}, use_global_device_ids=true, to_apply=%region_0.1 | all-reduce | flops 262144 | bytes 1572864 | tf_op jit(solution)/shard_map/psum | solution.py:127
  576.7 3.4 fusion.3
  580.1 0.5 copy.13
  580.7 0.8 convolution_convert_fusion.1
  581.5 2.5 copy.14
  584.0 11.8 all-to-all-start
  595.8 0.2 all-reduce.4.cloned.1.call-start
  596.0 0.1 fusion.39
  596.1 0.1 multiply_convert_fusion.3
  596.3 50.1 %all-to-all-done = bf16[128,32,256]{2,1,0:T(8,128)(2,1)S(1)} async-done(((bf16[128,32,256]{2,1,0:T(8,128)(2,1)}), bf16[128,32,256]{2,1,0:T(8,128)(2,1)S(1)}, u32[]{:S(2)}, u32[]{:S(2)}) %all-to-all-start) | async-done | bytes 2097184 | tf_op jit(solution)/shard_map/all_to_all | solution.py:88
  646.4 1.2 convert_bitcast_fusion
  647.6 0.6 copy.15
  648.2 2.9 copy.18
  651.1 3.3 fusion
  654.4 6.4 copy.16
  660.8 3.4 copy.19
  664.2 0.0 copy-start
  664.3 1.9 copy-done
  666.2 0.1 slice_bitcast_fusion
  666.3 1.4 collective-permute-start
  667.7 0.1 compare_select_fusion
  667.8 44.4 %collective-permute-done = bf16[1,64,64,256]{3,2,1,0:T(8,128)(2,1)} collective-permute-done((bf16[1,64,64,256]{3,2,1,0:T(8,128)(2,1)S(1)}, bf16[1,64,64,256]{3,2,1,0:T(8,128)(2,1)}, u32[]{:S(2)}, u32[]{:S(2)}) %collective-permute-start) | collective-permute-done | bytes 2097184 | tf_op jit(solution)/shard_map/ppermute | solution.py:24
  712.2 3.6 multiply_convert_fusion
  715.8 2.6 collective-permute-start.1
  718.4 43.8 %collective-permute-done.1 = bf16[4096,256]{1,0:T(8,128)(2,1)} collective-permute-done((bf16[4096,256]{1,0:T(8,128)(2,1)S(1)}, bf16[4096,256]{1,0:T(8,128)(2,1)}, u32[]{:S(2)}, u32[]{:S(2)}) %collective-permute-start.1) | collective-permute-done | bytes 2097184 | tf_op jit(solution)/shard_map/ppermute | solution.py:24
  762.2 3.1 convolution_multiply_fusion.1
  765.4 0.0 copy-start.1
  765.4 1.4 broadcast_select_fusion.1
  766.8 0.8 pad_maximum_fusion
  767.6 0.0 all-reduce.4.cloned.1.call-update
  767.6 0.0 copy-done.1
  767.6 0.6 dynamic-slice
  768.9 1009.9 %all-reduce.4.cloned.1.call-done = f32[256,512]{0,1:T(8,128)} async-done(((f32[256,512]{0,1:T(8,128)}), f32[256,512]{0,1:T(8,128)}) %all-reduce.4.cloned.1.call-update) | async-done | bytes 524304
  1778.8 1.3 constant_dynamic-slice_fusion
  (3 shorter events, 0.0 us)
Async XLA Ops:
  584.0 62.4 %all-to-all-start = ((bf16[128,32,256]{2,1,0:T(8,128)(2,1)}), bf16[128,32,256]{2,1,0:T(8,128)(2,1)S(1)}, u32[]{:S(2)}, u32[]{:S(2)}) async-start(bf16[128,32,256]{2,1,0:T(8,128)(2,1)} %copy.14), calls=%async_computation | async-start | bytes 4194304 | tf_op jit(solution)/shard_map/all_to_all | solution.py:88
  595.8 1183.0 %all-reduce.4.cloned.1.call-start = ((), (), s32[]{:S(2)}) async-start(), calls=%async_computation.1 | async-start | bytes 1048576
  664.2 1.9 copy-start
  666.3 45.9 %collective-permute-start = (bf16[1,64,64,256]{3,2,1,0:T(8,128)(2,1)S(1)}, bf16[1,64,64,256]{3,2,1,0:T(8,128)(2,1)}, u32[]{:S(2)}, u32[]{:S(2)}) collective-permute-start(bf16[1,64,64,256]{3,2,1,0:T(8,128)(2,1)S(1)} %slice_bitcast_fusion), channel_id=1, source_target_pairs={{0,128},{128,0},{2,130},{130,2},{4,132},{132,4},{6,134},{134,6},{8... | collective-permute-start | bytes 6291464 | tf_op jit(solution)/shard_map/ppermute | solution.py:24
  715.8 46.4 %collective-permute-start.1 = (bf16[4096,256]{1,0:T(8,128)(2,1)S(1)}, bf16[4096,256]{1,0:T(8,128)(2,1)}, u32[]{:S(2)}, u32[]{:S(2)}) collective-permute-start(bf16[4096,256]{1,0:T(8,128)(2,1)S(1)} %bitcast.85), channel_id=1, source_target_pairs={{0,1},{1,0},{2,3},{3,2},{4,5},{5,4},{6,7},{7,6},{8,9},{9,8},{10,11... | collective-permute-start | bytes 6291464 | tf_op jit(solution)/shard_map/ppermute | solution.py:24
  765.4 2.3 copy-start.1
Sparse Core Ops, SparseCore 0:
  767.7 1011.0 all-reduce.3
where the time goes:
time: 1790 us
  waiting for transfers between devices  1150 us (64%)
  blocking collectives  558 us (31%)
  local copies, waits for them, and re-layouts  31 us (2%)
    unnamed x2, waiting for transfers between devices  1010 us
    psum x1, blocking collectives, on_device(): point_values = lax.psum(picked, 'grid').astype(jnp.bfloat16)  558 us
    ppermute x2, waiting for transfers between devices, partner_2(): return lax.ppermute(block, axis, route)  88.2 us
    all_to_all x1, waiting for transfers between devices, coefficient_swap(): lax.all_to_all(planes, 'grid', split_axis=0, concat_axis=1, tiled=True)  50.1 us
  transfers between devices with their start and end apart: 4, of which 4 were waited for; matrix products, arithmetic and copies ran while one was open for 0% of the time, Pallas kernels for 0%

commit v1 on v0

v1 whole, which is shorter than its diff:
```python
import math

import jax
import jax.numpy as jnp
from jax import lax
from jax.experimental import pallas as pl
from jax.experimental.pallas import tpu as pltpu
from jax.sharding import Mesh
from jax.sharding import PartitionSpec as P

N = 64
NORB = 1024
NFIT = 256
HALF = NFIT // 2

screen_rate = 0.05
kernel_scale = 16.0

CHIPS = ("yl", "x", "z")
SAME_CORE = ("yl", "x", "z", "b")
F32 = jnp.float32
BF16 = jnp.bfloat16


def signed_freq(values):
    return jnp.where(values < N // 2, values, values - N).astype(F32)


def waves(freq, place):
    angles = (freq * place % N).astype(F32) * F32(2.0 * math.pi / N)
    return jnp.cos(angles) / math.sqrt(N), jnp.sin(angles) / math.sqrt(N)


def iota(shape, dim):
    return lax.broadcasted_iota(jnp.int32, shape, dim)


def pair_table(row, place):
    pair, part = row // 2, row % 2
    freq = jnp.where((pair == 0) & (part == 1), N // 2, pair)
    cosine, sine = waves(freq, place)
    return jnp.where((part == 0) | (pair == 0), cosine, -sine)


def x_table(lone):
    row, column = iota((256, 256), 0), iota((256, 256), 1)
    z_of, e, k = row // 128, row // 64 % 2, row % 64
    z_part, y_part, place = column // 128, column // 64 % 2, column % 64
    k_low = k % 32
    turned = (e == 1) & (k_low == 0)
    freq = jnp.where(lone, jnp.where(turned, N // 2, k_low), k)
    cosine, sine = waves(freq, place)
    both = jnp.where(e == y_part, cosine, jnp.where(e == 0, sine, -sine))
    both = jnp.where(z_of == z_part, both, F32(0.0))
    single = jnp.where((e == 0) | turned, cosine, -sine)
    kept = (y_part == k // 32) & (z_part == jnp.where(turned, 1 - z_of, z_of))
    return jnp.where(lone, jnp.where(kept, single, F32(0.0)), both).astype(BF16)


def screen_rows(y_pair, z_first):
    shape = (1024, 128)
    row = iota(shape, 0)
    out, k, z_pair = row // 256, row // 4 % 64, z_first + row % 4
    lone_y, lone_z = y_pair == 0, z_pair == 0
    k_low = k % 32
    edge = lone_y & (k_low == 0)
    second = (out == 1) | (out == 3)
    kx = jnp.where(lone_y, jnp.where(edge & second, N // 2, k_low), k)
    ky = jnp.where(lone_y, jnp.where(k >= 32, N // 2, 0), y_pair)
    z_late = (out == 2) | jnp.where(edge, out == 3, out == 1)
    kz = jnp.where(lone_z, jnp.where(z_late, N // 2, 0), z_pair)
    fx, fy, fz = signed_freq(kx), signed_freq(ky), signed_freq(kz)
    scaled = screen_rate * (fx * fx + fy * fy + fz * fz)
    positive = scaled > 0
    safe = jnp.where(positive, scaled, F32(1.0))
    screen = jnp.where(positive, -jnp.expm1(-safe) / safe, F32(0.0))
    copies = jnp.where(edge & lone_z, F32(1.0), F32(2.0))
    mixed = jnp.where(lone_z | edge, F32(0.0), F32(1.0))[:256]
    return screen * copies, mixed


def expand_kernel(y_small_ref, x_small_ref, y_ref, x_ref):
    block = pl.program_id(0)
    row = 256 * block + iota((256, 1024), 0)
    column = iota((256, 1024), 1)

    def spread(small, row_of, column_of):
        r = 256 * block + iota((256, small.shape[0]), 0)
        c = iota((small.shape[1], 1024), 1)
        left = jnp.where(row_of(r) == iota(r.shape, 1), F32(1.0), F32(0.0)).astype(BF16)
        right = jnp.where(column_of(c) == iota(c.shape, 0), F32(1.0), F32(0.0)).astype(BF16)
        tall = jnp.dot(left, small, preferred_element_type=F32).astype(BF16)
        return jnp.dot(tall, right, preferred_element_type=F32)

    wide = spread(y_small_ref[...], lambda r: (r >> 5) * 2 + ((r >> 3) & 1), lambda c: c >> 4)
    same = (((row >> 4) & 1) == ((column >> 3) & 1)) & ((row & 7) == (column & 7))
    y_ref[...] = jnp.where(same, wide, F32(0.0)).astype(BF16)
    wide = spread(
        x_small_ref[...],
        lambda r: r >> 2,
        lambda c: (c & 1) * 128 + ((c >> 3) & 1) * 64 + (c >> 4),
    )
    same = (row & 3) == ((column >> 1) & 3)
    x_ref[...] = jnp.where(same, wide, F32(0.0)).astype(BF16)


def expand(y_small, x_small):
    big = jax.ShapeDtypeStruct((1024, 1024), BF16)
    return pl.pallas_call(
        expand_kernel,
        out_shape=(big, big),
        grid=(4,),
        in_specs=[
            pl.BlockSpec((N, N), lambda i: (0, 0)),
            pl.BlockSpec((256, 256), lambda i: (0, 0)),
        ],
        out_specs=[pl.BlockSpec((256, 1024), lambda i: (i, 0))] * 2,
        cost_estimate=pl.CostEstimate(flops=2**31, bytes_accessed=2**22, transcendentals=0),
        name="expand",
    )(y_small, x_small)


def pick_kernel(offsets_ref, orbitals_ref, own_ref, other_ref, hot_ref):
    @pl.when(pl.program_id(0) == 0)
    def _():
        cell = lax.broadcasted_iota(jnp.int32, (2048, NFIT), 0)
        hot_ref[...] = jnp.where(cell == offsets_ref[...], F32(1.0), F32(0.0)).astype(BF16)

    got = jnp.dot(orbitals_ref[...], hot_ref[...], preferred_element_type=F32).astype(BF16)
    own_ref[...] = got[:, :HALF]
    other_ref[...] = got[:, HALF:]


def pick(offsets, orbitals):
    rows = 256
    half = jax.ShapeDtypeStruct((NORB, HALF), BF16)
    return pl.pallas_call(
        pick_kernel,
        out_shape=(half, half),
        grid=(NORB // rows,),
        in_specs=[
            pl.BlockSpec((1, NFIT), lambda i: (0, 0)),
            pl.BlockSpec((rows, 2048), lambda i: (i, 0)),
        ],
        out_specs=[pl.BlockSpec((rows, HALF), lambda i: (i, 0))] * 2,
        scratch_shapes=[pltpu.VMEM((2048, NFIT), BF16)],
        name="pick",
    )(offsets, orbitals)


def fit_kernel(core_ref, own_ref, other_ref, table_ref, orbitals_ref, near_ref, far_ref, values_ref):
    @pl.when(pl.program_id(0) == 0)
    def _():
        core = core_ref[0]
        mine = pl.multiple_of(core * HALF, HALF)
        theirs = pl.multiple_of((1 - core) * HALF, HALF)
        values_ref[pl.ds(mine, HALF), :] = own_ref[...].astype(F32).T.astype(BF16)
        values_ref[pl.ds(theirs, HALF), :] = other_ref[...].astype(F32).T.astype(BF16)

    density = jnp.dot(values_ref[...], orbitals_ref[...], preferred_element_type=F32)
    fitted = (density * density).astype(BF16)
    for s in range(2):
        half_z = lax.dot_general(
            table_ref[...],
            fitted[:, 256 * s : 256 * s + 256],
            (((1,), (1,)), ((), ())),
            preferred_element_type=F32,
        ).astype(BF16)
        near_ref[4 * s : 4 * s + 4] = half_z[:128].reshape(4, 32, NFIT)
        far_ref[4 * s : 4 * s + 4] = half_z[128:].reshape(4, 32, NFIT)


def fit(core, own, other, table, orbitals):
    half = jax.ShapeDtypeStruct((32, 32, NFIT), BF16)
    return pl.pallas_call(
        fit_kernel,
        out_shape=(half, half),
        grid=(4,),
        in_specs=[
            pl.BlockSpec(memory_space=pltpu.SMEM),
            pl.BlockSpec((NORB, HALF), lambda i: (0, 0)),
            pl.BlockSpec((NORB, HALF), lambda i: (0, 0)),
            pl.BlockSpec((256, 256), lambda i: (0, 0)),
            pl.BlockSpec((NORB, 512), lambda i: (0, i)),
        ],
        out_specs=[pl.BlockSpec((8, 32, NFIT), lambda i: (i, 0, 0))] * 2,
        scratch_shapes=[pltpu.VMEM((NFIT, NORB), BF16)],
        name="fit",
    )(core, own, other, table, orbitals)


def y_kernel(core_ref, near_ref, far_ref, table_ref, out_ref, rows_ref):
    core = core_ref[0]
    mine = pl.multiple_of(core * 512, 512)
    theirs = pl.multiple_of((1 - core) * 512, 512)
    for g in range(2):
        rows_ref[pl.ds(mine, 512), :] = near_ref[:, 16 * g : 16 * g + 16, :].reshape(512, NFIT)
        rows_ref[pl.ds(theirs, 512), :] = far_ref[:, 16 * g : 16 * g + 16, :].reshape(512, NFIT)
        for m in range(4):
            got = jnp.dot(
                table_ref[256 * m : 256 * m + 256, :], rows_ref[...], preferred_element_type=F32
            ).astype(BF16)
            out_ref[8 * m : 8 * m + 8, g] = got.reshape(8, 2, 16, NFIT)


def y_transform(core, near, far, table):
    return pl.pallas_call(
        y_kernel,
        out_shape=jax.ShapeDtypeStruct((32, 2, 2, 16, NFIT), BF16),
        in_specs=[pl.BlockSpec(memory_space=pltpu.SMEM)]
        + [pl.BlockSpec(memory_space=pltpu.VMEM)] * 3,
        out_specs=pl.BlockSpec(memory_space=pltpu.VMEM),
        scratch_shapes=[pltpu.VMEM((1024, NFIT), BF16)],
        name="y_transform",
    )(core, near, far, table)


def gram_kernel(
    core_ref, planes_ref, table_ref, screen_ref, mixed_ref, own_ref, other_ref, coeffs_ref, weighted_ref
):
    mixed = jnp.concatenate([mixed_ref[...]] * 2, axis=1)
    for b in range(2):
        rows = planes_ref[:, b].reshape(1024, NFIT)
        t0, t1, t2, t3 = [
            jnp.dot(table_ref[256 * t : 256 * t + 256, :], rows, preferred_element_type=F32)
            .astype(BF16)
            .astype(F32)
            for t in range(4)
        ]
        outs = (t0 - mixed * t3, mixed * t0 + t3, t2 + mixed * t1, mixed * t2 - t1)
        for o, value in enumerate(outs):
            at = slice(256 * o, 256 * o + 256)
            value = value.astype(BF16)
            coeffs_ref[at, 256 * b : 256 * b + 256] = value
            value = value.astype(F32)
            screen = screen_ref[at, :]
            for h in range(2):
                weighted_ref[h, at, 128 * b : 128 * b + 128] = (
                    value[:, 128 * h : 128 * h + 128] * screen
                ).astype(BF16)
    core = core_ref[0]
    for q in range(2):
        left = coeffs_ref[:, 256 * q : 256 * q + 256]
        for half, out_ref in ((core, own_ref), (1 - core, other_ref)):
            got = kernel_scale * lax.dot_general(
                left, weighted_ref[half], (((0,), (0,)), ((), ())), preferred_element_type=F32
            )
            for b in range(2):
                out_ref[32 * q : 32 * q + 32, b] = got[:, 128 * b : 128 * b + 128].reshape(32, 8, 128)


def gram(core, planes, table, screen, mixed):
    half = jax.ShapeDtypeStruct((N, 2, 8, 128), F32)
    return pl.pallas_call(
        gram_kernel,
        out_shape=(half, half),
        in_specs=[pl.BlockSpec(memory_space=pltpu.SMEM)]
        + [pl.BlockSpec(memory_space=pltpu.VMEM)] * 4,
        out_specs=[pl.BlockSpec(memory_space=pltpu.VMEM)] * 2,
        scratch_shapes=[pltpu.VMEM((1024, 512), BF16), pltpu.VMEM((2, 1024, 256), BF16)],
        name="gram",
    )(core, planes, table, screen, mixed)


def sibling(block):
    return lax.ppermute(block, "c", [(0, 1), (1, 0)])


def exchange(blocks, axes):
    return lax.all_to_all(blocks, axes, split_axis=0, concat_axis=0, tiled=True)


def on_device(orbitals, points):
    core = lax.axis_index("c")
    batch = lax.axis_index("b")
    chip = lax.axis_index(CHIPS)
    core_word = core.astype(jnp.int32)[None]
    y_pair, z_group = chip // 2, core * 4 + chip % 2 * 2 + batch
    small = pair_table(iota((N, N), 0), iota((N, N), 1)).astype(BF16)
    z_row, z_column = iota((256, 256), 0), iota((256, 256), 1)
    z_half = jnp.where(z_row < 128, core, 1 - core)
    z_table = pair_table(z_half * 32 + z_row % 32, z_column % N)
    z_table = jnp.where(z_row // 32 % 4 == z_column // N, z_table, F32(0.0)).astype(BF16)
    y_big, x_big = expand(small, x_table(y_pair == 0))
    screen, mixed = screen_rows(y_pair, z_group * 4)

    halves = points[0].reshape(2, HALF)
    halves = jnp.where(core == 0, halves, halves[::-1])
    offsets = halves.reshape(1, NFIT) - (chip * 2 + core) * 2048
    own, other = pick(offsets, orbitals)
    own = exchange((own + sibling(other)).reshape(N, 16, HALF), CHIPS)
    own = jnp.sum(own.astype(F32), axis=0).astype(BF16)
    own = exchange(jnp.broadcast_to(own[None], (N, 16, HALF)), CHIPS).reshape(NORB, HALF)
    other = sibling(own)
    near, far = fit(core_word, own, other, z_table, orbitals)
    planes = y_transform(core_word, near, sibling(far), y_big)
    planes = exchange(planes.reshape(128, 16, NFIT), SAME_CORE).reshape(N, 2, 16, NFIT)
    own, other = gram(core_word, planes, x_big, screen, mixed)
    sums = exchange((own + sibling(other)).reshape(128, 8, 128), SAME_CORE)
    sums = jnp.sum(sums, axis=0).reshape(2, 4, 128)
    mine = lax.dynamic_index_in_dim(sums, core, 0, keepdims=False)
    theirs = sibling(lax.dynamic_index_in_dim(sums, 1 - core, 0, keepdims=False))
    pair = jnp.where(core == 0, jnp.stack([mine, theirs]), jnp.stack([theirs, mine]))
    return pair.transpose(0, 2, 1).reshape(NFIT, 4)


def solution(mesh):
    fine = Mesh(mesh.devices.reshape(2, 4, 8, 2, 2), ("yl", "x", "z", "c", "b"))
    grid = ("yl", "x", "z", "c")
    return jax.shard_map(
        on_device,
        mesh=fine,
        in_specs=(P(None, grid), P("b", None)),
        out_specs=P("b", grid),
        check_vma=False,
    )
```

time: 1790 us -> 155 us (0.09)
  waiting for transfers between devices: 1150 us -> 64.6 us
  blocking collectives: 558 us -> 0 us
  starting transfers between devices: 16 us -> 45.9 us
  local copies, waits for them, and re-layouts: 31 us -> 3.95 us
  Pallas kernels: 0 us -> 24.7 us
    unnamed x2 -> x0, waiting for transfers between devices: 1010 us -> none
    psum x1 -> x0, blocking collectives: 558 us -> none  [on_device(): point_values = lax.psum(picked, 'grid').astype(jnp.bfloat16)]
    ppermute x2 -> x5, waiting for transfers between devices: 88.2 us -> 3.95 us  [sibling(): return lax.ppermute(block, 'c', [(0, 1), (1, 0)])]
    pallas_call x0 -> x5, Pallas kernels: none -> 24.7 us  [the longest x1 5.6 us: fit(): pl.pallas_call(fit_kernel, out_shape=(half, half), grid=(4,), in_specs=[p...]
    all_to_all x1 -> x4, starting transfers between devices: 11.8 us -> 33.2 us  [exchange(): return lax.all_to_all(blocks, axes, split_axis=0, concat_axis=0, tiled=True)]
    all_to_all x1 -> x4, waiting for transfers between devices: 50.1 us -> 60.7 us  [exchange(): return lax.all_to_all(blocks, axes, split_axis=0, concat_axis=0, tiled=True)]
  transfers between devices with their start and end apart: 4 -> 9, of which waited for: 4 -> 7; matrix products, arithmetic and copies ran while one was open for 0% -> 7% of each run, Pallas kernels for 0% -> 3%
where the time goes in v1:
time: 155 us
  waiting for transfers between devices  64.6 us (42%)
  starting transfers between devices  45.9 us (30%)
  Pallas kernels  24.7 us (16%)
  other arithmetic  15.3 us (10%)
  local copies, waits for them, and re-layouts  3.95 us (3%)
    all_to_all x4, waiting for transfers between devices, exchange(): return lax.all_to_all(blocks, axes, split_axis=0, concat_axis=0, tiled=True)  60.7 us
    all_to_all x4, starting transfers between devices, exchange(): return lax.all_to_all(blocks, axes, split_axis=0, concat_axis=0, tiled=True)  33.2 us
    ppermute x5, starting transfers between devices, sibling(): return lax.ppermute(block, 'c', [(0, 1), (1, 0)])  12.7 us
    pallas_call x1, Pallas kernels, fit(): pl.pallas_call(fit_kernel, out_shape=(half, half), grid=(4,), in_specs=[p...  5.6 us
    pallas_call x1, Pallas kernels, gram(): pl.pallas_call(gram_kernel, out_shape=(half, half), in_specs=[pl.BlockSpe...  5.2 us
    pallas_call x1, Pallas kernels, pick(): pl.pallas_call(pick_kernel, out_shape=(half, half), grid=(NORB // rows,),...  4.92 us
    pallas_call x1, Pallas kernels, expand(): pl.pallas_call(expand_kernel, out_shape=(big, big), grid=(4,), in_specs=[...  4.78 us
    pallas_call x1, Pallas kernels, y_transform(): pl.pallas_call(y_kernel, out_shape=jax.ShapeDtypeStruct((32, 2, 2, 16, NF...  4.23 us
  transfers between devices with their start and end apart: 9, of which 7 were waited for; matrix products, arithmetic and copies ran while one was open for 7% of the time, Pallas kernels for 3%

profile of v1, /device:TPU:1, one launch (start us, length us, event | category | flops | bytes accessed | tf_op | source)
XLA Modules:
  0.0 154.7 jit_solution(7709443719518018733)
XLA Ops:
  0.0 0.7 rev.3
  0.7 0.6 select_subtract_fusion.1
  1.3 4.9 %pick.1 = (bf16[1024,128]{1,0:T(8,128)(2,1)}, bf16[1024,128]{1,0:T(8,128)(2,1)}) custom-call(s32[1,256]{1,0:T(1,128)} %bitcast.21, bf16[1024,2048]{1,0:T(8,128)(2,1)} %orbitals_ref.3), custom_call_target="tpu_custom_call" | custom-call | tf_op jit(solution)/shard_map/pick/pallas_call | solution.py:137
  6.2 3.9 %collective-permute-start = (bf16[1024,128]{1,0:T(8,128)(2,1)}, bf16[1024,128]{1,0:T(8,128)(2,1)S(1)}, u32[]{:S(2)}, u32[]{:S(2)}) collective-permute-start(bf16[1024,128]{1,0:T(8,128)(2,1)} %get-tuple-element.14), channel_id=1, source_target_pairs={{0,2},{2,0},{1,3},{3,1},{4,6},{6,4},{5,7},{7,5},{8,10},{10,8},{9,1... | collective-permute-start | bytes 786440 | tf_op jit(solution)/shard_map/ppermute | solution.py:266
  10.1 1.4 collective-permute-done
  11.4 1.7 %add.176 = bf16[1024,128]{1,0:T(8,128)(2,1)} add(bf16[1024,128]{1,0:T(8,128)(2,1)} %get-tuple-element.13, bf16[1024,128]{1,0:T(8,128)(2,1)S(1)} %collective-permute-done) | non-fusion elementwise | flops 131072 | bytes 786432 | tf_op jit(solution)/shard_map/add | solution.py:291
  13.2 11.0 %all-to-all-start = ((bf16[64,16,128]{2,1,0:T(8,128)(2,1)}), bf16[64,16,128]{2,1,0:T(8,128)(2,1)S(1)}, u32[]{:S(2)}, u32[]{:S(2)}) async-start(bf16[64,16,128]{2,1,0:T(8,128)(2,1)} %bitcast.3), calls=%async_computation | async-start | bytes 524288 | tf_op jit(solution)/shard_map/all_to_all | solution.py:270
  24.2 11.9 %all-to-all-done = bf16[64,16,128]{2,1,0:T(8,128)(2,1)S(1)} async-done(((bf16[64,16,128]{2,1,0:T(8,128)(2,1)}), bf16[64,16,128]{2,1,0:T(8,128)(2,1)S(1)}, u32[]{:S(2)}, u32[]{:S(2)}) %all-to-all-start) | async-done | bytes 262176 | tf_op jit(solution)/shard_map/all_to_all | solution.py:270
  36.1 0.1 reduce_sum.21
  36.1 0.7 broadcast_in_dim.56
  36.9 5.6 %all-to-all-start.1 = ((bf16[64,16,128]{2,1,0:T(8,128)(2,1)}), bf16[64,16,128]{2,1,0:T(8,128)(2,1)S(1)}, u32[]{:S(2)}, u32[]{:S(2)}) async-start(bf16[64,16,128]{2,1,0:T(8,128)(2,1)} %broadcast_in_dim.56), calls=%async_computation.1 | async-start | bytes 524288 | tf_op jit(solution)/shard_map/all_to_all | solution.py:270
  42.5 10.9 %all-to-all-done.1 = bf16[64,16,128]{2,1,0:T(8,128)(2,1)S(1)} async-done(((bf16[64,16,128]{2,1,0:T(8,128)(2,1)}), bf16[64,16,128]{2,1,0:T(8,128)(2,1)S(1)}, u32[]{:S(2)}, u32[]{:S(2)}) %all-to-all-start.1) | async-done | bytes 262176 | tf_op jit(solution)/shard_map/all_to_all | solution.py:270
  53.5 0.0 copy-start.1
  53.5 3.5 %collective-permute-start.1 = (bf16[1024,128]{1,0:T(8,128)(2,1)S(1)}, bf16[1024,128]{1,0:T(8,128)(2,1)S(1)}, u32[]{:S(2)}, u32[]{:S(2)}) collective-permute-start(bf16[1024,128]{1,0:T(8,128)(2,1)S(1)} %bitcast.18), channel_id=1, source_target_pairs={{0,2},{2,0},{1,3},{3,1},{4,6},{6,4},{5,7},{7,5},{8,10},{10,8},{9,1... | collective-permute-start | bytes 786440 | tf_op jit(solution)/shard_map/ppermute | solution.py:266
  57.0 3.9 %fusion.19 = (bf16[256,256]{1,0:T(8,128)(2,1)}, bf16[256,256]{1,0:T(8,128)(2,1)}) fusion(s32[256]{0:T(256)S(1)} %get-tuple-element.33, s32[256]{0:T(256)S(1)} %get-tuple-element.39, s32[256]{0:T(256)S(1)} %get-tuple-element.34, s32[256]{0:T(256)S(1)} %get-tuple-element.40, s32[256]{0:T(256)S(1)} %get-tuple-element.35, s32[256]{0:T(256)S(1)} %get-tuple-element.37, ...), kind=kLoop, calls=%fused_computation.81 | loop fusion | flops 9502720 | bytes 274689 | tf_op jit(solution)/shard_map/convert_element_type | solution.py:57
  60.9 0.0 collective-permute-done.1.other_ref
  60.9 0.0 copy-start.3
  60.9 0.0 copy-done.1
  60.9 0.7 copy-done.3
  61.6 5.6 %fit.1 = (bf16[32,32,256]{2,1,0:T(8,128)(2,1)}, bf16[32,32,256]{2,1,0:T(8,128)(2,1)}) custom-call(s32[1]{0:T(128)} %bitcast.core_ref, bf16[1024,128]{1,0:T(8,128)(2,1)} %bitcast.19, bf16[1024,128]{1,0:T(8,128)(2,1)} %copy-done.3, bf16[256,256]{1,0:T(8,128)(2,1)} %get-tuple-element.22.table_ref, bf16[1024,2048]{1,0:T(8,128)(2,1)} %orbitals_ref.3), custom_call_target="tpu_custom_call" | custom-call | tf_op jit(solution)/shard_map/fit/pallas_call | solution.py:175
  67.2 0.0 collective-permute-start.2
  67.3 0.9 select_convert_fusion.1.y_small_ref
  68.1 4.8 %expand.1 = (bf16[1024,1024]{1,0:T(8,128)(2,1)}, bf16[1024,1024]{1,0:T(8,128)(2,1)}) custom-call(bf16[64,64]{1,0:T(8,128)(2,1)} %select_convert_fusion.1.y_small_ref, bf16[256,256]{1,0:T(8,128)(2,1)} %get-tuple-element.21.x_small_ref), custom_call_target="tpu_custom_call" | custom-call | flops 2147483648 | bytes 4194304 | tf_op jit(solution)/shard_map/expand/pallas_call | solution.py:109
  72.9 0.0 collective-permute-done.2.far_ref
  72.9 0.0 copy-start.2
  72.9 0.8 copy-done.2
  73.7 4.2 %y_transform.1 = bf16[32,2,2,16,256]{4,3,2,1,0:T(8,128)(2,1)} custom-call(s32[1]{0:T(128)} %bitcast.core_ref, bf16[32,32,256]{2,1,0:T(8,128)(2,1)} %get-tuple-element.15.near_ref, bf16[32,32,256]{2,1,0:T(8,128)(2,1)} %copy-done.2, bf16[1024,1024]{1,0:T(8,128)(2,1)} %get-tuple-element.17.table_ref), custom_call_target="tpu_custom_call" | custom-call | tf_op jit(solution)/shard_map/y_transform/pallas_call | solution.py:207
  77.9 7.9 %all-to-all-start.2 = ((bf16[128,16,256]{2,1,0:T(8,128)(2,1)}), bf16[128,16,256]{2,1,0:T(8,128)(2,1)S(1)}, u32[]{:S(2)}, u32[]{:S(2)}) async-start(bf16[128,16,256]{2,1,0:T(8,128)(2,1)} %bitcast.16), calls=%async_computation.2 | async-start | bytes 2097152 | tf_op jit(solution)/shard_map/all_to_all | solution.py:270
  85.9 0.9 fusion.14
  86.8 1.0 compare_and_fusion
  87.8 0.7 fusion.40.mixed_ref
  88.5 2.9 %fusion.2.screen_ref = f32[1024,128]{1,0:T(8,128)} fusion(s32[1024]{0:T(1024)S(1)} %get-tuple-element.46, s32[1024]{0:T(1024)S(1)} %get-tuple-element.48, s32[]{:T(128)S(6)} %mul.81, s32[]{:T(128)S(6)} %select_n.333, s32[1024]{0:T(1024)S(1)} %get-tuple-element.47, s32[1024]{0:T(1024)S(1)} %get-tuple-element.51, s32[1024]{0:T(1024)S(1)} %get-tuple-element.45, ...), kind=kLoop, calls=%fused_computation.27 | loop fusion | flops 9175040 | bytes 551945 | tf_op jit(solution)/shard_map/mul | solution.py:79
  91.4 21.5 %all-to-all-done.2 = bf16[128,16,256]{2,1,0:T(8,128)(2,1)S(1)} async-done(((bf16[128,16,256]{2,1,0:T(8,128)(2,1)}), bf16[128,16,256]{2,1,0:T(8,128)(2,1)S(1)}, u32[]{:S(2)}, u32[]{:S(2)}) %all-to-all-start.2) | async-done | bytes 1048608 | tf_op jit(solution)/shard_map/all_to_all | solution.py:270
  112.9 0.0 copy-start
  112.9 1.0 copy-done
  113.9 5.2 %gram.1 = (f32[64,2,8,128]{3,2,1,0:T(8,128)}, f32[64,2,8,128]{3,2,1,0:T(8,128)}) custom-call(s32[1]{0:T(128)} %bitcast.core_ref, bf16[64,2,16,256]{3,2,1,0:T(8,128)(2,1)} %bitcast.17, bf16[1024,1024]{1,0:T(8,128)(2,1)} %get-tuple-element.18.table_ref, f32[1024,128]{1,0:T(8,128)} %fusion.2.screen_ref, f32[256,128]{1,0:T(8,128)} %fusion.40.mixed_ref), custom_call_target="tpu_custom_call" | custom-call | tf_op jit(solution)/shard_map/gram/pallas_call | solution.py:254
  119.1 2.5 %collective-permute-start.3 = (f32[64,2,8,128]{3,2,1,0:T(8,128)}, f32[64,2,8,128]{3,2,1,0:T(8,128)S(1)}, u32[]{:S(2)}, u32[]{:S(2)}) collective-permute-start(f32[64,2,8,128]{3,2,1,0:T(8,128)} %get-tuple-element.20), channel_id=1, source_target_pairs={{0,2},{2,0},{1,3},{3,1},{4,6},{6,4},{5,7},{7,5},{8,10},{10,8},{9,1... | collective-permute-start | bytes 1572872 | tf_op jit(solution)/shard_map/ppermute | solution.py:266
  121.6 1.7 %collective-permute-done.3 = f32[64,2,8,128]{3,2,1,0:T(8,128)S(1)} collective-permute-done((f32[64,2,8,128]{3,2,1,0:T(8,128)}, f32[64,2,8,128]{3,2,1,0:T(8,128)S(1)}, u32[]{:S(2)}, u32[]{:S(2)}) %collective-permute-start.3) | collective-permute-done | bytes 524320 | tf_op jit(solution)/shard_map/ppermute | solution.py:266
  123.3 1.9 %add.199 = f32[64,2,8,128]{3,2,1,0:T(8,128)} add(f32[64,2,8,128]{3,2,1,0:T(8,128)} %get-tuple-element.19, f32[64,2,8,128]{3,2,1,0:T(8,128)S(1)} %collective-permute-done.3) | non-fusion elementwise | flops 131072 | bytes 1572864 | tf_op jit(solution)/shard_map/add | solution.py:299
  125.3 8.7 %all-to-all-start.3 = ((f32[128,8,128]{2,1,0:T(8,128)}), f32[128,8,128]{2,1,0:T(8,128)S(1)}, u32[]{:S(2)}, u32[]{:S(2)}) async-start(f32[128,8,128]{2,1,0:T(8,128)} %bitcast.7), calls=%async_computation.3 | async-start | bytes 1048576 | tf_op jit(solution)/shard_map/all_to_all | solution.py:270
  134.0 16.3 %all-to-all-done.3 = f32[128,8,128]{2,1,0:T(8,128)S(1)} async-done(((f32[128,8,128]{2,1,0:T(8,128)}), f32[128,8,128]{2,1,0:T(8,128)S(1)}, u32[]{:S(2)}, u32[]{:S(2)}) %all-to-all-start.3) | async-done | bytes 524320 | tf_op jit(solution)/shard_map/all_to_all | solution.py:270
  150.3 0.1 reduce_sum.22
  150.5 2.8 %collective-permute-start.4 = (f32[4,128]{1,0:T(4,128)S(1)}, f32[4,128]{1,0:T(4,128)S(1)}, u32[]{:S(2)}, u32[]{:S(2)}) collective-permute-start(f32[4,128]{1,0:T(4,128)S(1)} %get-tuple-element.24), channel_id=1, source_target_pairs={{0,2},{2,0},{1,3},{3,1},{4,6},{6,4},{5,7},{7,5},{8,10},{10,8},{9,1... | collective-permute-start | bytes 6152 | tf_op jit(solution)/shard_map/ppermute | solution.py:266
  153.3 0.8 collective-permute-done.4
  154.1 0.6 fusion.55
  (18 shorter events, 0.1 us)
Async XLA Ops:
  6.2 5.3 %collective-permute-start = (bf16[1024,128]{1,0:T(8,128)(2,1)}, bf16[1024,128]{1,0:T(8,128)(2,1)S(1)}, u32[]{:S(2)}, u32[]{:S(2)}) collective-permute-start(bf16[1024,128]{1,0:T(8,128)(2,1)} %get-tuple-element.14), channel_id=1, source_target_pairs={{0,2},{2,0},{1,3},{3,1},{4,6},{6,4},{5,7},{7,5},{8,10},{10,8},{9,1... | collective-permute-start | bytes 786440 | tf_op jit(solution)/shard_map/ppermute | solution.py:266
  13.2 22.9 %all-to-all-start = ((bf16[64,16,128]{2,1,0:T(8,128)(2,1)}), bf16[64,16,128]{2,1,0:T(8,128)(2,1)S(1)}, u32[]{:S(2)}, u32[]{:S(2)}) async-start(bf16[64,16,128]{2,1,0:T(8,128)(2,1)} %bitcast.3), calls=%async_computation | async-start | bytes 524288 | tf_op jit(solution)/shard_map/all_to_all | solution.py:270
  36.9 16.6 %all-to-all-start.1 = ((bf16[64,16,128]{2,1,0:T(8,128)(2,1)}), bf16[64,16,128]{2,1,0:T(8,128)(2,1)S(1)}, u32[]{:S(2)}, u32[]{:S(2)}) async-start(bf16[64,16,128]{2,1,0:T(8,128)(2,1)} %broadcast_in_dim.56), calls=%async_computation.1 | async-start | bytes 524288 | tf_op jit(solution)/shard_map/all_to_all | solution.py:270
  53.5 7.5 %copy-start.1 = (bf16[64,16,128]{2,1,0:T(8,128)(2,1)}, bf16[64,16,128]{2,1,0:T(8,128)(2,1)S(1)}, u32[]{:S(2)}) copy-start(bf16[64,16,128]{2,1,0:T(8,128)(2,1)S(1)} %all-to-all-done.1) | copy-start | bytes 786436
  53.5 7.4 %collective-permute-start.1 = (bf16[1024,128]{1,0:T(8,128)(2,1)S(1)}, bf16[1024,128]{1,0:T(8,128)(2,1)S(1)}, u32[]{:S(2)}, u32[]{:S(2)}) collective-permute-start(bf16[1024,128]{1,0:T(8,128)(2,1)S(1)} %bitcast.18), channel_id=1, source_target_pairs={{0,2},{2,0},{1,3},{3,1},{4,6},{6,4},{5,7},{7,5},{8,10},{10,8},{9,1... | collective-permute-start | bytes 786440 | tf_op jit(solution)/shard_map/ppermute | solution.py:266
  60.9 0.7 copy-start.3
  67.2 5.7 %collective-permute-start.2 = (bf16[32,32,256]{2,1,0:T(8,128)(2,1)}, bf16[32,32,256]{2,1,0:T(8,128)(2,1)S(1)}, u32[]{:S(2)}, u32[]{:S(2)}) collective-permute-start(bf16[32,32,256]{2,1,0:T(8,128)(2,1)} %get-tuple-element.16), channel_id=1, source_target_pairs={{0,2},{2,0},{1,3},{3,1},{4,6},{6,4},{5,7},{7,5},{8,10},{10,8},{9,1... | collective-permute-start | bytes 1572872 | tf_op jit(solution)/shard_map/ppermute | solution.py:266
  72.9 0.8 copy-start.2
  77.9 35.0 %all-to-all-start.2 = ((bf16[128,16,256]{2,1,0:T(8,128)(2,1)}), bf16[128,16,256]{2,1,0:T(8,128)(2,1)S(1)}, u32[]{:S(2)}, u32[]{:S(2)}) async-start(bf16[128,16,256]{2,1,0:T(8,128)(2,1)} %bitcast.16), calls=%async_computation.2 | async-start | bytes 2097152 | tf_op jit(solution)/shard_map/all_to_all | solution.py:270
  112.9 1.0 copy-start
  119.1 4.3 %collective-permute-start.3 = (f32[64,2,8,128]{3,2,1,0:T(8,128)}, f32[64,2,8,128]{3,2,1,0:T(8,128)S(1)}, u32[]{:S(2)}, u32[]{:S(2)}) collective-permute-start(f32[64,2,8,128]{3,2,1,0:T(8,128)} %get-tuple-element.20), channel_id=1, source_target_pairs={{0,2},{2,0},{1,3},{3,1},{4,6},{6,4},{5,7},{7,5},{8,10},{10,8},{9,1... | collective-permute-start | bytes 1572872 | tf_op jit(solution)/shard_map/ppermute | solution.py:266
  125.3 25.1 %all-to-all-start.3 = ((f32[128,8,128]{2,1,0:T(8,128)}), f32[128,8,128]{2,1,0:T(8,128)S(1)}, u32[]{:S(2)}, u32[]{:S(2)}) async-start(f32[128,8,128]{2,1,0:T(8,128)} %bitcast.7), calls=%async_computation.3 | async-start | bytes 1048576 | tf_op jit(solution)/shard_map/all_to_all | solution.py:270
  150.5 3.6 %collective-permute-start.4 = (f32[4,128]{1,0:T(4,128)S(1)}, f32[4,128]{1,0:T(4,128)S(1)}, u32[]{:S(2)}, u32[]{:S(2)}) collective-permute-start(f32[4,128]{1,0:T(4,128)S(1)} %get-tuple-element.24), channel_id=1, source_target_pairs={{0,2},{2,0},{1,3},{3,1},{4,6},{6,4},{5,7},{7,5},{8,10},{10,8},{9,1... | collective-permute-start | bytes 6152 | tf_op jit(solution)/shard_map/ppermute | solution.py:266

commit v2 on v1

--- a/solution.py
+++ b/solution.py
@@ -116,77 +116,89 @@
         ],
         out_specs=[pl.BlockSpec((256, 1024), lambda i: (i, 0))] * 2,
         cost_estimate=pl.CostEstimate(flops=2**31, bytes_accessed=2**22, transcendentals=0),
+        compiler_params=pltpu.CompilerParams(vmem_limit_bytes=16 << 20),
         name="expand",
     )(y_small, x_small)
 
 
-def pick_kernel(offsets_ref, orbitals_ref, own_ref, other_ref, hot_ref):
-    @pl.when(pl.program_id(0) == 0)
-    def _():
-        cell = lax.broadcasted_iota(jnp.int32, (2048, NFIT), 0)
-        hot_ref[...] = jnp.where(cell == offsets_ref[...], F32(1.0), F32(0.0)).astype(BF16)
-
-    got = jnp.dot(orbitals_ref[...], hot_ref[...], preferred_element_type=F32).astype(BF16)
+def pick_kernel(offsets_ref, orbitals_ref, own_ref, other_ref, held_ref, hot_ref, sem):
+    copy = pltpu.make_async_copy(orbitals_ref, held_ref, sem)
+    copy.start()
+    cell = iota((2048, NFIT), 0)
+    hot_ref[...] = jnp.where(cell == offsets_ref[...], F32(1.0), F32(0.0)).astype(BF16)
+    copy.wait()
+    got = jnp.dot(held_ref[...], hot_ref[...], preferred_element_type=F32).astype(BF16)
     own_ref[...] = got[:, :HALF]
     other_ref[...] = got[:, HALF:]
 
 
 def pick(offsets, orbitals):
-    rows = 256
     half = jax.ShapeDtypeStruct((NORB, HALF), BF16)
+    vmem = pl.BlockSpec(memory_space=pltpu.VMEM)
     return pl.pallas_call(
         pick_kernel,
         out_shape=(half, half),
-        grid=(NORB // rows,),
-        in_specs=[
-            pl.BlockSpec((1, NFIT), lambda i: (0, 0)),
-            pl.BlockSpec((rows, 2048), lambda i: (i, 0)),
+        in_specs=[vmem, pl.BlockSpec(memory_space=pltpu.HBM)],
+        out_specs=[vmem] * 2,
+        scratch_shapes=[
+            pltpu.VMEM((NORB, 2048), BF16),
+            pltpu.VMEM((2048, NFIT), BF16),
+            pltpu.SemaphoreType.DMA(()),
         ],
-        out_specs=[pl.BlockSpec((rows, HALF), lambda i: (i, 0))] * 2,
-        scratch_shapes=[pltpu.VMEM((2048, NFIT), BF16)],
+        compiler_params=pltpu.CompilerParams(vmem_limit_bytes=16 << 20),
         name="pick",
     )(offsets, orbitals)
 
 
+def hold_kernel(orbitals_ref, held_ref, sem):
+    copy = pltpu.make_async_copy(orbitals_ref, held_ref, sem)
+    copy.start()
+    copy.wait()
+
+
+def hold(orbitals):
+    return pl.pallas_call(
+        hold_kernel,
+        out_shape=jax.ShapeDtypeStruct(orbitals.shape, orbitals.dtype),
+        in_specs=[pl.BlockSpec(memory_space=pltpu.HBM)],
+        out_specs=pl.BlockSpec(memory_space=pltpu.VMEM),
+        scratch_shapes=[pltpu.SemaphoreType.DMA(())],
+        compiler_params=pltpu.CompilerParams(vmem_limit_bytes=8 << 20),
+        cost_estimate=pl.CostEstimate(flops=0, bytes_accessed=2**23, transcendentals=0),
+        name="hold",
+    )(orbitals)
+
+
 def fit_kernel(core_ref, own_ref, other_ref, table_ref, orbitals_ref, near_ref, far_ref, values_ref):
-    @pl.when(pl.program_id(0) == 0)
-    def _():
-        core = core_ref[0]
-        mine = pl.multiple_of(core * HALF, HALF)
-        theirs = pl.multiple_of((1 - core) * HALF, HALF)
-        values_ref[pl.ds(mine, HALF), :] = own_ref[...].astype(F32).T.astype(BF16)
-        values_ref[pl.ds(theirs, HALF), :] = other_ref[...].astype(F32).T.astype(BF16)
-
-    density = jnp.dot(values_ref[...], orbitals_ref[...], preferred_element_type=F32)
+    core = core_ref[0]
+    mine = pl.multiple_of(core * HALF, HALF)
+    theirs = pl.multiple_of((1 - core) * HALF, HALF)
+    values_ref[:, pl.ds(mine, HALF)] = own_ref[...]
+    values_ref[:, pl.ds(theirs, HALF)] = other_ref[...]
+    density = lax.dot_general(
+        orbitals_ref[...], values_ref[...], (((0,), (0,)), ((), ())), preferred_element_type=F32
+    )
     fitted = (density * density).astype(BF16)
-    for s in range(2):
-        half_z = lax.dot_general(
-            table_ref[...],
-            fitted[:, 256 * s : 256 * s + 256],
-            (((1,), (1,)), ((), ())),
-            preferred_element_type=F32,
+    for j in range(8):
+        half_z = jnp.dot(
+            table_ref[...], fitted[256 * j : 256 * j + 256], preferred_element_type=F32
         ).astype(BF16)
-        near_ref[4 * s : 4 * s + 4] = half_z[:128].reshape(4, 32, NFIT)
-        far_ref[4 * s : 4 * s + 4] = half_z[128:].reshape(4, 32, NFIT)
-
-
-def fit(core, own, other, table, orbitals):
+        near_ref[4 * j : 4 * j + 4] = half_z[:128].reshape(4, 32, NFIT)
+        far_ref[4 * j : 4 * j + 4] = half_z[128:].reshape(4, 32, NFIT)
+
+
+def fit(core, own, other, table, held):
     half = jax.ShapeDtypeStruct((32, 32, NFIT), BF16)
+    vmem = pl.BlockSpec(memory_space=pltpu.VMEM)
     return pl.pallas_call(
         fit_kernel,
         out_shape=(half, half),
-        grid=(4,),
-        in_specs=[
-            pl.BlockSpec(memory_space=pltpu.SMEM),
-            pl.BlockSpec((NORB, HALF), lambda i: (0, 0)),
-            pl.BlockSpec((NORB, HALF), lambda i: (0, 0)),
-            pl.BlockSpec((256, 256), lambda i: (0, 0)),
-            pl.BlockSpec((NORB, 512), lambda i: (0, i)),
-        ],
-        out_specs=[pl.BlockSpec((8, 32, NFIT), lambda i: (i, 0, 0))] * 2,
-        scratch_shapes=[pltpu.VMEM((NFIT, NORB), BF16)],
+        in_specs=[pl.BlockSpec(memory_space=pltpu.SMEM)] + [vmem] * 4,
+        out_specs=[vmem] * 2,
+        scratch_shapes=[pltpu.VMEM((NORB, NFIT), BF16)],
+        compiler_params=pltpu.CompilerParams(vmem_limit_bytes=16 << 20),
         name="fit",
-    )(core, own, other, table, orbitals)
+    )(core, own, other, table, held)
 
 
 def y_kernel(core_ref, near_ref, far_ref, table_ref, out_ref, rows_ref):
@@ -211,6 +223,7 @@
         + [pl.BlockSpec(memory_space=pltpu.VMEM)] * 3,
         out_specs=pl.BlockSpec(memory_space=pltpu.VMEM),
         scratch_shapes=[pltpu.VMEM((1024, NFIT), BF16)],
+        compiler_params=pltpu.CompilerParams(vmem_limit_bytes=14 << 20),
         name="y_transform",
     )(core, near, far, table)
 
@@ -258,6 +271,7 @@
         + [pl.BlockSpec(memory_space=pltpu.VMEM)] * 4,
         out_specs=[pl.BlockSpec(memory_space=pltpu.VMEM)] * 2,
         scratch_shapes=[pltpu.VMEM((1024, 512), BF16), pltpu.VMEM((2, 1024, 256), BF16)],
+        compiler_params=pltpu.CompilerParams(vmem_limit_bytes=20 << 20),
         name="gram",
     )(core, planes, table, screen, mixed)
 
@@ -287,12 +301,16 @@
     halves = points[0].reshape(2, HALF)
     halves = jnp.where(core == 0, halves, halves[::-1])
     offsets = halves.reshape(1, NFIT) - (chip * 2 + core) * 2048
+    orbitals = pltpu.with_memory_space_constraint(orbitals, pltpu.HBM)
     own, other = pick(offsets, orbitals)
     own = exchange((own + sibling(other)).reshape(N, 16, HALF), CHIPS)
     own = jnp.sum(own.astype(F32), axis=0).astype(BF16)
     own = exchange(jnp.broadcast_to(own[None], (N, 16, HALF)), CHIPS).reshape(NORB, HALF)
-    other = sibling(own)
-    near, far = fit(core_word, own, other, z_table, orbitals)
+    own, z_table, y_big, x_big, orbitals = lax.optimization_barrier(
+        (own, z_table, y_big, x_big, orbitals)
+    )
+    held = hold(orbitals)
+    near, far = fit(core_word, own, sibling(own), z_table, held)
     planes = y_transform(core_word, near, sibling(far), y_big)
     planes = exchange(planes.reshape(128, 16, NFIT), SAME_CORE).reshape(N, 2, 16, NFIT)
     own, other = gram(core_word, planes, x_big, screen, mixed)

time: 155 us -> 135 us (0.87)
  Pallas kernels: 24.7 us -> 15 us
  waiting for transfers between devices: 64.6 us -> 59.3 us
  other arithmetic: 15.3 us -> 10.7 us
    all_to_all x4, waiting for transfers between devices: 60.7 us -> 54 us  [exchange(): return lax.all_to_all(blocks, axes, split_axis=0, concat_axis=0, tiled=True)]
    pallas_call x2 -> x3, Pallas kernels: 10.5 us -> 7.45 us  [the longest x1 3.43 us: pick(): pl.pallas_call(pick_kernel, out_shape=(half, half), in_specs=[vmem, pl.Bl...]
    pallas_call x1, Pallas kernels: 5.2 us -> 2.24 us  [gram(): pl.pallas_call(gram_kernel, out_shape=(half, half), in_specs=[pl.BlockSpe...]
    pallas_call x1, Pallas kernels: 4.23 us -> 2.3 us  [y_transform(): pl.pallas_call(y_kernel, out_shape=jax.ShapeDtypeStruct((32, 2, 2, 16, NF...]
    pallas_call x1, Pallas kernels: 4.78 us -> 3.02 us  [expand(): pl.pallas_call(expand_kernel, out_shape=(big, big), grid=(4,), in_specs=[...]
  transfers between devices with their start and end apart: 9 -> 9, of which waited for: 7 -> 8; matrix products, arithmetic and copies ran while one was open for 7% -> 6% of each run, Pallas kernels for 3% -> 4%
where the time goes in v2:
time: 135 us
  waiting for transfers between devices  59.3 us (44%)
  starting transfers between devices  45.8 us (34%)
  Pallas kernels  15 us (11%)
  other arithmetic  10.7 us (8%)
  local copies, waits for them, and re-layouts  3.84 us (3%)
    all_to_all x4, waiting for transfers between devices, exchange(): return lax.all_to_all(blocks, axes, split_axis=0, concat_axis=0, tiled=True)  54 us
    all_to_all x4, starting transfers between devices, exchange(): return lax.all_to_all(blocks, axes, split_axis=0, concat_axis=0, tiled=True)  33 us
    ppermute x5, starting transfers between devices, sibling(): return lax.ppermute(block, 'c', [(0, 1), (1, 0)])  12.8 us
    ppermute x5, waiting for transfers between devices, sibling(): return lax.ppermute(block, 'c', [(0, 1), (1, 0)])  5.3 us
    pallas_call x1, Pallas kernels, pick(): pl.pallas_call(pick_kernel, out_shape=(half, half), in_specs=[vmem, pl.Bl...  3.43 us
    convert_element_type x1, other arithmetic, x_table(): return jnp.where(lone, jnp.where(kept, single, F32(0.0)), both).astype(BF16)  3.06 us
    pallas_call x1, Pallas kernels, expand(): pl.pallas_call(expand_kernel, out_shape=(big, big), grid=(4,), in_specs=[...  3.02 us
    mul x1, other arithmetic, screen_rows(): return (screen * copies, mixed)  2.96 us
  transfers between devices with their start and end apart: 9, of which 8 were waited for; matrix products, arithmetic and copies ran while one was open for 6% of the time, Pallas kernels for 4%

profile of v2, /device:TPU:1, one launch (start us, length us, event | category | flops | bytes accessed | tf_op | source)
XLA Modules:
  0.0 134.9 jit_solution(13004440834483772686)
XLA Ops:
  0.0 0.7 rev.3
  0.7 3.4 %pick.1 = (bf16[1024,128]{1,0:T(8,128)(2,1)S(1)}, bf16[1024,128]{1,0:T(8,128)(2,1)S(1)}) custom-call(s32[1,256]{1,0:T(1,128)S(1)} %bitcast.19, bf16[1024,2048]{1,0:T(8,128)(2,1)} %orbitals_ref.2), custom_call_target="tpu_custom_call" | custom-call | tf_op jit(solution)/shard_map/pick/pallas_call | solution.py:138
  4.1 4.0 %collective-permute-start = (bf16[1024,128]{1,0:T(8,128)(2,1)S(1)}, bf16[1024,128]{1,0:T(8,128)(2,1)S(1)}, u32[]{:S(2)}, u32[]{:S(2)}) collective-permute-start(bf16[1024,128]{1,0:T(8,128)(2,1)S(1)} %get-tuple-element.19), channel_id=1, source_target_pairs={{0,2},{2,0},{1,3},{3,1},{4,6},{6,4},{5,7},{7,5},{8,10},{10,8},{9,1... | collective-permute-start | bytes 786440 | tf_op jit(solution)/shard_map/ppermute | solution.py:280
  8.2 1.0 collective-permute-done
  9.3 0.8 add.176
  10.1 11.0 %all-to-all-start = ((bf16[64,16,128]{2,1,0:T(8,128)(2,1)}), bf16[64,16,128]{2,1,0:T(8,128)(2,1)S(1)}, u32[]{:S(2)}, u32[]{:S(2)}) async-start(bf16[64,16,128]{2,1,0:T(8,128)(2,1)} %bitcast.3), calls=%async_computation | async-start | bytes 524288 | tf_op jit(solution)/shard_map/all_to_all | solution.py:284
  21.0 3.1 %fusion.19 = (bf16[256,256]{1,0:T(8,128)(2,1)S(1)}, bf16[256,256]{1,0:T(8,128)(2,1)S(1)}) fusion(s32[256]{0:T(256)S(1)} %get-tuple-element.43, s32[256]{0:T(256)S(1)} %get-tuple-element.49, s32[256]{0:T(256)S(1)} %get-tuple-element.44, s32[256]{0:T(256)S(1)} %get-tuple-element.50, s32[256]{0:T(256)S(1)} %get-tuple-element.45, s32[256]{0:T(256)S(1)} %get-tuple-element.47, ...), kind=kLoop, calls=%fused_computation.81 | loop fusion | flops 9502720 | bytes 274689 | tf_op jit(solution)/shard_map/convert_element_type | solution.py:57
  24.1 8.8 %all-to-all-done = bf16[64,16,128]{2,1,0:T(8,128)(2,1)S(1)} async-done(((bf16[64,16,128]{2,1,0:T(8,128)(2,1)}), bf16[64,16,128]{2,1,0:T(8,128)(2,1)S(1)}, u32[]{:S(2)}, u32[]{:S(2)}) %all-to-all-start) | async-done | bytes 262176 | tf_op jit(solution)/shard_map/all_to_all | solution.py:284
  32.9 0.1 reduce_sum.21
  33.0 0.7 broadcast_in_dim.56
  33.8 5.6 %all-to-all-start.1 = ((bf16[64,16,128]{2,1,0:T(8,128)(2,1)}), bf16[64,16,128]{2,1,0:T(8,128)(2,1)S(1)}, u32[]{:S(2)}, u32[]{:S(2)}) async-start(bf16[64,16,128]{2,1,0:T(8,128)(2,1)} %broadcast_in_dim.56), calls=%async_computation.1 | async-start | bytes 524288 | tf_op jit(solution)/shard_map/all_to_all | solution.py:284
  39.4 0.3 select_convert_fusion.1.y_small_ref
  39.6 3.0 %expand.1 = (bf16[1024,1024]{1,0:T(8,128)(2,1)S(1)}, bf16[1024,1024]{1,0:T(8,128)(2,1)S(1)}) custom-call(bf16[64,64]{1,0:T(8,128)(2,1)S(1)} %select_convert_fusion.1.y_small_ref, bf16[256,256]{1,0:T(8,128)(2,1)S(1)} %get-tuple-element.31.x_small_ref), custom_call_target="tpu_custom_call" | custom-call | flops 2147483648 | bytes 4194304 | tf_op jit(solution)/shard_map/expand/pallas_call | solution.py:109
  42.6 0.0 copy-start
  42.7 1.3 copy-done
  44.0 6.3 %all-to-all-done.1 = bf16[64,16,128]{2,1,0:T(8,128)(2,1)S(1)} async-done(((bf16[64,16,128]{2,1,0:T(8,128)(2,1)}), bf16[64,16,128]{2,1,0:T(8,128)(2,1)S(1)}, u32[]{:S(2)}, u32[]{:S(2)}) %all-to-all-start.1) | async-done | bytes 262176 | tf_op jit(solution)/shard_map/all_to_all | solution.py:284
  50.3 3.5 %collective-permute-start.1 = (bf16[1024,128]{1,0:T(8,128)(2,1)S(1)}, bf16[1024,128]{1,0:T(8,128)(2,1)S(1)}, u32[]{:S(2)}, u32[]{:S(2)}) collective-permute-start(bf16[1024,128]{1,0:T(8,128)(2,1)S(1)} %bitcast.17), channel_id=1, source_target_pairs={{0,2},{2,0},{1,3},{3,1},{4,6},{6,4},{5,7},{7,5},{8,10},{10,8},{9,1... | collective-permute-start | bytes 786440 | tf_op jit(solution)/shard_map/ppermute | solution.py:280
  53.9 2.2 %hold.1.orbitals_ref = bf16[1024,2048]{1,0:T(8,128)(2,1)S(1)} custom-call(bf16[1024,2048]{1,0:T(8,128)(2,1)} %orbitals_ref.2), custom_call_target="tpu_custom_call" | custom-call | bytes 8388608 | tf_op jit(solution)/shard_map/hold/pallas_call | solution.py:160
  56.1 0.0 copy-start.1
  56.1 0.0 collective-permute-done.1.other_ref
  56.1 1.8 %fit.1 = (bf16[32,32,256]{2,1,0:T(8,128)(2,1)S(1)}, bf16[32,32,256]{2,1,0:T(8,128)(2,1)S(1)}) custom-call(s32[1]{0:T(128)} %bitcast.core_ref, bf16[1024,128]{1,0:T(8,128)(2,1)S(1)} %bitcast.18, bf16[1024,128]{1,0:T(8,128)(2,1)S(1)} %collective-permute-done.1.other_ref, bf16[256,256]{1,0:T(8,128)(2,1)S(1)} %get-tuple-element.23.table_ref, ...), custom_call_target="tpu_custom_call" | custom-call | tf_op jit(solution)/shard_map/fit/pallas_call | solution.py:193
  57.9 0.1 collective-permute-start.2
  58.0 1.9 %collective-permute-done.2.far_ref = bf16[32,32,256]{2,1,0:T(8,128)(2,1)S(1)} collective-permute-done((bf16[32,32,256]{2,1,0:T(8,128)(2,1)S(1)}, bf16[32,32,256]{2,1,0:T(8,128)(2,1)S(1)}, u32[]{:S(2)}, u32[]{:S(2)}) %collective-permute-start.2) | collective-permute-done | bytes 524320 | tf_op jit(solution)/shard_map/ppermute | solution.py:280
  59.9 0.0 copy-done.1
  59.9 2.3 %y_transform.1 = bf16[32,2,2,16,256]{4,3,2,1,0:T(8,128)(2,1)} custom-call(s32[1]{0:T(128)} %bitcast.core_ref, bf16[32,32,256]{2,1,0:T(8,128)(2,1)S(1)} %get-tuple-element.25.near_ref, bf16[32,32,256]{2,1,0:T(8,128)(2,1)S(1)} %collective-permute-done.2.far_ref, bf16[1024,1024]{1,0:T(8,128)(2,1)S(1)} %copy-done.1), custom_call_target="tpu_custom_call" | custom-call | tf_op jit(solution)/shard_map/y_transform/pallas_call | solution.py:219
  62.2 7.7 %all-to-all-start.2 = ((bf16[128,16,256]{2,1,0:T(8,128)(2,1)}), bf16[128,16,256]{2,1,0:T(8,128)(2,1)S(1)}, u32[]{:S(2)}, u32[]{:S(2)}) async-start(bf16[128,16,256]{2,1,0:T(8,128)(2,1)} %bitcast.5), calls=%async_computation.2 | async-start | bytes 2097152 | tf_op jit(solution)/shard_map/all_to_all | solution.py:284
  70.0 0.9 fusion.14
  70.9 1.0 compare_and_fusion
  71.9 3.0 %fusion.2.screen_ref = f32[1024,128]{1,0:T(8,128)} fusion(s32[1024]{0:T(1024)S(1)} %get-tuple-element.56, s32[1024]{0:T(1024)S(1)} %get-tuple-element.58, s32[]{:T(128)S(6)} %mul.81, s32[]{:T(128)S(6)} %select_n.333, s32[1024]{0:T(1024)S(1)} %get-tuple-element.57, s32[1024]{0:T(1024)S(1)} %get-tuple-element.61, s32[1024]{0:T(1024)S(1)} %get-tuple-element.55, ...), kind=kLoop, calls=%fused_computation.27 | loop fusion | flops 9175040 | bytes 551945 | tf_op jit(solution)/shard_map/mul | solution.py:79
  74.9 22.4 %all-to-all-done.2 = bf16[128,16,256]{2,1,0:T(8,128)(2,1)S(1)} async-done(((bf16[128,16,256]{2,1,0:T(8,128)(2,1)}), bf16[128,16,256]{2,1,0:T(8,128)(2,1)S(1)}, u32[]{:S(2)}, u32[]{:S(2)}) %all-to-all-start.2) | async-done | bytes 1048608 | tf_op jit(solution)/shard_map/all_to_all | solution.py:284
  97.3 0.0 copy-start.2
  97.3 1.0 copy-done.2
  98.4 2.2 %gram.1 = (f32[64,2,8,128]{3,2,1,0:T(8,128)S(1)}, f32[64,2,8,128]{3,2,1,0:T(8,128)S(1)}) custom-call(s32[1]{0:T(128)} %bitcast.core_ref, bf16[64,2,16,256]{3,2,1,0:T(8,128)(2,1)S(1)} %bitcast.16, bf16[1024,1024]{1,0:T(8,128)(2,1)S(1)} %get-tuple-element.28.table_ref, f32[1024,128]{1,0:T(8,128)S(1)} %copy-done.2, f32[256,128]{1,0:T(8,128)S(1)} %fusion.40.mixed_ref), custom_call_target="tpu_custom_call" | custom-call | tf_op jit(solution)/shard_map/gram/pallas_call | solution.py:267
  100.6 2.4 %collective-permute-start.3 = (f32[64,2,8,128]{3,2,1,0:T(8,128)S(1)}, f32[64,2,8,128]{3,2,1,0:T(8,128)S(1)}, u32[]{:S(2)}, u32[]{:S(2)}) collective-permute-start(f32[64,2,8,128]{3,2,1,0:T(8,128)S(1)} %get-tuple-element.30), channel_id=1, source_target_pairs={{0,2},{2,0},{1,3},{3,1},{4,6},{6,4},{5,7},{7,5},{8,10},{10,8},{9,1... | collective-permute-start | bytes 1572872 | tf_op jit(solution)/shard_map/ppermute | solution.py:280
  103.0 1.5 %collective-permute-done.3 = f32[64,2,8,128]{3,2,1,0:T(8,128)S(1)} collective-permute-done((f32[64,2,8,128]{3,2,1,0:T(8,128)S(1)}, f32[64,2,8,128]{3,2,1,0:T(8,128)S(1)}, u32[]{:S(2)}, u32[]{:S(2)}) %collective-permute-start.3) | collective-permute-done | bytes 524320 | tf_op jit(solution)/shard_map/ppermute | solution.py:280
  104.6 0.9 add.199
  105.5 8.7 %all-to-all-start.3 = ((f32[128,8,128]{2,1,0:T(8,128)}), f32[128,8,128]{2,1,0:T(8,128)S(1)}, u32[]{:S(2)}, u32[]{:S(2)}) async-start(f32[128,8,128]{2,1,0:T(8,128)} %bitcast.7), calls=%async_computation.3 | async-start | bytes 1048576 | tf_op jit(solution)/shard_map/all_to_all | solution.py:284
  114.2 16.3 %all-to-all-done.3 = f32[128,8,128]{2,1,0:T(8,128)S(1)} async-done(((f32[128,8,128]{2,1,0:T(8,128)}), f32[128,8,128]{2,1,0:T(8,128)S(1)}, u32[]{:S(2)}, u32[]{:S(2)}) %all-to-all-start.3) | async-done | bytes 524320 | tf_op jit(solution)/shard_map/all_to_all | solution.py:284
  130.6 0.1 reduce_sum.22
  130.7 2.8 %collective-permute-start.4 = (f32[4,128]{1,0:T(4,128)S(1)}, f32[4,128]{1,0:T(4,128)S(1)}, u32[]{:S(2)}, u32[]{:S(2)}) collective-permute-start(f32[4,128]{1,0:T(4,128)S(1)} %get-tuple-element.34), channel_id=1, source_target_pairs={{0,2},{2,0},{1,3},{3,1},{4,6},{6,4},{5,7},{7,5},{8,10},{10,8},{9,1... | collective-permute-start | bytes 6152 | tf_op jit(solution)/shard_map/ppermute | solution.py:280
  133.5 0.8 collective-permute-done.4
  134.3 0.6 fusion.55
  (20 shorter events, 0.1 us)
Async XLA Ops:
  4.1 5.1 %collective-permute-start = (bf16[1024,128]{1,0:T(8,128)(2,1)S(1)}, bf16[1024,128]{1,0:T(8,128)(2,1)S(1)}, u32[]{:S(2)}, u32[]{:S(2)}) collective-permute-start(bf16[1024,128]{1,0:T(8,128)(2,1)S(1)} %get-tuple-element.19), channel_id=1, source_target_pairs={{0,2},{2,0},{1,3},{3,1},{4,6},{6,4},{5,7},{7,5},{8,10},{10,8},{9,1... | collective-permute-start | bytes 786440 | tf_op jit(solution)/shard_map/ppermute | solution.py:280
  10.1 22.9 %all-to-all-start = ((bf16[64,16,128]{2,1,0:T(8,128)(2,1)}), bf16[64,16,128]{2,1,0:T(8,128)(2,1)S(1)}, u32[]{:S(2)}, u32[]{:S(2)}) async-start(bf16[64,16,128]{2,1,0:T(8,128)(2,1)} %bitcast.3), calls=%async_computation | async-start | bytes 524288 | tf_op jit(solution)/shard_map/all_to_all | solution.py:284
  33.8 16.6 %all-to-all-start.1 = ((bf16[64,16,128]{2,1,0:T(8,128)(2,1)}), bf16[64,16,128]{2,1,0:T(8,128)(2,1)S(1)}, u32[]{:S(2)}, u32[]{:S(2)}) async-start(bf16[64,16,128]{2,1,0:T(8,128)(2,1)} %broadcast_in_dim.56), calls=%async_computation.1 | async-start | bytes 524288 | tf_op jit(solution)/shard_map/all_to_all | solution.py:284
  42.6 1.4 %copy-start = (bf16[1024,1024]{1,0:T(8,128)(2,1)}, bf16[1024,1024]{1,0:T(8,128)(2,1)S(1)}, u32[]{:S(2)}) copy-start(bf16[1024,1024]{1,0:T(8,128)(2,1)S(1)} %get-tuple-element.27.table_ref) | copy-start | bytes 6291460
  50.3 5.8 %collective-permute-start.1 = (bf16[1024,128]{1,0:T(8,128)(2,1)S(1)}, bf16[1024,128]{1,0:T(8,128)(2,1)S(1)}, u32[]{:S(2)}, u32[]{:S(2)}) collective-permute-start(bf16[1024,128]{1,0:T(8,128)(2,1)S(1)} %bitcast.17), channel_id=1, source_target_pairs={{0,2},{2,0},{1,3},{3,1},{4,6},{6,4},{5,7},{7,5},{8,10},{10,8},{9,1... | collective-permute-start | bytes 786440 | tf_op jit(solution)/shard_map/ppermute | solution.py:280
  56.1 3.9 %copy-start.1 = (bf16[1024,1024]{1,0:T(8,128)(2,1)S(1)}, bf16[1024,1024]{1,0:T(8,128)(2,1)}, u32[]{:S(2)}) copy-start(bf16[1024,1024]{1,0:T(8,128)(2,1)} %copy-done) | copy-start | bytes 6291460
  57.9 2.0 %collective-permute-start.2 = (bf16[32,32,256]{2,1,0:T(8,128)(2,1)S(1)}, bf16[32,32,256]{2,1,0:T(8,128)(2,1)S(1)}, u32[]{:S(2)}, u32[]{:S(2)}) collective-permute-start(bf16[32,32,256]{2,1,0:T(8,128)(2,1)S(1)} %get-tuple-element.26), channel_id=1, source_target_pairs={{0,2},{2,0},{1,3},{3,1},{4,6},{6,4},{5,7},{7,5},{8,10},{10,8},{9,1... | collective-permute-start | bytes 1572872 | tf_op jit(solution)/shard_map/ppermute | solution.py:280
  62.2 35.1 %all-to-all-start.2 = ((bf16[128,16,256]{2,1,0:T(8,128)(2,1)}), bf16[128,16,256]{2,1,0:T(8,128)(2,1)S(1)}, u32[]{:S(2)}, u32[]{:S(2)}) async-start(bf16[128,16,256]{2,1,0:T(8,128)(2,1)} %bitcast.5), calls=%async_computation.2 | async-start | bytes 2097152 | tf_op jit(solution)/shard_map/all_to_all | solution.py:284
  97.3 1.0 copy-start.2
  100.6 4.0 %collective-permute-start.3 = (f32[64,2,8,128]{3,2,1,0:T(8,128)S(1)}, f32[64,2,8,128]{3,2,1,0:T(8,128)S(1)}, u32[]{:S(2)}, u32[]{:S(2)}) collective-permute-start(f32[64,2,8,128]{3,2,1,0:T(8,128)S(1)} %get-tuple-element.30), channel_id=1, source_target_pairs={{0,2},{2,0},{1,3},{3,1},{4,6},{6,4},{5,7},{7,5},{8,10},{10,8},{9,1... | collective-permute-start | bytes 1572872 | tf_op jit(solution)/shard_map/ppermute | solution.py:280
  105.5 25.1 %all-to-all-start.3 = ((f32[128,8,128]{2,1,0:T(8,128)}), f32[128,8,128]{2,1,0:T(8,128)S(1)}, u32[]{:S(2)}, u32[]{:S(2)}) async-start(f32[128,8,128]{2,1,0:T(8,128)} %bitcast.7), calls=%async_computation.3 | async-start | bytes 1048576 | tf_op jit(solution)/shard_map/all_to_all | solution.py:284
  130.7 3.6 %collective-permute-start.4 = (f32[4,128]{1,0:T(4,128)S(1)}, f32[4,128]{1,0:T(4,128)S(1)}, u32[]{:S(2)}, u32[]{:S(2)}) collective-permute-start(f32[4,128]{1,0:T(4,128)S(1)} %get-tuple-element.34), channel_id=1, source_target_pairs={{0,2},{2,0},{1,3},{3,1},{4,6},{6,4},{5,7},{7,5},{8,10},{10,8},{9,1... | collective-permute-start | bytes 6152 | tf_op jit(solution)/shard_map/ppermute | solution.py:280

commit v3 on v2

--- a/solution.py
+++ b/solution.py
@@ -121,33 +121,36 @@
     )(y_small, x_small)
 
 
-def pick_kernel(offsets_ref, orbitals_ref, own_ref, other_ref, held_ref, hot_ref, sem):
+def pick_kernel(place_ref, points_ref, orbitals_ref, own_ref, other_ref, held_ref, hot_ref, got_ref, sem):
     copy = pltpu.make_async_copy(orbitals_ref, held_ref, sem)
     copy.start()
-    cell = iota((2048, NFIT), 0)
-    hot_ref[...] = jnp.where(cell == offsets_ref[...], F32(1.0), F32(0.0)).astype(BF16)
+    cell = iota((2048, NFIT), 0) + place_ref[1]
+    hot_ref[...] = jnp.where(cell == points_ref[...], F32(1.0), F32(0.0)).astype(BF16)
     copy.wait()
-    got = jnp.dot(held_ref[...], hot_ref[...], preferred_element_type=F32).astype(BF16)
-    own_ref[...] = got[:, :HALF]
-    other_ref[...] = got[:, HALF:]
-
-
-def pick(offsets, orbitals):
+    got_ref[...] = jnp.dot(held_ref[...], hot_ref[...], preferred_element_type=F32).astype(BF16)
+    mine = pl.multiple_of(place_ref[0] * HALF, HALF)
+    theirs = pl.multiple_of((1 - place_ref[0]) * HALF, HALF)
+    own_ref[...] = got_ref[:, pl.ds(mine, HALF)]
+    other_ref[...] = got_ref[:, pl.ds(theirs, HALF)]
+
+
+def pick(place, points, orbitals):
     half = jax.ShapeDtypeStruct((NORB, HALF), BF16)
     vmem = pl.BlockSpec(memory_space=pltpu.VMEM)
     return pl.pallas_call(
         pick_kernel,
         out_shape=(half, half),
-        in_specs=[vmem, pl.BlockSpec(memory_space=pltpu.HBM)],
+        in_specs=[pl.BlockSpec(memory_space=pltpu.SMEM), vmem, pl.BlockSpec(memory_space=pltpu.HBM)],
         out_specs=[vmem] * 2,
         scratch_shapes=[
             pltpu.VMEM((NORB, 2048), BF16),
             pltpu.VMEM((2048, NFIT), BF16),
+            pltpu.VMEM((NORB, NFIT), BF16),
             pltpu.SemaphoreType.DMA(()),
         ],
         compiler_params=pltpu.CompilerParams(vmem_limit_bytes=16 << 20),
         name="pick",
-    )(offsets, orbitals)
+    )(place, points, orbitals)
 
 
 def hold_kernel(orbitals_ref, held_ref, sem):
@@ -229,8 +232,20 @@
 
 
 def gram_kernel(
-    core_ref, planes_ref, table_ref, screen_ref, mixed_ref, own_ref, other_ref, coeffs_ref, weighted_ref
+    core_ref,
+    planes_ref,
+    table_ref,
+    screens_ref,
+    mixed_ref,
+    own_ref,
+    other_ref,
+    coeffs_ref,
+    weighted_ref,
+    screen_ref,
+    sem,
 ):
+    copy = pltpu.make_async_copy(screens_ref, screen_ref, sem)
+    copy.start()
     mixed = jnp.concatenate([mixed_ref[...]] * 2, axis=1)
     for b in range(2):
         rows = planes_ref[:, b].reshape(1024, NFIT)
@@ -240,6 +255,8 @@
             .astype(F32)
             for t in range(4)
         ]
+        if b == 0:
+            copy.wait()
         outs = (t0 - mixed * t3, mixed * t0 + t3, t2 + mixed * t1, mixed * t2 - t1)
         for o, value in enumerate(outs):
             at = slice(256 * o, 256 * o + 256)
@@ -268,9 +285,15 @@
         gram_kernel,
         out_shape=(half, half),
         in_specs=[pl.BlockSpec(memory_space=pltpu.SMEM)]
-        + [pl.BlockSpec(memory_space=pltpu.VMEM)] * 4,
+        + [pl.BlockSpec(memory_space=pltpu.VMEM)] * 2
+        + [pl.BlockSpec(memory_space=pltpu.HBM), pl.BlockSpec(memory_space=pltpu.VMEM)],
         out_specs=[pl.BlockSpec(memory_space=pltpu.VMEM)] * 2,
-        scratch_shapes=[pltpu.VMEM((1024, 512), BF16), pltpu.VMEM((2, 1024, 256), BF16)],
+        scratch_shapes=[
+            pltpu.VMEM((1024, 512), BF16),
+            pltpu.VMEM((2, 1024, 256), BF16),
+            pltpu.VMEM((1024, 128), F32),
+            pltpu.SemaphoreType.DMA(()),
+        ],
         compiler_params=pltpu.CompilerParams(vmem_limit_bytes=20 << 20),
         name="gram",
     )(core, planes, table, screen, mixed)
@@ -297,12 +320,11 @@
     z_table = jnp.where(z_row // 32 % 4 == z_column // N, z_table, F32(0.0)).astype(BF16)
     y_big, x_big = expand(small, x_table(y_pair == 0))
     screen, mixed = screen_rows(y_pair, z_group * 4)
-
-    halves = points[0].reshape(2, HALF)
-    halves = jnp.where(core == 0, halves, halves[::-1])
-    offsets = halves.reshape(1, NFIT) - (chip * 2 + core) * 2048
+    screen = pltpu.with_memory_space_constraint(screen, pltpu.HBM)
+
+    place = jnp.stack([core, (chip * 2 + core) * 2048]).astype(jnp.int32)
     orbitals = pltpu.with_memory_space_constraint(orbitals, pltpu.HBM)
-    own, other = pick(offsets, orbitals)
+    own, other = pick(place, points, orbitals)
     own = exchange((own + sibling(other)).reshape(N, 16, HALF), CHIPS)
     own = jnp.sum(own.astype(F32), axis=0).astype(BF16)
     own = exchange(jnp.broadcast_to(own[None], (N, 16, HALF)), CHIPS).reshape(NORB, HALF)

time: 135 us -> 135 us (level)
  no operation moved by 1% of the time
where the time goes in v3:
time: 135 us; the launch traced here: 134 us
  waiting for transfers between devices  59.3 us (44%)
  starting transfers between devices  45.1 us (33%)
  Pallas kernels  16.1 us (12%)
  other arithmetic  10.8 us (8%)
  local copies, waits for them, and re-layouts  2.78 us (2%)
    all_to_all x4, waiting for transfers between devices, exchange(): return lax.all_to_all(blocks, axes, split_axis=0, concat_axis=0, tiled=True)  54 us
    all_to_all x4, starting transfers between devices, exchange(): return lax.all_to_all(blocks, axes, split_axis=0, concat_axis=0, tiled=True)  33 us
    ppermute x5, starting transfers between devices, sibling(): return lax.ppermute(block, 'c', [(0, 1), (1, 0)])  12.2 us
    ppermute x5, waiting for transfers between devices, sibling(): return lax.ppermute(block, 'c', [(0, 1), (1, 0)])  5.3 us
    pallas_call x1, Pallas kernels, pick(): pl.pallas_call(pick_kernel, out_shape=(half, half), in_specs=[pl.BlockSpe...  4.05 us
    convert_element_type x1, other arithmetic, x_table(): return jnp.where(lone, jnp.where(kept, single, F32(0.0)), both).astype(BF16)  3.06 us
    pallas_call x1, Pallas kernels, expand(): pl.pallas_call(expand_kernel, out_shape=(big, big), grid=(4,), in_specs=[...  3.02 us
    mul x1, other arithmetic, screen_rows(): return (screen * copies, mixed)  2.96 us
  transfers between devices with their start and end apart: 9, of which 8 were waited for; matrix products, arithmetic and copies ran while one was open for 6% of the time, Pallas kernels for 4%

profile of v3, /device:TPU:1, one launch (start us, length us, event | category | flops | bytes accessed | tf_op | source)
XLA Modules:
  0.0 134.4 jit_solution(8382208388724300127)
XLA Ops:
  0.0 0.1 pad_add_fusion.place_ref
  0.1 0.0 copy-start.2
  0.1 0.7 copy-done.2
  0.8 4.1 %pick.1 = (bf16[1024,128]{1,0:T(8,128)(2,1)S(1)}, bf16[1024,128]{1,0:T(8,128)(2,1)S(1)}) custom-call(s32[2]{0:T(128)S(1)} %pad_add_fusion.place_ref, s32[1,256]{1,0:T(1,128)S(1)} %copy-done.2, bf16[1024,2048]{1,0:T(8,128)(2,1)} %orbitals_ref.2), custom_call_target="tpu_custom_call" | custom-call | tf_op jit(solution)/shard_map/pick/pallas_call | solution.py:140
  4.8 3.3 %collective-permute-start = (bf16[1024,128]{1,0:T(8,128)(2,1)S(1)}, bf16[1024,128]{1,0:T(8,128)(2,1)S(1)}, u32[]{:S(2)}, u32[]{:S(2)}) collective-permute-start(bf16[1024,128]{1,0:T(8,128)(2,1)S(1)} %get-tuple-element.19), channel_id=1, source_target_pairs={{0,2},{2,0},{1,3},{3,1},{4,6},{6,4},{5,7},{7,5},{8,10},{10,8},{9,1... | collective-permute-start | bytes 786440 | tf_op jit(solution)/shard_map/ppermute | solution.py:303
  8.2 1.0 collective-permute-done
  9.3 0.8 add.176
  10.0 11.0 %all-to-all-start = ((bf16[64,16,128]{2,1,0:T(8,128)(2,1)}), bf16[64,16,128]{2,1,0:T(8,128)(2,1)S(1)}, u32[]{:S(2)}, u32[]{:S(2)}) async-start(bf16[64,16,128]{2,1,0:T(8,128)(2,1)} %bitcast.2), calls=%async_computation | async-start | bytes 524288 | tf_op jit(solution)/shard_map/all_to_all | solution.py:307
  21.0 3.1 %fusion.19 = (bf16[256,256]{1,0:T(8,128)(2,1)S(1)}, bf16[256,256]{1,0:T(8,128)(2,1)S(1)}) fusion(s32[256]{0:T(256)S(1)} %get-tuple-element.43, s32[256]{0:T(256)S(1)} %get-tuple-element.49, s32[256]{0:T(256)S(1)} %get-tuple-element.44, s32[256]{0:T(256)S(1)} %get-tuple-element.50, s32[256]{0:T(256)S(1)} %get-tuple-element.45, s32[256]{0:T(256)S(1)} %get-tuple-element.47, ...), kind=kLoop, calls=%fused_computation.81 | loop fusion | flops 9502720 | bytes 274689 | tf_op jit(solution)/shard_map/convert_element_type | solution.py:57
  24.1 8.8 %all-to-all-done = bf16[64,16,128]{2,1,0:T(8,128)(2,1)S(1)} async-done(((bf16[64,16,128]{2,1,0:T(8,128)(2,1)}), bf16[64,16,128]{2,1,0:T(8,128)(2,1)S(1)}, u32[]{:S(2)}, u32[]{:S(2)}) %all-to-all-start) | async-done | bytes 262176 | tf_op jit(solution)/shard_map/all_to_all | solution.py:307
  32.9 0.1 reduce_sum.21
  33.0 0.7 broadcast_in_dim.56
  33.8 5.6 %all-to-all-start.1 = ((bf16[64,16,128]{2,1,0:T(8,128)(2,1)}), bf16[64,16,128]{2,1,0:T(8,128)(2,1)S(1)}, u32[]{:S(2)}, u32[]{:S(2)}) async-start(bf16[64,16,128]{2,1,0:T(8,128)(2,1)} %broadcast_in_dim.56), calls=%async_computation.1 | async-start | bytes 524288 | tf_op jit(solution)/shard_map/all_to_all | solution.py:307
  39.3 0.3 select_convert_fusion.1.y_small_ref
  39.6 3.0 %expand.1 = (bf16[1024,1024]{1,0:T(8,128)(2,1)S(1)}, bf16[1024,1024]{1,0:T(8,128)(2,1)S(1)}) custom-call(bf16[64,64]{1,0:T(8,128)(2,1)S(1)} %select_convert_fusion.1.y_small_ref, bf16[256,256]{1,0:T(8,128)(2,1)S(1)} %get-tuple-element.31.x_small_ref), custom_call_target="tpu_custom_call" | custom-call | flops 2147483648 | bytes 4194304 | tf_op jit(solution)/shard_map/expand/pallas_call | solution.py:109
  42.6 0.0 copy-start
  42.6 1.3 copy-done
  44.0 6.3 %all-to-all-done.1 = bf16[64,16,128]{2,1,0:T(8,128)(2,1)S(1)} async-done(((bf16[64,16,128]{2,1,0:T(8,128)(2,1)}), bf16[64,16,128]{2,1,0:T(8,128)(2,1)S(1)}, u32[]{:S(2)}, u32[]{:S(2)}) %all-to-all-start.1) | async-done | bytes 262176 | tf_op jit(solution)/shard_map/all_to_all | solution.py:307
  50.3 3.5 %collective-permute-start.1 = (bf16[1024,128]{1,0:T(8,128)(2,1)S(1)}, bf16[1024,128]{1,0:T(8,128)(2,1)S(1)}, u32[]{:S(2)}, u32[]{:S(2)}) collective-permute-start(bf16[1024,128]{1,0:T(8,128)(2,1)S(1)} %bitcast.16), channel_id=1, source_target_pairs={{0,2},{2,0},{1,3},{3,1},{4,6},{6,4},{5,7},{7,5},{8,10},{10,8},{9,1... | collective-permute-start | bytes 786440 | tf_op jit(solution)/shard_map/ppermute | solution.py:303
  53.9 2.2 %hold.1.orbitals_ref = bf16[1024,2048]{1,0:T(8,128)(2,1)S(1)} custom-call(bf16[1024,2048]{1,0:T(8,128)(2,1)} %orbitals_ref.2), custom_call_target="tpu_custom_call" | custom-call | bytes 8388608 | tf_op jit(solution)/shard_map/hold/pallas_call | solution.py:163
  56.1 0.0 copy-start.1
  56.1 0.0 collective-permute-done.1.other_ref
  56.1 1.8 %fit.1 = (bf16[32,32,256]{2,1,0:T(8,128)(2,1)S(1)}, bf16[32,32,256]{2,1,0:T(8,128)(2,1)S(1)}) custom-call(s32[1]{0:T(128)} %bitcast.core_ref, bf16[1024,128]{1,0:T(8,128)(2,1)S(1)} %bitcast.17, bf16[1024,128]{1,0:T(8,128)(2,1)S(1)} %collective-permute-done.1.other_ref, bf16[256,256]{1,0:T(8,128)(2,1)S(1)} %get-tuple-element.23.table_ref, ...), custom_call_target="tpu_custom_call" | custom-call | tf_op jit(solution)/shard_map/fit/pallas_call | solution.py:196
  57.9 0.1 collective-permute-start.2
  58.0 1.9 %collective-permute-done.2.far_ref = bf16[32,32,256]{2,1,0:T(8,128)(2,1)S(1)} collective-permute-done((bf16[32,32,256]{2,1,0:T(8,128)(2,1)S(1)}, bf16[32,32,256]{2,1,0:T(8,128)(2,1)S(1)}, u32[]{:S(2)}, u32[]{:S(2)}) %collective-permute-start.2) | collective-permute-done | bytes 524320 | tf_op jit(solution)/shard_map/ppermute | solution.py:303
  59.9 0.0 copy-done.1
  59.9 2.3 %y_transform.1 = bf16[32,2,2,16,256]{4,3,2,1,0:T(8,128)(2,1)} custom-call(s32[1]{0:T(128)} %bitcast.core_ref, bf16[32,32,256]{2,1,0:T(8,128)(2,1)S(1)} %get-tuple-element.25.near_ref, bf16[32,32,256]{2,1,0:T(8,128)(2,1)S(1)} %collective-permute-done.2.far_ref, bf16[1024,1024]{1,0:T(8,128)(2,1)S(1)} %copy-done.1), custom_call_target="tpu_custom_call" | custom-call | tf_op jit(solution)/shard_map/y_transform/pallas_call | solution.py:222
  62.2 7.7 %all-to-all-start.2 = ((bf16[128,16,256]{2,1,0:T(8,128)(2,1)}), bf16[128,16,256]{2,1,0:T(8,128)(2,1)S(1)}, u32[]{:S(2)}, u32[]{:S(2)}) async-start(bf16[128,16,256]{2,1,0:T(8,128)(2,1)} %bitcast.4), calls=%async_computation.2 | async-start | bytes 2097152 | tf_op jit(solution)/shard_map/all_to_all | solution.py:307
  70.0 0.9 fusion.14
  70.9 1.0 compare_and_fusion
  71.9 3.0 %fusion.2.screens_ref = f32[1024,128]{1,0:T(8,128)} fusion(s32[1024]{0:T(1024)S(1)} %get-tuple-element.56, s32[1024]{0:T(1024)S(1)} %get-tuple-element.58, s32[]{:T(128)S(6)} %mul.81, s32[]{:T(128)S(6)} %select_n.323, s32[1024]{0:T(1024)S(1)} %get-tuple-element.57, s32[1024]{0:T(1024)S(1)} %get-tuple-element.61, s32[1024]{0:T(1024)S(1)} %get-tuple-element.55, ...), kind=kLoop, calls=%fused_computation.27 | loop fusion | flops 9175040 | bytes 551945 | tf_op jit(solution)/shard_map/mul | solution.py:79
  74.9 22.4 %all-to-all-done.2 = bf16[128,16,256]{2,1,0:T(8,128)(2,1)S(1)} async-done(((bf16[128,16,256]{2,1,0:T(8,128)(2,1)}), bf16[128,16,256]{2,1,0:T(8,128)(2,1)S(1)}, u32[]{:S(2)}, u32[]{:S(2)}) %all-to-all-start.2) | async-done | bytes 1048608 | tf_op jit(solution)/shard_map/all_to_all | solution.py:307
  97.3 2.7 %gram.1 = (f32[64,2,8,128]{3,2,1,0:T(8,128)S(1)}, f32[64,2,8,128]{3,2,1,0:T(8,128)S(1)}) custom-call(s32[1]{0:T(128)} %bitcast.core_ref, bf16[64,2,16,256]{3,2,1,0:T(8,128)(2,1)S(1)} %bitcast.15, bf16[1024,1024]{1,0:T(8,128)(2,1)S(1)} %get-tuple-element.28.table_ref, f32[1024,128]{1,0:T(8,128)} %fusion.2.screens_ref, f32[256,128]{1,0:T(8,128)S(1)} %fusion.40.mixed_ref), custom_call_target="tpu_custom_call" | custom-call | tf_op jit(solution)/shard_map/gram/pallas_call | solution.py:284
  100.1 2.4 %collective-permute-start.3 = (f32[64,2,8,128]{3,2,1,0:T(8,128)S(1)}, f32[64,2,8,128]{3,2,1,0:T(8,128)S(1)}, u32[]{:S(2)}, u32[]{:S(2)}) collective-permute-start(f32[64,2,8,128]{3,2,1,0:T(8,128)S(1)} %get-tuple-element.30), channel_id=1, source_target_pairs={{0,2},{2,0},{1,3},{3,1},{4,6},{6,4},{5,7},{7,5},{8,10},{10,8},{9,1... | collective-permute-start | bytes 1572872 | tf_op jit(solution)/shard_map/ppermute | solution.py:303
  102.5 1.5 %collective-permute-done.3 = f32[64,2,8,128]{3,2,1,0:T(8,128)S(1)} collective-permute-done((f32[64,2,8,128]{3,2,1,0:T(8,128)S(1)}, f32[64,2,8,128]{3,2,1,0:T(8,128)S(1)}, u32[]{:S(2)}, u32[]{:S(2)}) %collective-permute-start.3) | collective-permute-done | bytes 524320 | tf_op jit(solution)/shard_map/ppermute | solution.py:303
  104.0 0.9 add.199
  104.9 8.7 %all-to-all-start.3 = ((f32[128,8,128]{2,1,0:T(8,128)}), f32[128,8,128]{2,1,0:T(8,128)S(1)}, u32[]{:S(2)}, u32[]{:S(2)}) async-start(f32[128,8,128]{2,1,0:T(8,128)} %bitcast.6), calls=%async_computation.3 | async-start | bytes 1048576 | tf_op jit(solution)/shard_map/all_to_all | solution.py:307
  113.7 16.3 %all-to-all-done.3 = f32[128,8,128]{2,1,0:T(8,128)S(1)} async-done(((f32[128,8,128]{2,1,0:T(8,128)}), f32[128,8,128]{2,1,0:T(8,128)S(1)}, u32[]{:S(2)}, u32[]{:S(2)}) %all-to-all-start.3) | async-done | bytes 524320 | tf_op jit(solution)/shard_map/all_to_all | solution.py:307
  130.0 0.1 reduce_sum.22
  130.2 2.8 %collective-permute-start.4 = (f32[4,128]{1,0:T(4,128)S(1)}, f32[4,128]{1,0:T(4,128)S(1)}, u32[]{:S(2)}, u32[]{:S(2)}) collective-permute-start(f32[4,128]{1,0:T(4,128)S(1)} %get-tuple-element.34), channel_id=1, source_target_pairs={{0,2},{2,0},{1,3},{3,1},{4,6},{6,4},{5,7},{7,5},{8,10},{10,8},{9,1... | collective-permute-start | bytes 6152 | tf_op jit(solution)/shard_map/ppermute | solution.py:303
  133.0 0.8 collective-permute-done.4
  133.8 0.6 fusion.55
  (19 shorter events, 0.1 us)
Async XLA Ops:
  0.1 0.7 copy-start.2
  4.8 4.5 %collective-permute-start = (bf16[1024,128]{1,0:T(8,128)(2,1)S(1)}, bf16[1024,128]{1,0:T(8,128)(2,1)S(1)}, u32[]{:S(2)}, u32[]{:S(2)}) collective-permute-start(bf16[1024,128]{1,0:T(8,128)(2,1)S(1)} %get-tuple-element.19), channel_id=1, source_target_pairs={{0,2},{2,0},{1,3},{3,1},{4,6},{6,4},{5,7},{7,5},{8,10},{10,8},{9,1... | collective-permute-start | bytes 786440 | tf_op jit(solution)/shard_map/ppermute | solution.py:303
  10.0 22.9 %all-to-all-start = ((bf16[64,16,128]{2,1,0:T(8,128)(2,1)}), bf16[64,16,128]{2,1,0:T(8,128)(2,1)S(1)}, u32[]{:S(2)}, u32[]{:S(2)}) async-start(bf16[64,16,128]{2,1,0:T(8,128)(2,1)} %bitcast.2), calls=%async_computation | async-start | bytes 524288 | tf_op jit(solution)/shard_map/all_to_all | solution.py:307
  33.8 16.6 %all-to-all-start.1 = ((bf16[64,16,128]{2,1,0:T(8,128)(2,1)}), bf16[64,16,128]{2,1,0:T(8,128)(2,1)S(1)}, u32[]{:S(2)}, u32[]{:S(2)}) async-start(bf16[64,16,128]{2,1,0:T(8,128)(2,1)} %broadcast_in_dim.56), calls=%async_computation.1 | async-start | bytes 524288 | tf_op jit(solution)/shard_map/all_to_all | solution.py:307
  42.6 1.4 %copy-start = (bf16[1024,1024]{1,0:T(8,128)(2,1)}, bf16[1024,1024]{1,0:T(8,128)(2,1)S(1)}, u32[]{:S(2)}) copy-start(bf16[1024,1024]{1,0:T(8,128)(2,1)S(1)} %get-tuple-element.27.table_ref) | copy-start | bytes 6291460
  50.3 5.8 %collective-permute-start.1 = (bf16[1024,128]{1,0:T(8,128)(2,1)S(1)}, bf16[1024,128]{1,0:T(8,128)(2,1)S(1)}, u32[]{:S(2)}, u32[]{:S(2)}) collective-permute-start(bf16[1024,128]{1,0:T(8,128)(2,1)S(1)} %bitcast.16), channel_id=1, source_target_pairs={{0,2},{2,0},{1,3},{3,1},{4,6},{6,4},{5,7},{7,5},{8,10},{10,8},{9,1... | collective-permute-start | bytes 786440 | tf_op jit(solution)/shard_map/ppermute | solution.py:303
  56.1 3.9 %copy-start.1 = (bf16[1024,1024]{1,0:T(8,128)(2,1)S(1)}, bf16[1024,1024]{1,0:T(8,128)(2,1)}, u32[]{:S(2)}) copy-start(bf16[1024,1024]{1,0:T(8,128)(2,1)} %copy-done) | copy-start | bytes 6291460
  57.9 2.0 %collective-permute-start.2 = (bf16[32,32,256]{2,1,0:T(8,128)(2,1)S(1)}, bf16[32,32,256]{2,1,0:T(8,128)(2,1)S(1)}, u32[]{:S(2)}, u32[]{:S(2)}) collective-permute-start(bf16[32,32,256]{2,1,0:T(8,128)(2,1)S(1)} %get-tuple-element.26), channel_id=1, source_target_pairs={{0,2},{2,0},{1,3},{3,1},{4,6},{6,4},{5,7},{7,5},{8,10},{10,8},{9,1... | collective-permute-start | bytes 1572872 | tf_op jit(solution)/shard_map/ppermute | solution.py:303
  62.2 35.1 %all-to-all-start.2 = ((bf16[128,16,256]{2,1,0:T(8,128)(2,1)}), bf16[128,16,256]{2,1,0:T(8,128)(2,1)S(1)}, u32[]{:S(2)}, u32[]{:S(2)}) async-start(bf16[128,16,256]{2,1,0:T(8,128)(2,1)} %bitcast.4), calls=%async_computation.2 | async-start | bytes 2097152 | tf_op jit(solution)/shard_map/all_to_all | solution.py:307
  100.1 4.0 %collective-permute-start.3 = (f32[64,2,8,128]{3,2,1,0:T(8,128)S(1)}, f32[64,2,8,128]{3,2,1,0:T(8,128)S(1)}, u32[]{:S(2)}, u32[]{:S(2)}) collective-permute-start(f32[64,2,8,128]{3,2,1,0:T(8,128)S(1)} %get-tuple-element.30), channel_id=1, source_target_pairs={{0,2},{2,0},{1,3},{3,1},{4,6},{6,4},{5,7},{7,5},{8,10},{10,8},{9,1... | collective-permute-start | bytes 1572872 | tf_op jit(solution)/shard_map/ppermute | solution.py:303
  104.9 25.1 %all-to-all-start.3 = ((f32[128,8,128]{2,1,0:T(8,128)}), f32[128,8,128]{2,1,0:T(8,128)S(1)}, u32[]{:S(2)}, u32[]{:S(2)}) async-start(f32[128,8,128]{2,1,0:T(8,128)} %bitcast.6), calls=%async_computation.3 | async-start | bytes 1048576 | tf_op jit(solution)/shard_map/all_to_all | solution.py:307
  130.2 3.6 %collective-permute-start.4 = (f32[4,128]{1,0:T(4,128)S(1)}, f32[4,128]{1,0:T(4,128)S(1)}, u32[]{:S(2)}, u32[]{:S(2)}) collective-permute-start(f32[4,128]{1,0:T(4,128)S(1)} %get-tuple-element.34), channel_id=1, source_target_pairs={{0,2},{2,0},{1,3},{3,1},{4,6},{6,4},{5,7},{7,5},{8,10},{10,8},{9,1... | collective-permute-start | bytes 6152 | tf_op jit(solution)/shard_map/ppermute | solution.py:303

commit v4 on v3

--- a/solution.py
+++ b/solution.py
@@ -11,12 +11,15 @@
 N = 64
 NORB = 1024
 NFIT = 256
-HALF = NFIT // 2
+HALF = NORB // 2
+CHIP_SLOTS = 16
+LINE_SLOTS = 64
 
 screen_rate = 0.05
 kernel_scale = 16.0
 
 CHIPS = ("yl", "x", "z")
+LINES = ("yl", "x")
 SAME_CORE = ("yl", "x", "z", "b")
 F32 = jnp.float32
 BF16 = jnp.bfloat16
@@ -79,78 +82,205 @@
     return screen * copies, mixed
 
 
-def expand_kernel(y_small_ref, x_small_ref, y_ref, x_ref):
-    block = pl.program_id(0)
-    row = 256 * block + iota((256, 1024), 0)
+def spread(small, row_of, column_of, first, rows, columns):
+    r = first + iota((rows, small.shape[0]), 0)
+    c = iota((small.shape[1], columns), 1)
+    left = jnp.where(row_of(r) == iota(r.shape, 1), F32(1.0), F32(0.0)).astype(BF16)
+    right = jnp.where(column_of(c) == iota(c.shape, 0), F32(1.0), F32(0.0)).astype(BF16)
+    tall = jnp.dot(left, small, preferred_element_type=F32).astype(BF16)
+    return jnp.dot(tall, right, preferred_element_type=F32)
+
+
+def expand_yz_kernel(core_ref, small_ref, z_ref, y_ref):
+    core = core_ref[0]
+    small = small_ref[...]
+    row, column = iota((256, 256), 0), iota((256, 256), 1)
+    wide = spread(
+        small,
+        lambda r: jnp.where(r < 128, core, 1 - core) * 32 + (r & 31),
+        lambda c: c & 63,
+        0,
+        256,
+        256,
+    )
+    same = ((row >> 5) & 3) == (column >> 6)
+    z_ref[...] = jnp.where(same, wide, F32(0.0)).astype(BF16)
     column = iota((256, 1024), 1)
-
-    def spread(small, row_of, column_of):
-        r = 256 * block + iota((256, small.shape[0]), 0)
-        c = iota((small.shape[1], 1024), 1)
-        left = jnp.where(row_of(r) == iota(r.shape, 1), F32(1.0), F32(0.0)).astype(BF16)
-        right = jnp.where(column_of(c) == iota(c.shape, 0), F32(1.0), F32(0.0)).astype(BF16)
-        tall = jnp.dot(left, small, preferred_element_type=F32).astype(BF16)
-        return jnp.dot(tall, right, preferred_element_type=F32)
-
-    wide = spread(y_small_ref[...], lambda r: (r >> 5) * 2 + ((r >> 3) & 1), lambda c: c >> 4)
-    same = (((row >> 4) & 1) == ((column >> 3) & 1)) & ((row & 7) == (column & 7))
-    y_ref[...] = jnp.where(same, wide, F32(0.0)).astype(BF16)
-    wide = spread(
-        x_small_ref[...],
-        lambda r: r >> 2,
-        lambda c: (c & 1) * 128 + ((c >> 3) & 1) * 64 + (c >> 4),
-    )
-    same = (row & 3) == ((column >> 1) & 3)
-    x_ref[...] = jnp.where(same, wide, F32(0.0)).astype(BF16)
-
-
-def expand(y_small, x_small):
-    big = jax.ShapeDtypeStruct((1024, 1024), BF16)
-    return pl.pallas_call(
-        expand_kernel,
-        out_shape=(big, big),
-        grid=(4,),
-        in_specs=[
-            pl.BlockSpec((N, N), lambda i: (0, 0)),
-            pl.BlockSpec((256, 256), lambda i: (0, 0)),
-        ],
-        out_specs=[pl.BlockSpec((256, 1024), lambda i: (i, 0))] * 2,
-        cost_estimate=pl.CostEstimate(flops=2**31, bytes_accessed=2**22, transcendentals=0),
+    for block in range(4):
+        row = 256 * block + iota((256, 1024), 0)
+        wide = spread(
+            small, lambda r: (r >> 5) * 2 + ((r >> 3) & 1), lambda c: c >> 4, 256 * block, 256, 1024
+        )
+        same = (((row >> 4) & 1) == ((column >> 3) & 1)) & ((row & 7) == (column & 7))
+        y_ref[256 * block : 256 * block + 256, :] = jnp.where(same, wide, F32(0.0)).astype(BF16)
+
+
+def expand_yz(core, small):
+    vmem = pl.BlockSpec(memory_space=pltpu.VMEM)
+    return pl.pallas_call(
+        expand_yz_kernel,
+        out_shape=(
+            jax.ShapeDtypeStruct((256, 256), BF16),
+            jax.ShapeDtypeStruct((1024, 1024), BF16),
+        ),
+        in_specs=[pl.BlockSpec(memory_space=pltpu.SMEM), vmem],
+        out_specs=[vmem] * 2,
         compiler_params=pltpu.CompilerParams(vmem_limit_bytes=16 << 20),
-        name="expand",
-    )(y_small, x_small)
-
-
-def pick_kernel(place_ref, points_ref, orbitals_ref, own_ref, other_ref, held_ref, hot_ref, got_ref, sem):
+        cost_estimate=pl.CostEstimate(flops=2**30, bytes_accessed=2**21, transcendentals=0),
+        name="expand_yz",
+    )(core, small)
+
+
+def expand_x_kernel(small_ref, x_ref):
+    column = iota((256, 1024), 1)
+    for block in range(4):
+        row = 256 * block + iota((256, 1024), 0)
+        wide = spread(
+            small_ref[...],
+            lambda r: r >> 2,
+            lambda c: (c & 1) * 128 + ((c >> 3) & 1) * 64 + (c >> 4),
+            256 * block,
+            256,
+            1024,
+        )
+        same = (row & 3) == ((column >> 1) & 3)
+        x_ref[256 * block : 256 * block + 256, :] = jnp.where(same, wide, F32(0.0)).astype(BF16)
+
+
+def expand_x(small):
+    vmem = pl.BlockSpec(memory_space=pltpu.VMEM)
+    return pl.pallas_call(
+        expand_x_kernel,
+        out_shape=jax.ShapeDtypeStruct((1024, 1024), BF16),
+        in_specs=[vmem],
+        out_specs=vmem,
+        compiler_params=pltpu.CompilerParams(vmem_limit_bytes=16 << 20),
+        cost_estimate=pl.CostEstimate(flops=2**31, bytes_accessed=2**21, transcendentals=0),
+        name="expand_x",
+    )(small)
+
+
+def pick_kernel(
+    place_ref, points_ref, orbitals_ref, own_ref, other_ref, ranks_ref, merge_ref, held_ref, got_ref, sem
+):
     copy = pltpu.make_async_copy(orbitals_ref, held_ref, sem)
     copy.start()
-    cell = iota((2048, NFIT), 0) + place_ref[1]
-    hot_ref[...] = jnp.where(cell == points_ref[...], F32(1.0), F32(0.0)).astype(BF16)
+    core, chip, base = place_ref[0], place_ref[1], place_ref[2]
+    points = points_ref[...]
+    columns = jnp.broadcast_to(points.astype(F32), (128, NFIT)).T.astype(jnp.int32)
+    column = jnp.concatenate([columns] * 2, axis=1)
+    before_row = iota((NFIT, NFIT), 0) < iota((NFIT, NFIT), 1)
+    before_column = iota((NFIT, NFIT), 1) < iota((NFIT, NFIT), 0)
+
+    def count(matches, axis):
+        return jnp.sum(jnp.where(matches, F32(1.0), F32(0.0)), axis=axis, keepdims=True)
+
+    same_chip = (column >> 12) == (points >> 12)
+    same_line = (column >> 15) == (points >> 15)
+    chip_rank = count(same_chip & before_row, 0).astype(jnp.int32)
+    line_rank = count(same_line & before_row, 0).astype(jnp.int32)
+    rank_column = count(same_chip & before_column, 1).astype(jnp.int32)
+    ranks_ref[0:1, :] = chip_rank
+    ranks_ref[1:2, :] = line_rank
+    ranks_ref[2:3, :] = points >> 15
+
+    slot = iota((NFIT, 128), 1)
+    chosen = ((columns >> 12) == chip) & (rank_column == slot)
+    offsets = jnp.max(
+        jnp.where(chosen, (columns - base).astype(F32), F32(-1.0)), axis=0, keepdims=True
+    ).astype(jnp.int32)
+    hot = jnp.where(iota((2048, 128), 0) == offsets, F32(1.0), F32(0.0)).astype(BF16)
+
+    to_slot = ((points >> 15) == (chip >> 3)) & (line_rank == iota((LINE_SLOTS, NFIT), 0))
+    from_slot = (((columns >> 12) & 7) == (slot >> 4)) & (rank_column == (slot & 15))
+    merge_ref[...] = jnp.dot(
+        jnp.where(to_slot, F32(1.0), F32(0.0)).astype(BF16),
+        jnp.where(from_slot, F32(1.0), F32(0.0)).astype(BF16),
+        preferred_element_type=F32,
+    ).astype(BF16)
+
     copy.wait()
-    got_ref[...] = jnp.dot(held_ref[...], hot_ref[...], preferred_element_type=F32).astype(BF16)
-    mine = pl.multiple_of(place_ref[0] * HALF, HALF)
-    theirs = pl.multiple_of((1 - place_ref[0]) * HALF, HALF)
-    own_ref[...] = got_ref[:, pl.ds(mine, HALF)]
-    other_ref[...] = got_ref[:, pl.ds(theirs, HALF)]
+    got = jnp.dot(held_ref[...], hot, preferred_element_type=F32)
+    got_ref[...] = got.T[:CHIP_SLOTS].astype(BF16)
+    own_ref[...] = got_ref[:, pl.ds(pl.multiple_of(core * HALF, HALF), HALF)]
+    other_ref[...] = got_ref[:, pl.ds(pl.multiple_of((1 - core) * HALF, HALF), HALF)]
 
 
 def pick(place, points, orbitals):
-    half = jax.ShapeDtypeStruct((NORB, HALF), BF16)
+    half = jax.ShapeDtypeStruct((CHIP_SLOTS, HALF), BF16)
     vmem = pl.BlockSpec(memory_space=pltpu.VMEM)
     return pl.pallas_call(
         pick_kernel,
-        out_shape=(half, half),
+        out_shape=(
+            half,
+            half,
+            jax.ShapeDtypeStruct((8, NFIT), jnp.int32),
+            jax.ShapeDtypeStruct((LINE_SLOTS, 128), BF16),
+        ),
         in_specs=[pl.BlockSpec(memory_space=pltpu.SMEM), vmem, pl.BlockSpec(memory_space=pltpu.HBM)],
-        out_specs=[vmem] * 2,
+        out_specs=[vmem] * 4,
         scratch_shapes=[
             pltpu.VMEM((NORB, 2048), BF16),
-            pltpu.VMEM((2048, NFIT), BF16),
-            pltpu.VMEM((NORB, NFIT), BF16),
+            pltpu.VMEM((CHIP_SLOTS, NORB), BF16),
             pltpu.SemaphoreType.DMA(()),
         ],
         compiler_params=pltpu.CompilerParams(vmem_limit_bytes=16 << 20),
         name="pick",
     )(place, points, orbitals)
+
+
+def merge_kernel(merge_ref, slots_ref, out_ref):
+    got = jnp.dot(
+        merge_ref[...], slots_ref[...].reshape(128, HALF), preferred_element_type=F32
+    ).astype(BF16)
+    for i in range(8):
+        out_ref[i] = got
+
+
+def merge(table, slots):
+    vmem = pl.BlockSpec(memory_space=pltpu.VMEM)
+    return pl.pallas_call(
+        merge_kernel,
+        out_shape=jax.ShapeDtypeStruct((8, LINE_SLOTS, HALF), BF16),
+        in_specs=[vmem] * 2,
+        out_specs=vmem,
+        compiler_params=pltpu.CompilerParams(vmem_limit_bytes=8 << 20),
+        name="merge",
+    )(table, slots)
+
+
+def order_kernel(ranks_ref, slots_ref, out_ref):
+    row = iota((8 * LINE_SLOTS, NFIT), 0)
+    here = ((row >> 6) == ranks_ref[2:3, :]) & ((row & 63) == ranks_ref[1:2, :])
+    out_ref[...] = lax.dot_general(
+        slots_ref[...].reshape(8 * LINE_SLOTS, HALF),
+        jnp.where(here, F32(1.0), F32(0.0)).astype(BF16),
+        (((0,), (0,)), ((), ())),
+        preferred_element_type=F32,
+    ).astype(BF16)
+
+
+def order(ranks, slots):
+    vmem = pl.BlockSpec(memory_space=pltpu.VMEM)
+    return pl.pallas_call(
+        order_kernel,
+        out_shape=jax.ShapeDtypeStruct((HALF, NFIT), BF16),
+        in_specs=[vmem] * 2,
+        out_specs=vmem,
+        compiler_params=pltpu.CompilerParams(vmem_limit_bytes=8 << 20),
+        name="order",
+    )(ranks, slots)
+
+
+def any_points(points, orbitals, core, base):
+    cell = iota((2048, NFIT), 0) + base
+    hot = jnp.where(cell == points, F32(1.0), F32(0.0)).astype(BF16)
+    got = jnp.dot(orbitals, hot, preferred_element_type=F32).astype(BF16)
+    own = lax.dynamic_slice_in_dim(got, core * HALF, HALF, 0)
+    other = lax.dynamic_slice_in_dim(got, (1 - core) * HALF, HALF, 0)
+    own = exchange((own + sibling(other)).reshape(N, 8, NFIT), CHIPS)
+    own = jnp.sum(own.astype(F32), axis=0).astype(BF16)
+    return exchange(jnp.broadcast_to(own[None], (N, 8, NFIT)), CHIPS).reshape(HALF, NFIT)
 
 
 def hold_kernel(orbitals_ref, held_ref, sem):
@@ -176,8 +306,8 @@
     core = core_ref[0]
     mine = pl.multiple_of(core * HALF, HALF)
     theirs = pl.multiple_of((1 - core) * HALF, HALF)
-    values_ref[:, pl.ds(mine, HALF)] = own_ref[...]
-    values_ref[:, pl.ds(theirs, HALF)] = other_ref[...]
+    values_ref[pl.ds(mine, HALF), :] = own_ref[...]
+    values_ref[pl.ds(theirs, HALF), :] = other_ref[...]
     density = lax.dot_general(
         orbitals_ref[...], values_ref[...], (((0,), (0,)), ((), ())), preferred_element_type=F32
     )
@@ -313,26 +443,33 @@
     chip = lax.axis_index(CHIPS)
     core_word = core.astype(jnp.int32)[None]
     y_pair, z_group = chip // 2, core * 4 + chip % 2 * 2 + batch
+    base = (chip * 2 + core) * 2048
+    place = jnp.stack([core, chip, base]).astype(jnp.int32)
+    own, other, ranks, merge_table = pick(place, points, orbitals)
+    own = own + sibling(other)
+    slots = exchange(jnp.broadcast_to(own[None], (8, CHIP_SLOTS, HALF)), ("z",))
+
     small = pair_table(iota((N, N), 0), iota((N, N), 1)).astype(BF16)
-    z_row, z_column = iota((256, 256), 0), iota((256, 256), 1)
-    z_half = jnp.where(z_row < 128, core, 1 - core)
-    z_table = pair_table(z_half * 32 + z_row % 32, z_column % N)
-    z_table = jnp.where(z_row // 32 % 4 == z_column // N, z_table, F32(0.0)).astype(BF16)
-    y_big, x_big = expand(small, x_table(y_pair == 0))
-    screen, mixed = screen_rows(y_pair, z_group * 4)
-    screen = pltpu.with_memory_space_constraint(screen, pltpu.HBM)
-
-    place = jnp.stack([core, (chip * 2 + core) * 2048]).astype(jnp.int32)
-    orbitals = pltpu.with_memory_space_constraint(orbitals, pltpu.HBM)
-    own, other = pick(place, points, orbitals)
-    own = exchange((own + sibling(other)).reshape(N, 16, HALF), CHIPS)
-    own = jnp.sum(own.astype(F32), axis=0).astype(BF16)
-    own = exchange(jnp.broadcast_to(own[None], (N, 16, HALF)), CHIPS).reshape(NORB, HALF)
-    own, z_table, y_big, x_big, orbitals = lax.optimization_barrier(
-        (own, z_table, y_big, x_big, orbitals)
+    z_table, y_big = expand_yz(core_word, small)
+    full = (jnp.max(ranks[0]) >= CHIP_SLOTS) | (jnp.max(ranks[1]) >= LINE_SLOTS)
+    full = jnp.where(full, F32(1.0), F32(0.0))[None]
+    slots, z_table, y_big, full = lax.optimization_barrier((slots, z_table, y_big, full))
+    slots = exchange(merge(merge_table, slots), LINES)
+    full = full + lax.ppermute(full, "b", [(0, 1), (1, 0)])
+    x_small = x_table(y_pair == 0)
+    slots, full, x_small, orbitals = lax.optimization_barrier((slots, full, x_small, orbitals))
+    own = order(ranks, slots)
+    own = lax.cond(
+        full[0] > 0,
+        lambda o: any_points(points, orbitals, core, base),
+        lambda o: o,
+        own,
     )
     held = hold(orbitals)
     near, far = fit(core_word, own, sibling(own), z_table, held)
+    x_big = expand_x(x_small)
+    screen, mixed = screen_rows(y_pair, z_group * 4)
+    screen = pltpu.with_memory_space_constraint(screen, pltpu.HBM)
     planes = y_transform(core_word, near, sibling(far), y_big)
     planes = exchange(planes.reshape(128, 16, NFIT), SAME_CORE).reshape(N, 2, 16, NFIT)
     own, other = gram(core_word, planes, x_big, screen, mixed)

time: 135 us -> 123 us (0.911)
  waiting for transfers between devices: 59.3 us -> 51.1 us
  starting transfers between devices: 45.1 us -> 41.6 us
  local copies, waits for them, and re-layouts: 2.78 us -> 0.67 us
  between operations: 0.29 us -> 2.23 us
  other arithmetic: 10.8 us -> 9.26 us
    all_to_all x4, waiting for transfers between devices: 54 us -> 46.1 us  [exchange(): return lax.all_to_all(blocks, axes, split_axis=0, concat_axis=0, tiled=True)]
    all_to_all x4, starting transfers between devices: 33 us -> 27.8 us  [exchange(): return lax.all_to_all(blocks, axes, split_axis=0, concat_axis=0, tiled=True)]
    ppermute x0 -> x1, starting transfers between devices: none -> 3.43 us  [on_device(): full = full + lax.ppermute(full, 'b', [(0, 1), (1, 0)])]
    unnamed x6 -> x2, local copies, waits for them, and re-layouts: 2.03 us -> 0.01 us
    ppermute x5, starting transfers between devices: 12.2 us -> 10.4 us  [sibling(): return lax.ppermute(block, 'c', [(0, 1), (1, 0)])]
    pallas_call x2 -> x5, Pallas kernels: 7.07 us -> 8.4 us  [the longest x1 4.34 us: pick(): pl.pallas_call(pick_kernel, out_shape=(half, half, jax.ShapeDtypeStruct((...]
  transfers between devices with their start and end apart: 9 -> 10, of which waited for: 8 -> 8; matrix products, arithmetic and copies ran while one was open for 6% -> 6% of each run, Pallas kernels for 4% -> 4%
where the time goes in v4:
time: 123 us; the launch traced here: 122 us
  waiting for transfers between devices  51.1 us (42%)
  starting transfers between devices  41.6 us (34%)
  Pallas kernels  17.4 us (14%)
  other arithmetic  9.26 us (8%)
  between operations  2.23 us (2%)
    all_to_all x4, waiting for transfers between devices, exchange(): return lax.all_to_all(blocks, axes, split_axis=0, concat_axis=0, tiled=True)  46.1 us
    all_to_all x4, starting transfers between devices, exchange(): return lax.all_to_all(blocks, axes, split_axis=0, concat_axis=0, tiled=True)  27.8 us
    ppermute x5, starting transfers between devices, sibling(): return lax.ppermute(block, 'c', [(0, 1), (1, 0)])  10.4 us
    pallas_call x1, Pallas kernels, pick(): pl.pallas_call(pick_kernel, out_shape=(half, half, jax.ShapeDtypeStruct((...  4.34 us
    ppermute x5, waiting for transfers between devices, sibling(): return lax.ppermute(block, 'c', [(0, 1), (1, 0)])  4.26 us
    ppermute x1, starting transfers between devices, on_device(): full = full + lax.ppermute(full, 'b', [(0, 1), (1, 0)])  3.43 us
    mul x1, other arithmetic, screen_rows(): return (screen * copies, mixed)  2.93 us
    pallas_call x1, Pallas kernels, gram(): pl.pallas_call(gram_kernel, out_shape=(half, half), in_specs=[pl.BlockSpe...  2.76 us
  transfers between devices with their start and end apart: 10, of which 8 were waited for; matrix products, arithmetic and copies ran while one was open for 6% of the time, Pallas kernels for 4%

profile of v4, /device:TPU:1, one launch (start us, length us, event | category | flops | bytes accessed | tf_op | source)
XLA Modules:
  0.0 122.3 jit_solution(2429199910552099769)
XLA Ops:
  0.0 0.1 pad_add_fusion.place_ref
  0.1 4.3 %pick.1 = (bf16[16,512]{1,0:T(8,128)(2,1)S(1)}, bf16[16,512]{1,0:T(8,128)(2,1)S(1)}, s32[8,256]{1,0:T(8,128)S(1)}, bf16[64,128]{1,0:T(8,128)(2,1)S(1)}) custom-call(s32[3]{0:T(128)S(1)} %pad_add_fusion.place_ref, s32[1,256]{1,0:T(1,128)} %points_ref.1, bf16[1024,2048]{1,0:T(8,128)(2,1)} %orbitals_ref.2), custom_call_target="tpu_custom_call" | custom-call | tf_op jit(solution)/shard_map/pick/pallas_call | solution.py:212
  4.4 3.3 %collective-permute-start.1 = (bf16[16,512]{1,0:T(8,128)(2,1)S(1)}, bf16[16,512]{1,0:T(8,128)(2,1)S(1)}, u32[]{:S(2)}, u32[]{:S(2)}) collective-permute-start(bf16[16,512]{1,0:T(8,128)(2,1)S(1)} %get-tuple-element.41), channel_id=1, source_target_pairs={{0,2},{2,0},{1,3},{3,1},{4,6},{6,4},{5,7},{7,5},{8,10},{10,8},{9,1... | collective-permute-start | bytes 49160 | tf_op jit(solution)/shard_map/ppermute | solution.py:433
  7.7 0.7 slice_reduce_fusion
  8.5 0.3 select_convert_fusion.2.small_ref
  8.7 0.0 collective-permute-done.1
  8.8 0.7 broadcast_in_dim.63
  9.4 6.5 %all-to-all-start.2 = ((bf16[8,16,512]{2,1,0:T(8,128)(2,1)}), bf16[8,16,512]{2,1,0:T(8,128)(2,1)S(1)}, u32[]{:S(2)}, u32[]{:S(2)}) async-start(bf16[8,16,512]{2,1,0:T(8,128)(2,1)} %broadcast_in_dim.63), calls=%async_computation.2 | async-start | bytes 262144 | tf_op jit(solution)/shard_map/all_to_all | solution.py:437
  15.9 1.4 %expand_yz.1 = (bf16[256,256]{1,0:T(8,128)(2,1)S(1)}, bf16[1024,1024]{1,0:T(8,128)(2,1)S(1)}) custom-call(s32[1]{0:T(128)} %bitcast.5.core_ref, bf16[64,64]{1,0:T(8,128)(2,1)S(1)} %select_convert_fusion.2.small_ref), custom_call_target="tpu_custom_call" | custom-call | flops 1073741824 | bytes 2097152 | tf_op jit(solution)/shard_map/expand_yz/pallas_call | solution.py:120
  17.3 0.0 copy-start
  18.6 5.7 %all-to-all-done.2.slots_ref = bf16[8,16,512]{2,1,0:T(8,128)(2,1)S(1)} async-done(((bf16[8,16,512]{2,1,0:T(8,128)(2,1)}), bf16[8,16,512]{2,1,0:T(8,128)(2,1)S(1)}, u32[]{:S(2)}, u32[]{:S(2)}) %all-to-all-start.2) | async-done | bytes 131104 | tf_op jit(solution)/shard_map/all_to_all | solution.py:437
  24.2 1.0 merge.1
  25.2 5.0 %all-to-all-start.3 = ((bf16[8,64,512]{2,1,0:T(8,128)(2,1)}), bf16[8,64,512]{2,1,0:T(8,128)(2,1)S(1)}, u32[]{:S(2)}, u32[]{:S(2)}) async-start(bf16[8,64,512]{2,1,0:T(8,128)(2,1)} %merge.1), calls=%async_computation.3 | async-start | bytes 1048576 | tf_op jit(solution)/shard_map/all_to_all | solution.py:437
  30.3 1.7 %fusion.25.small_ref = bf16[256,256]{1,0:T(8,128)(2,1)S(1)} fusion(s32[256]{0:T(256)S(1)} %get-tuple-element.69, s32[256]{0:T(256)S(1)} %get-tuple-element.70, s32[256]{0:T(256)S(1)} %get-tuple-element.67, s32[256]{0:T(256)S(1)} %get-tuple-element.73, s32[256]{0:T(256)S(1)} %get-tuple-element.68, s32[256]{0:T(256)S(1)} %get-tuple-element.74, ...), kind=kLoop, calls=%fused_computation.76 | loop fusion | flops 5570560 | bytes 137985 | tf_op jit(solution)/shard_map/convert_element_type | solution.py:60
  32.0 3.4 %collective-permute-start.2 = (f32[1]{0:T(128)}, f32[1]{0:T(128)}, u32[]{:S(2)}, u32[]{:S(2)}) collective-permute-start(f32[1]{0:T(128)} %bitcast.8), channel_id=1, source_target_pairs={{0,1},{1,0},{2,3},{3,2},{4,5},{5,4},{6,7},{7,6},{8,9},{9,8},{10,11... | collective-permute-start | bytes 20 | tf_op jit(solution)/shard_map/ppermute | solution.py:458
  35.5 0.7 collective-permute-done.2
  36.9 2.9 %all-to-all-done.3.slots_ref = bf16[8,64,512]{2,1,0:T(8,128)(2,1)S(1)} async-done(((bf16[8,64,512]{2,1,0:T(8,128)(2,1)}), bf16[8,64,512]{2,1,0:T(8,128)(2,1)S(1)}, u32[]{:S(2)}, u32[]{:S(2)}) %all-to-all-start.3) | async-done | bytes 524320 | tf_op jit(solution)/shard_map/all_to_all | solution.py:437
  39.8 0.4 order.1
  40.2 0.0 copy-done
  40.2 1.7 %collective-permute-start.3 = (bf16[512,256]{1,0:T(8,128)(2,1)S(1)}, bf16[512,256]{1,0:T(8,128)(2,1)S(1)}, u32[]{:S(2)}, u32[]{:S(2)}) collective-permute-start(bf16[512,256]{1,0:T(8,128)(2,1)S(1)} %get-tuple-element.83.own_ref), channel_id=1, source_target_pairs={{0,2},{2,0},{1,3},{3,1},{4,6},{6,4},{5,7},{7,5},{8,10},{10,8},{9,1... | collective-permute-start | bytes 786440 | tf_op jit(solution)/shard_map/ppermute | solution.py:433
  42.0 2.2 %hold.1.orbitals_ref = bf16[1024,2048]{1,0:T(8,128)(2,1)S(1)} custom-call(bf16[1024,2048]{1,0:T(8,128)(2,1)} %orbitals_ref.2), custom_call_target="tpu_custom_call" | custom-call | bytes 8388608 | tf_op jit(solution)/shard_map/hold/pallas_call | solution.py:293
  44.2 0.0 collective-permute-done.3.other_ref
  44.2 1.8 %fit.1 = (bf16[32,32,256]{2,1,0:T(8,128)(2,1)S(1)}, bf16[32,32,256]{2,1,0:T(8,128)(2,1)S(1)}) custom-call(s32[1]{0:T(128)} %bitcast.5.core_ref, bf16[512,256]{1,0:T(8,128)(2,1)S(1)} %get-tuple-element.83.own_ref, bf16[512,256]{1,0:T(8,128)(2,1)S(1)} %collective-permute-done.3.other_ref, bf16[256,256]{1,0:T(8,128)(2,1)S(1)} %get-tuple-element.50.table_ref, ...), custom_call_target="tpu_custom_call" | custom-call | tf_op jit(solution)/shard_map/fit/pallas_call | solution.py:326
  46.0 0.1 collective-permute-start.4
  46.1 1.9 %collective-permute-done.4.far_ref = bf16[32,32,256]{2,1,0:T(8,128)(2,1)S(1)} collective-permute-done((bf16[32,32,256]{2,1,0:T(8,128)(2,1)S(1)}, bf16[32,32,256]{2,1,0:T(8,128)(2,1)S(1)}, u32[]{:S(2)}, u32[]{:S(2)}) %collective-permute-start.4) | collective-permute-done | bytes 524320 | tf_op jit(solution)/shard_map/ppermute | solution.py:433
  48.0 2.3 %y_transform.1 = bf16[32,2,2,16,256]{4,3,2,1,0:T(8,128)(2,1)} custom-call(s32[1]{0:T(128)} %bitcast.5.core_ref, bf16[32,32,256]{2,1,0:T(8,128)(2,1)S(1)} %get-tuple-element.51.near_ref, bf16[32,32,256]{2,1,0:T(8,128)(2,1)S(1)} %collective-permute-done.4.far_ref, bf16[1024,1024]{1,0:T(8,128)(2,1)S(1)} %get-tuple-element.53.table_ref), custom_call_target="tpu_custom_call" | custom-call | tf_op jit(solution)/shard_map/y_transform/pallas_call | solution.py:352
  50.3 7.6 %all-to-all-start.4 = ((bf16[128,16,256]{2,1,0:T(8,128)(2,1)}), bf16[128,16,256]{2,1,0:T(8,128)(2,1)S(1)}, u32[]{:S(2)}, u32[]{:S(2)}) async-start(bf16[128,16,256]{2,1,0:T(8,128)(2,1)} %bitcast.10), calls=%async_computation.4 | async-start | bytes 2097152 | tf_op jit(solution)/shard_map/all_to_all | solution.py:437
  57.9 0.9 fusion.20
  58.8 1.0 compare_and_fusion
  59.8 2.9 %fusion.8.screens_ref = f32[1024,128]{1,0:T(8,128)} fusion(s32[1024]{0:T(1024)S(1)} %get-tuple-element.76, s32[1024]{0:T(1024)S(1)} %get-tuple-element.78, s32[]{:T(128)S(6)} %mul.77, s32[]{:T(128)S(6)} %select_n.283, s32[1024]{0:T(1024)S(1)} %get-tuple-element.77, s32[1024]{0:T(1024)S(1)} %get-tuple-element.81, s32[1024]{0:T(1024)S(1)} %get-tuple-element.75, ...), kind=kLoop, calls=%fused_computation.34 | loop fusion | flops 9175040 | bytes 551945 | tf_op jit(solution)/shard_map/mul | solution.py:82
  62.7 1.3 %expand_x.1.table_ref = bf16[1024,1024]{1,0:T(8,128)(2,1)S(1)} custom-call(bf16[256,256]{1,0:T(8,128)(2,1)S(1)} %fusion.25.small_ref), custom_call_target="tpu_custom_call" | custom-call | flops 2147483648 | bytes 2097152 | tf_op jit(solution)/shard_map/expand_x/pallas_call | solution.py:152
  64.1 21.1 %all-to-all-done.4 = bf16[128,16,256]{2,1,0:T(8,128)(2,1)S(1)} async-done(((bf16[128,16,256]{2,1,0:T(8,128)(2,1)}), bf16[128,16,256]{2,1,0:T(8,128)(2,1)S(1)}, u32[]{:S(2)}, u32[]{:S(2)}) %all-to-all-start.4) | async-done | bytes 1048608 | tf_op jit(solution)/shard_map/all_to_all | solution.py:437
  85.2 2.8 %gram.1 = (f32[64,2,8,128]{3,2,1,0:T(8,128)S(1)}, f32[64,2,8,128]{3,2,1,0:T(8,128)S(1)}) custom-call(s32[1]{0:T(128)} %bitcast.5.core_ref, bf16[64,2,16,256]{3,2,1,0:T(8,128)(2,1)S(1)} %bitcast.24, bf16[1024,1024]{1,0:T(8,128)(2,1)S(1)} %expand_x.1.table_ref, f32[1024,128]{1,0:T(8,128)} %fusion.8.screens_ref, f32[256,128]{1,0:T(8,128)S(1)} %fusion.40.mixed_ref), custom_call_target="tpu_custom_call" | custom-call | tf_op jit(solution)/shard_map/gram/pallas_call | solution.py:414
  88.0 2.4 %collective-permute-start.5 = (f32[64,2,8,128]{3,2,1,0:T(8,128)S(1)}, f32[64,2,8,128]{3,2,1,0:T(8,128)S(1)}, u32[]{:S(2)}, u32[]{:S(2)}) collective-permute-start(f32[64,2,8,128]{3,2,1,0:T(8,128)S(1)} %get-tuple-element.56), channel_id=1, source_target_pairs={{0,2},{2,0},{1,3},{3,1},{4,6},{6,4},{5,7},{7,5},{8,10},{10,8},{9,1... | collective-permute-start | bytes 1572872 | tf_op jit(solution)/shard_map/ppermute | solution.py:433
  90.4 1.5 %collective-permute-done.5 = f32[64,2,8,128]{3,2,1,0:T(8,128)S(1)} collective-permute-done((f32[64,2,8,128]{3,2,1,0:T(8,128)S(1)}, f32[64,2,8,128]{3,2,1,0:T(8,128)S(1)}, u32[]{:S(2)}, u32[]{:S(2)}) %collective-permute-start.5) | collective-permute-done | bytes 524320 | tf_op jit(solution)/shard_map/ppermute | solution.py:433
  92.0 0.9 add.187
  92.8 8.7 %all-to-all-start.5 = ((f32[128,8,128]{2,1,0:T(8,128)}), f32[128,8,128]{2,1,0:T(8,128)S(1)}, u32[]{:S(2)}, u32[]{:S(2)}) async-start(f32[128,8,128]{2,1,0:T(8,128)} %bitcast.12), calls=%async_computation.5 | async-start | bytes 1048576 | tf_op jit(solution)/shard_map/all_to_all | solution.py:437
  101.6 16.3 %all-to-all-done.5 = f32[128,8,128]{2,1,0:T(8,128)S(1)} async-done(((f32[128,8,128]{2,1,0:T(8,128)}), f32[128,8,128]{2,1,0:T(8,128)S(1)}, u32[]{:S(2)}, u32[]{:S(2)}) %all-to-all-start.5) | async-done | bytes 524320 | tf_op jit(solution)/shard_map/all_to_all | solution.py:437
  117.9 0.1 reduce_sum.21
  118.1 2.8 %collective-permute-start.6 = (f32[4,128]{1,0:T(4,128)S(1)}, f32[4,128]{1,0:T(4,128)S(1)}, u32[]{:S(2)}, u32[]{:S(2)}) collective-permute-start(f32[4,128]{1,0:T(4,128)S(1)} %get-tuple-element.60), channel_id=1, source_target_pairs={{0,2},{2,0},{1,3},{3,1},{4,6},{6,4},{5,7},{7,5},{8,10},{10,8},{9,1... | collective-permute-start | bytes 6152 | tf_op jit(solution)/shard_map/ppermute | solution.py:433
  120.9 0.8 collective-permute-done.6
  121.7 0.6 fusion.55
  (17 shorter events, 0.1 us)
Async XLA Ops:
  4.4 4.3 %collective-permute-start.1 = (bf16[16,512]{1,0:T(8,128)(2,1)S(1)}, bf16[16,512]{1,0:T(8,128)(2,1)S(1)}, u32[]{:S(2)}, u32[]{:S(2)}) collective-permute-start(bf16[16,512]{1,0:T(8,128)(2,1)S(1)} %get-tuple-element.41), channel_id=1, source_target_pairs={{0,2},{2,0},{1,3},{3,1},{4,6},{6,4},{5,7},{7,5},{8,10},{10,8},{9,1... | collective-permute-start | bytes 49160 | tf_op jit(solution)/shard_map/ppermute | solution.py:433
  9.4 14.8 %all-to-all-start.2 = ((bf16[8,16,512]{2,1,0:T(8,128)(2,1)}), bf16[8,16,512]{2,1,0:T(8,128)(2,1)S(1)}, u32[]{:S(2)}, u32[]{:S(2)}) async-start(bf16[8,16,512]{2,1,0:T(8,128)(2,1)} %broadcast_in_dim.63), calls=%async_computation.2 | async-start | bytes 262144 | tf_op jit(solution)/shard_map/all_to_all | solution.py:437
  17.3 22.9 %copy-start = (s32[1,256]{1,0:T(1,128)S(1)}, s32[1,256]{1,0:T(1,128)}, u32[]{:S(2)}) copy-start(s32[1,256]{1,0:T(1,128)} %points_ref.1) | copy-start | bytes 3076
  25.2 14.6 %all-to-all-start.3 = ((bf16[8,64,512]{2,1,0:T(8,128)(2,1)}), bf16[8,64,512]{2,1,0:T(8,128)(2,1)S(1)}, u32[]{:S(2)}, u32[]{:S(2)}) async-start(bf16[8,64,512]{2,1,0:T(8,128)(2,1)} %merge.1), calls=%async_computation.3 | async-start | bytes 1048576 | tf_op jit(solution)/shard_map/all_to_all | solution.py:437
  32.0 4.2 %collective-permute-start.2 = (f32[1]{0:T(128)}, f32[1]{0:T(128)}, u32[]{:S(2)}, u32[]{:S(2)}) collective-permute-start(f32[1]{0:T(128)} %bitcast.8), channel_id=1, source_target_pairs={{0,1},{1,0},{2,3},{3,2},{4,5},{5,4},{6,7},{7,6},{8,9},{9,8},{10,11... | collective-permute-start | bytes 20 | tf_op jit(solution)/shard_map/ppermute | solution.py:458
  40.2 3.9 %collective-permute-start.3 = (bf16[512,256]{1,0:T(8,128)(2,1)S(1)}, bf16[512,256]{1,0:T(8,128)(2,1)S(1)}, u32[]{:S(2)}, u32[]{:S(2)}) collective-permute-start(bf16[512,256]{1,0:T(8,128)(2,1)S(1)} %get-tuple-element.83.own_ref), channel_id=1, source_target_pairs={{0,2},{2,0},{1,3},{3,1},{4,6},{6,4},{5,7},{7,5},{8,10},{10,8},{9,1... | collective-permute-start | bytes 786440 | tf_op jit(solution)/shard_map/ppermute | solution.py:433
  46.0 2.0 %collective-permute-start.4 = (bf16[32,32,256]{2,1,0:T(8,128)(2,1)S(1)}, bf16[32,32,256]{2,1,0:T(8,128)(2,1)S(1)}, u32[]{:S(2)}, u32[]{:S(2)}) collective-permute-start(bf16[32,32,256]{2,1,0:T(8,128)(2,1)S(1)} %get-tuple-element.52), channel_id=1, source_target_pairs={{0,2},{2,0},{1,3},{3,1},{4,6},{6,4},{5,7},{7,5},{8,10},{10,8},{9,1... | collective-permute-start | bytes 1572872 | tf_op jit(solution)/shard_map/ppermute | solution.py:433
  50.3 35.0 %all-to-all-start.4 = ((bf16[128,16,256]{2,1,0:T(8,128)(2,1)}), bf16[128,16,256]{2,1,0:T(8,128)(2,1)S(1)}, u32[]{:S(2)}, u32[]{:S(2)}) async-start(bf16[128,16,256]{2,1,0:T(8,128)(2,1)} %bitcast.10), calls=%async_computation.4 | async-start | bytes 2097152 | tf_op jit(solution)/shard_map/all_to_all | solution.py:437
  88.0 4.0 %collective-permute-start.5 = (f32[64,2,8,128]{3,2,1,0:T(8,128)S(1)}, f32[64,2,8,128]{3,2,1,0:T(8,128)S(1)}, u32[]{:S(2)}, u32[]{:S(2)}) collective-permute-start(f32[64,2,8,128]{3,2,1,0:T(8,128)S(1)} %get-tuple-element.56), channel_id=1, source_target_pairs={{0,2},{2,0},{1,3},{3,1},{4,6},{6,4},{5,7},{7,5},{8,10},{10,8},{9,1... | collective-permute-start | bytes 1572872 | tf_op jit(solution)/shard_map/ppermute | solution.py:433
  92.8 25.1 %all-to-all-start.5 = ((f32[128,8,128]{2,1,0:T(8,128)}), f32[128,8,128]{2,1,0:T(8,128)S(1)}, u32[]{:S(2)}, u32[]{:S(2)}) async-start(f32[128,8,128]{2,1,0:T(8,128)} %bitcast.12), calls=%async_computation.5 | async-start | bytes 1048576 | tf_op jit(solution)/shard_map/all_to_all | solution.py:437
  118.1 3.6 %collective-permute-start.6 = (f32[4,128]{1,0:T(4,128)S(1)}, f32[4,128]{1,0:T(4,128)S(1)}, u32[]{:S(2)}, u32[]{:S(2)}) collective-permute-start(f32[4,128]{1,0:T(4,128)S(1)} %get-tuple-element.60), channel_id=1, source_target_pairs={{0,2},{2,0},{1,3},{3,1},{4,6},{6,4},{5,7},{7,5},{8,10},{10,8},{9,1... | collective-permute-start | bytes 6152 | tf_op jit(solution)/shard_map/ppermute | solution.py:433

commit v5 on v4

--- a/solution.py
+++ b/solution.py
@@ -20,7 +20,7 @@
 
 CHIPS = ("yl", "x", "z")
 LINES = ("yl", "x")
-SAME_CORE = ("yl", "x", "z", "b")
+SAME_CORE = ("b", "x", "z", "yl")
 F32 = jnp.float32
 BF16 = jnp.bfloat16
 
@@ -48,7 +48,8 @@
 def x_table(lone):
     row, column = iota((256, 256), 0), iota((256, 256), 1)
     z_of, e, k = row // 128, row // 64 % 2, row % 64
-    z_part, y_part, place = column // 128, column // 64 % 2, column % 64
+    z_part, y_part, chip = column // 128, column // 64 % 2, column % 64
+    place = chip % 2 * 32 + chip // 16 * 8 + chip // 2 % 8
     k_low = k % 32
     turned = (e == 1) & (k_low == 0)
     freq = jnp.where(lone, jnp.where(turned, N // 2, k_low), k)
@@ -378,7 +379,7 @@
     copy.start()
     mixed = jnp.concatenate([mixed_ref[...]] * 2, axis=1)
     for b in range(2):
-        rows = planes_ref[:, b].reshape(1024, NFIT)
+        rows = planes_ref[b].reshape(1024, NFIT)
         t0, t1, t2, t3 = [
             jnp.dot(table_ref[256 * t : 256 * t + 256, :], rows, preferred_element_type=F32)
             .astype(BF16)
@@ -406,11 +407,11 @@
                 left, weighted_ref[half], (((0,), (0,)), ((), ())), preferred_element_type=F32
             )
             for b in range(2):
-                out_ref[32 * q : 32 * q + 32, b] = got[:, 128 * b : 128 * b + 128].reshape(32, 8, 128)
+                out_ref[b, :, q] = got[:, 128 * b : 128 * b + 128].reshape(32, 8, 128)
 
 
 def gram(core, planes, table, screen, mixed):
-    half = jax.ShapeDtypeStruct((N, 2, 8, 128), F32)
+    half = jax.ShapeDtypeStruct((2, 32, 2, 8, 128), F32)
     return pl.pallas_call(
         gram_kernel,
         out_shape=(half, half),
@@ -442,7 +443,8 @@
     batch = lax.axis_index("b")
     chip = lax.axis_index(CHIPS)
     core_word = core.astype(jnp.int32)[None]
-    y_pair, z_group = chip // 2, core * 4 + chip % 2 * 2 + batch
+    turn = lax.axis_index(SAME_CORE)
+    y_pair, z_group = turn // 4, core * 4 + turn % 4
     base = (chip * 2 + core) * 2048
     place = jnp.stack([core, chip, base]).astype(jnp.int32)
     own, other, ranks, merge_table = pick(place, points, orbitals)
@@ -457,7 +459,7 @@
     slots = exchange(merge(merge_table, slots), LINES)
     full = full + lax.ppermute(full, "b", [(0, 1), (1, 0)])
     x_small = x_table(y_pair == 0)
-    slots, full, x_small, orbitals = lax.optimization_barrier((slots, full, x_small, orbitals))
+    slots, full, orbitals = lax.optimization_barrier((slots, full, orbitals))
     own = order(ranks, slots)
     own = lax.cond(
         full[0] > 0,
@@ -471,7 +473,7 @@
     screen, mixed = screen_rows(y_pair, z_group * 4)
     screen = pltpu.with_memory_space_constraint(screen, pltpu.HBM)
     planes = y_transform(core_word, near, sibling(far), y_big)
-    planes = exchange(planes.reshape(128, 16, NFIT), SAME_CORE).reshape(N, 2, 16, NFIT)
+    planes = exchange(planes.reshape(128, 16, NFIT), SAME_CORE).reshape(2, N, 16, NFIT)
     own, other = gram(core_word, planes, x_big, screen, mixed)
     sums = exchange((own + sibling(other)).reshape(128, 8, 128), SAME_CORE)
     sums = jnp.sum(sums, axis=0).reshape(2, 4, 128)

time: 123 us -> 124 us (level)
  waiting for transfers between devices: 51.1 us -> 54.4 us
  starting transfers between devices: 41.6 us -> 39.8 us
    all_to_all x4, waiting for transfers between devices: 46.1 us -> 49 us  [exchange(): return lax.all_to_all(blocks, axes, split_axis=0, concat_axis=0, tiled=True)]
    all_to_all x4, starting transfers between devices: 27.8 us -> 26.3 us  [exchange(): return lax.all_to_all(blocks, axes, split_axis=0, concat_axis=0, tiled=True)]
where the time goes in v5:
time: 124 us
  waiting for transfers between devices  54.4 us (44%)
  starting transfers between devices  39.8 us (32%)
  Pallas kernels  17.4 us (14%)
  other arithmetic  9.25 us (7%)
  between operations  2.15 us (2%)
    all_to_all x4, waiting for transfers between devices, exchange(): return lax.all_to_all(blocks, axes, split_axis=0, concat_axis=0, tiled=True)  49 us
    all_to_all x4, starting transfers between devices, exchange(): return lax.all_to_all(blocks, axes, split_axis=0, concat_axis=0, tiled=True)  26.3 us
    ppermute x5, starting transfers between devices, sibling(): return lax.ppermute(block, 'c', [(0, 1), (1, 0)])  10 us
    pallas_call x1, Pallas kernels, pick(): pl.pallas_call(pick_kernel, out_shape=(half, half, jax.ShapeDtypeStruct((...  4.34 us
    ppermute x5, waiting for transfers between devices, sibling(): return lax.ppermute(block, 'c', [(0, 1), (1, 0)])  4.2 us
    ppermute x1, starting transfers between devices, on_device(): full = full + lax.ppermute(full, 'b', [(0, 1), (1, 0)])  3.42 us
    mul x1, other arithmetic, screen_rows(): return (screen * copies, mixed)  2.93 us
    pallas_call x1, Pallas kernels, gram(): pl.pallas_call(gram_kernel, out_shape=(half, half), in_specs=[pl.BlockSpe...  2.75 us
  transfers between devices with their start and end apart: 10, of which 8 were waited for; matrix products, arithmetic and copies ran while one was open for 6% of the time, Pallas kernels for 4%

profile of v5, /device:TPU:1, one launch (start us, length us, event | category | flops | bytes accessed | tf_op | source)
XLA Modules:
  0.0 123.7 jit_solution(12279273732278720629)
XLA Ops:
  0.0 0.1 pad_add_fusion.place_ref
  0.1 4.3 %pick.1 = (bf16[16,512]{1,0:T(8,128)(2,1)S(1)}, bf16[16,512]{1,0:T(8,128)(2,1)S(1)}, s32[8,256]{1,0:T(8,128)S(1)}, bf16[64,128]{1,0:T(8,128)(2,1)S(1)}) custom-call(s32[3]{0:T(128)S(1)} %pad_add_fusion.place_ref, s32[1,256]{1,0:T(1,128)} %points_ref.1, bf16[1024,2048]{1,0:T(8,128)(2,1)} %orbitals_ref.2), custom_call_target="tpu_custom_call" | custom-call | tf_op jit(solution)/shard_map/pick/pallas_call | solution.py:213
  4.4 3.3 %collective-permute-start.1 = (bf16[16,512]{1,0:T(8,128)(2,1)S(1)}, bf16[16,512]{1,0:T(8,128)(2,1)S(1)}, u32[]{:S(2)}, u32[]{:S(2)}) collective-permute-start(bf16[16,512]{1,0:T(8,128)(2,1)S(1)} %get-tuple-element.40), channel_id=1, source_target_pairs={{0,2},{2,0},{1,3},{3,1},{4,6},{6,4},{5,7},{7,5},{8,10},{10,8},{9,1... | collective-permute-start | bytes 49160 | tf_op jit(solution)/shard_map/ppermute | solution.py:434
  7.7 0.7 slice_reduce_fusion
  9.7 0.0 collective-permute-done.1
  9.7 0.7 broadcast_in_dim.63
  10.4 6.5 %all-to-all-start.2 = ((bf16[8,16,512]{2,1,0:T(8,128)(2,1)}), bf16[8,16,512]{2,1,0:T(8,128)(2,1)S(1)}, u32[]{:S(2)}, u32[]{:S(2)}) async-start(bf16[8,16,512]{2,1,0:T(8,128)(2,1)} %broadcast_in_dim.63), calls=%async_computation.2 | async-start | bytes 262144 | tf_op jit(solution)/shard_map/all_to_all | solution.py:438
  16.9 0.3 select_convert_fusion.2.small_ref
  17.1 1.4 %expand_yz.1 = (bf16[256,256]{1,0:T(8,128)(2,1)S(1)}, bf16[1024,1024]{1,0:T(8,128)(2,1)S(1)}) custom-call(s32[1]{0:T(128)} %bitcast.5.core_ref, bf16[64,64]{1,0:T(8,128)(2,1)S(1)} %select_convert_fusion.2.small_ref), custom_call_target="tpu_custom_call" | custom-call | flops 1073741824 | bytes 2097152 | tf_op jit(solution)/shard_map/expand_yz/pallas_call | solution.py:121
  18.5 0.0 copy-start
  18.5 6.8 %all-to-all-done.2.slots_ref = bf16[8,16,512]{2,1,0:T(8,128)(2,1)S(1)} async-done(((bf16[8,16,512]{2,1,0:T(8,128)(2,1)}), bf16[8,16,512]{2,1,0:T(8,128)(2,1)S(1)}, u32[]{:S(2)}, u32[]{:S(2)}) %all-to-all-start.2) | async-done | bytes 131104 | tf_op jit(solution)/shard_map/all_to_all | solution.py:438
  25.3 1.0 merge.1
  26.3 5.0 %all-to-all-start.3 = ((bf16[8,64,512]{2,1,0:T(8,128)(2,1)}), bf16[8,64,512]{2,1,0:T(8,128)(2,1)S(1)}, u32[]{:S(2)}, u32[]{:S(2)}) async-start(bf16[8,64,512]{2,1,0:T(8,128)(2,1)} %merge.1), calls=%async_computation.3 | async-start | bytes 1048576 | tf_op jit(solution)/shard_map/all_to_all | solution.py:438
  31.3 3.4 %collective-permute-start.2 = (f32[1]{0:T(128)}, f32[1]{0:T(128)}, u32[]{:S(2)}, u32[]{:S(2)}) collective-permute-start(f32[1]{0:T(128)} %bitcast.8), channel_id=1, source_target_pairs={{0,1},{1,0},{2,3},{3,2},{4,5},{5,4},{6,7},{7,6},{8,9},{9,8},{10,11... | collective-permute-start | bytes 20 | tf_op jit(solution)/shard_map/ppermute | solution.py:460
  34.7 1.2 collective-permute-done.2
  36.5 4.4 %all-to-all-done.3.slots_ref = bf16[8,64,512]{2,1,0:T(8,128)(2,1)S(1)} async-done(((bf16[8,64,512]{2,1,0:T(8,128)(2,1)}), bf16[8,64,512]{2,1,0:T(8,128)(2,1)S(1)}, u32[]{:S(2)}, u32[]{:S(2)}) %all-to-all-start.3) | async-done | bytes 524320 | tf_op jit(solution)/shard_map/all_to_all | solution.py:438
  40.9 0.4 order.1
  41.3 0.0 copy-done
  41.3 1.5 %collective-permute-start.3 = (bf16[512,256]{1,0:T(8,128)(2,1)S(1)}, bf16[512,256]{1,0:T(8,128)(2,1)S(1)}, u32[]{:S(2)}, u32[]{:S(2)}) collective-permute-start(bf16[512,256]{1,0:T(8,128)(2,1)S(1)} %get-tuple-element.81.own_ref), channel_id=1, source_target_pairs={{0,2},{2,0},{1,3},{3,1},{4,6},{6,4},{5,7},{7,5},{8,10},{10,8},{9,1... | collective-permute-start | bytes 786440 | tf_op jit(solution)/shard_map/ppermute | solution.py:434
  42.8 2.2 %hold.1.orbitals_ref = bf16[1024,2048]{1,0:T(8,128)(2,1)S(1)} custom-call(bf16[1024,2048]{1,0:T(8,128)(2,1)} %orbitals_ref.2), custom_call_target="tpu_custom_call" | custom-call | bytes 8388608 | tf_op jit(solution)/shard_map/hold/pallas_call | solution.py:294
  45.1 0.0 collective-permute-done.3.other_ref
  45.1 1.8 %fit.1 = (bf16[32,32,256]{2,1,0:T(8,128)(2,1)S(1)}, bf16[32,32,256]{2,1,0:T(8,128)(2,1)S(1)}) custom-call(s32[1]{0:T(128)} %bitcast.5.core_ref, bf16[512,256]{1,0:T(8,128)(2,1)S(1)} %get-tuple-element.81.own_ref, bf16[512,256]{1,0:T(8,128)(2,1)S(1)} %collective-permute-done.3.other_ref, bf16[256,256]{1,0:T(8,128)(2,1)S(1)} %get-tuple-element.49.table_ref, ...), custom_call_target="tpu_custom_call" | custom-call | tf_op jit(solution)/shard_map/fit/pallas_call | solution.py:327
  46.9 0.3 collective-permute-start.4
  47.2 1.8 %collective-permute-done.4.far_ref = bf16[32,32,256]{2,1,0:T(8,128)(2,1)S(1)} collective-permute-done((bf16[32,32,256]{2,1,0:T(8,128)(2,1)S(1)}, bf16[32,32,256]{2,1,0:T(8,128)(2,1)S(1)}, u32[]{:S(2)}, u32[]{:S(2)}) %collective-permute-start.4) | collective-permute-done | bytes 524320 | tf_op jit(solution)/shard_map/ppermute | solution.py:434
  49.0 2.3 %y_transform.1 = bf16[32,2,2,16,256]{4,3,2,1,0:T(8,128)(2,1)} custom-call(s32[1]{0:T(128)} %bitcast.5.core_ref, bf16[32,32,256]{2,1,0:T(8,128)(2,1)S(1)} %get-tuple-element.50.near_ref, bf16[32,32,256]{2,1,0:T(8,128)(2,1)S(1)} %collective-permute-done.4.far_ref, bf16[1024,1024]{1,0:T(8,128)(2,1)S(1)} %get-tuple-element.52.table_ref), custom_call_target="tpu_custom_call" | custom-call | tf_op jit(solution)/shard_map/y_transform/pallas_call | solution.py:353
  51.3 7.5 %all-to-all-start.4 = ((bf16[128,16,256]{2,1,0:T(8,128)(2,1)}), bf16[128,16,256]{2,1,0:T(8,128)(2,1)S(1)}, u32[]{:S(2)}, u32[]{:S(2)}) async-start(bf16[128,16,256]{2,1,0:T(8,128)(2,1)} %bitcast.10), calls=%async_computation.4 | async-start | bytes 2097152 | tf_op jit(solution)/shard_map/all_to_all | solution.py:438
  58.9 1.7 %fusion.25.small_ref = bf16[256,256]{1,0:T(8,128)(2,1)S(1)} fusion(s32[256]{0:T(256)S(1)} %get-tuple-element.67, s32[256]{0:T(256)S(1)} %get-tuple-element.68, s32[256]{0:T(256)S(1)} %get-tuple-element.65, s32[256]{0:T(256)S(1)} %get-tuple-element.71, s32[256]{0:T(256)S(1)} %get-tuple-element.66, s32[256]{0:T(256)S(1)} %get-tuple-element.72, ...), kind=kLoop, calls=%fused_computation.90 | loop fusion | flops 8454144 | bytes 137985 | tf_op jit(solution)/shard_map/convert_element_type | solution.py:61
  60.6 1.3 %expand_x.1.table_ref = bf16[1024,1024]{1,0:T(8,128)(2,1)S(1)} custom-call(bf16[256,256]{1,0:T(8,128)(2,1)S(1)} %fusion.25.small_ref), custom_call_target="tpu_custom_call" | custom-call | flops 2147483648 | bytes 2097152 | tf_op jit(solution)/shard_map/expand_x/pallas_call | solution.py:153
  62.0 0.9 fusion.20
  62.9 1.0 compare_and_fusion
  63.9 2.9 %fusion.8.screens_ref = f32[1024,128]{1,0:T(8,128)} fusion(s32[1024]{0:T(1024)S(1)} %get-tuple-element.74, s32[1024]{0:T(1024)S(1)} %get-tuple-element.76, s32[]{:T(128)S(6)} %mul.98, s32[]{:T(128)S(6)} %select_n.297, s32[1024]{0:T(1024)S(1)} %get-tuple-element.75, s32[1024]{0:T(1024)S(1)} %get-tuple-element.79, s32[1024]{0:T(1024)S(1)} %get-tuple-element.73, ...), kind=kLoop, calls=%fused_computation.38 | loop fusion | flops 9175040 | bytes 551945 | tf_op jit(solution)/shard_map/mul | solution.py:83
  66.8 20.5 %all-to-all-done.4 = bf16[128,16,256]{2,1,0:T(8,128)(2,1)S(1)} async-done(((bf16[128,16,256]{2,1,0:T(8,128)(2,1)}), bf16[128,16,256]{2,1,0:T(8,128)(2,1)S(1)}, u32[]{:S(2)}, u32[]{:S(2)}) %all-to-all-start.4) | async-done | bytes 1048608 | tf_op jit(solution)/shard_map/all_to_all | solution.py:438
  87.3 2.8 %gram.1 = (f32[2,32,2,8,128]{4,3,2,1,0:T(8,128)S(1)}, f32[2,32,2,8,128]{4,3,2,1,0:T(8,128)S(1)}) custom-call(s32[1]{0:T(128)} %bitcast.5.core_ref, bf16[2,64,16,256]{3,2,1,0:T(8,128)(2,1)S(1)} %bitcast.24, bf16[1024,1024]{1,0:T(8,128)(2,1)S(1)} %expand_x.1.table_ref, f32[1024,128]{1,0:T(8,128)} %fusion.8.screens_ref, f32[256,128]{1,0:T(8,128)S(1)} %fusion.52.mixed_ref), custom_call_target="tpu_custom_call" | custom-call | tf_op jit(solution)/shard_map/gram/pallas_call | solution.py:415
  90.1 2.5 %collective-permute-start.5 = (f32[2,32,2,8,128]{4,3,2,1,0:T(8,128)S(1)}, f32[2,32,2,8,128]{4,3,2,1,0:T(8,128)S(1)}, u32[]{:S(2)}, u32[]{:S(2)}) collective-permute-start(f32[2,32,2,8,128]{4,3,2,1,0:T(8,128)S(1)} %get-tuple-element.54), channel_id=1, source_target_pairs={{0,2},{2,0},{1,3},{3,1},{4,6},{6,4},{5,7},{7,5},{8,10},{10,8},{9,1... | collective-permute-start | bytes 1572872 | tf_op jit(solution)/shard_map/ppermute | solution.py:434
  92.6 1.5 %collective-permute-done.5 = f32[2,32,2,8,128]{4,3,2,1,0:T(8,128)S(1)} collective-permute-done((f32[2,32,2,8,128]{4,3,2,1,0:T(8,128)S(1)}, f32[2,32,2,8,128]{4,3,2,1,0:T(8,128)S(1)}, u32[]{:S(2)}, u32[]{:S(2)}) %collective-permute-start.5) | collective-permute-done | bytes 524320 | tf_op jit(solution)/shard_map/ppermute | solution.py:434
  94.1 0.9 add.215
  95.0 7.4 %all-to-all-start.5 = ((f32[128,8,128]{2,1,0:T(8,128)}), f32[128,8,128]{2,1,0:T(8,128)S(1)}, u32[]{:S(2)}, u32[]{:S(2)}) async-start(f32[128,8,128]{2,1,0:T(8,128)} %bitcast.12), calls=%async_computation.5 | async-start | bytes 1048576 | tf_op jit(solution)/shard_map/all_to_all | solution.py:438
  102.4 17.3 %all-to-all-done.5 = f32[128,8,128]{2,1,0:T(8,128)S(1)} async-done(((f32[128,8,128]{2,1,0:T(8,128)}), f32[128,8,128]{2,1,0:T(8,128)S(1)}, u32[]{:S(2)}, u32[]{:S(2)}) %all-to-all-start.5) | async-done | bytes 524320 | tf_op jit(solution)/shard_map/all_to_all | solution.py:438
  119.7 0.1 reduce_sum.21
  119.8 2.4 %collective-permute-start.6 = (f32[4,128]{1,0:T(4,128)S(1)}, f32[4,128]{1,0:T(4,128)S(1)}, u32[]{:S(2)}, u32[]{:S(2)}) collective-permute-start(f32[4,128]{1,0:T(4,128)S(1)} %get-tuple-element.58), channel_id=1, source_target_pairs={{0,2},{2,0},{1,3},{3,1},{4,6},{6,4},{5,7},{7,5},{8,10},{10,8},{9,1... | collective-permute-start | bytes 6152 | tf_op jit(solution)/shard_map/ppermute | solution.py:434
  122.3 0.8 collective-permute-done.6
  123.1 0.6 fusion.67
  (17 shorter events, 0.1 us)
Async XLA Ops:
  4.4 5.3 %collective-permute-start.1 = (bf16[16,512]{1,0:T(8,128)(2,1)S(1)}, bf16[16,512]{1,0:T(8,128)(2,1)S(1)}, u32[]{:S(2)}, u32[]{:S(2)}) collective-permute-start(bf16[16,512]{1,0:T(8,128)(2,1)S(1)} %get-tuple-element.40), channel_id=1, source_target_pairs={{0,2},{2,0},{1,3},{3,1},{4,6},{6,4},{5,7},{7,5},{8,10},{10,8},{9,1... | collective-permute-start | bytes 49160 | tf_op jit(solution)/shard_map/ppermute | solution.py:434
  10.4 14.9 %all-to-all-start.2 = ((bf16[8,16,512]{2,1,0:T(8,128)(2,1)}), bf16[8,16,512]{2,1,0:T(8,128)(2,1)S(1)}, u32[]{:S(2)}, u32[]{:S(2)}) async-start(bf16[8,16,512]{2,1,0:T(8,128)(2,1)} %broadcast_in_dim.63), calls=%async_computation.2 | async-start | bytes 262144 | tf_op jit(solution)/shard_map/all_to_all | solution.py:438
  18.5 22.8 %copy-start = (s32[1,256]{1,0:T(1,128)S(1)}, s32[1,256]{1,0:T(1,128)}, u32[]{:S(2)}) copy-start(s32[1,256]{1,0:T(1,128)} %points_ref.1) | copy-start | bytes 3076
  26.3 14.6 %all-to-all-start.3 = ((bf16[8,64,512]{2,1,0:T(8,128)(2,1)}), bf16[8,64,512]{2,1,0:T(8,128)(2,1)S(1)}, u32[]{:S(2)}, u32[]{:S(2)}) async-start(bf16[8,64,512]{2,1,0:T(8,128)(2,1)} %merge.1), calls=%async_computation.3 | async-start | bytes 1048576 | tf_op jit(solution)/shard_map/all_to_all | solution.py:438
  31.3 4.6 %collective-permute-start.2 = (f32[1]{0:T(128)}, f32[1]{0:T(128)}, u32[]{:S(2)}, u32[]{:S(2)}) collective-permute-start(f32[1]{0:T(128)} %bitcast.8), channel_id=1, source_target_pairs={{0,1},{1,0},{2,3},{3,2},{4,5},{5,4},{6,7},{7,6},{8,9},{9,8},{10,11... | collective-permute-start | bytes 20 | tf_op jit(solution)/shard_map/ppermute | solution.py:460
  41.3 3.8 %collective-permute-start.3 = (bf16[512,256]{1,0:T(8,128)(2,1)S(1)}, bf16[512,256]{1,0:T(8,128)(2,1)S(1)}, u32[]{:S(2)}, u32[]{:S(2)}) collective-permute-start(bf16[512,256]{1,0:T(8,128)(2,1)S(1)} %get-tuple-element.81.own_ref), channel_id=1, source_target_pairs={{0,2},{2,0},{1,3},{3,1},{4,6},{6,4},{5,7},{7,5},{8,10},{10,8},{9,1... | collective-permute-start | bytes 786440 | tf_op jit(solution)/shard_map/ppermute | solution.py:434
  46.9 2.2 %collective-permute-start.4 = (bf16[32,32,256]{2,1,0:T(8,128)(2,1)S(1)}, bf16[32,32,256]{2,1,0:T(8,128)(2,1)S(1)}, u32[]{:S(2)}, u32[]{:S(2)}) collective-permute-start(bf16[32,32,256]{2,1,0:T(8,128)(2,1)S(1)} %get-tuple-element.51), channel_id=1, source_target_pairs={{0,2},{2,0},{1,3},{3,1},{4,6},{6,4},{5,7},{7,5},{8,10},{10,8},{9,1... | collective-permute-start | bytes 1572872 | tf_op jit(solution)/shard_map/ppermute | solution.py:434
  51.3 36.0 %all-to-all-start.4 = ((bf16[128,16,256]{2,1,0:T(8,128)(2,1)}), bf16[128,16,256]{2,1,0:T(8,128)(2,1)S(1)}, u32[]{:S(2)}, u32[]{:S(2)}) async-start(bf16[128,16,256]{2,1,0:T(8,128)(2,1)} %bitcast.10), calls=%async_computation.4 | async-start | bytes 2097152 | tf_op jit(solution)/shard_map/all_to_all | solution.py:438
  90.1 4.0 %collective-permute-start.5 = (f32[2,32,2,8,128]{4,3,2,1,0:T(8,128)S(1)}, f32[2,32,2,8,128]{4,3,2,1,0:T(8,128)S(1)}, u32[]{:S(2)}, u32[]{:S(2)}) collective-permute-start(f32[2,32,2,8,128]{4,3,2,1,0:T(8,128)S(1)} %get-tuple-element.54), channel_id=1, source_target_pairs={{0,2},{2,0},{1,3},{3,1},{4,6},{6,4},{5,7},{7,5},{8,10},{10,8},{9,1... | collective-permute-start | bytes 1572872 | tf_op jit(solution)/shard_map/ppermute | solution.py:434
  95.0 24.7 %all-to-all-start.5 = ((f32[128,8,128]{2,1,0:T(8,128)}), f32[128,8,128]{2,1,0:T(8,128)S(1)}, u32[]{:S(2)}, u32[]{:S(2)}) async-start(f32[128,8,128]{2,1,0:T(8,128)} %bitcast.12), calls=%async_computation.5 | async-start | bytes 1048576 | tf_op jit(solution)/shard_map/all_to_all | solution.py:438
  119.8 3.2 %collective-permute-start.6 = (f32[4,128]{1,0:T(4,128)S(1)}, f32[4,128]{1,0:T(4,128)S(1)}, u32[]{:S(2)}, u32[]{:S(2)}) collective-permute-start(f32[4,128]{1,0:T(4,128)S(1)} %get-tuple-element.58), channel_id=1, source_target_pairs={{0,2},{2,0},{1,3},{3,1},{4,6},{6,4},{5,7},{7,5},{8,10},{10,8},{9,1... | collective-permute-start | bytes 6152 | tf_op jit(solution)/shard_map/ppermute | solution.py:434

commit v6 on v4

--- a/solution.py
+++ b/solution.py
@@ -334,31 +334,44 @@
     )(core, own, other, table, held)
 
 
-def y_kernel(core_ref, near_ref, far_ref, table_ref, out_ref, rows_ref):
-    core = core_ref[0]
-    mine = pl.multiple_of(core * 512, 512)
-    theirs = pl.multiple_of((1 - core) * 512, 512)
+def y_near_kernel(core_ref, near_ref, table_ref, part_ref):
+    at = pl.ds(pl.multiple_of(core_ref[0] * 512, 512), 512)
     for g in range(2):
-        rows_ref[pl.ds(mine, 512), :] = near_ref[:, 16 * g : 16 * g + 16, :].reshape(512, NFIT)
-        rows_ref[pl.ds(theirs, 512), :] = far_ref[:, 16 * g : 16 * g + 16, :].reshape(512, NFIT)
-        for m in range(4):
-            got = jnp.dot(
-                table_ref[256 * m : 256 * m + 256, :], rows_ref[...], preferred_element_type=F32
-            ).astype(BF16)
-            out_ref[8 * m : 8 * m + 8, g] = got.reshape(8, 2, 16, NFIT)
-
-
-def y_transform(core, near, far, table):
-    return pl.pallas_call(
-        y_kernel,
+        rows = near_ref[:, 16 * g : 16 * g + 16, :].reshape(512, NFIT)
+        part_ref[g] = jnp.dot(table_ref[:, at], rows, preferred_element_type=F32)
+
+
+def y_near(core, near, table):
+    vmem = pl.BlockSpec(memory_space=pltpu.VMEM)
+    return pl.pallas_call(
+        y_near_kernel,
+        out_shape=jax.ShapeDtypeStruct((2, 1024, NFIT), F32),
+        in_specs=[pl.BlockSpec(memory_space=pltpu.SMEM)] + [vmem] * 2,
+        out_specs=vmem,
+        compiler_params=pltpu.CompilerParams(vmem_limit_bytes=12 << 20),
+        cost_estimate=pl.CostEstimate(flops=2**29, bytes_accessed=2**22, transcendentals=0),
+        name="y_near",
+    )(core, near, table)
+
+
+def y_far_kernel(core_ref, far_ref, table_ref, part_ref, out_ref):
+    at = pl.ds(pl.multiple_of((1 - core_ref[0]) * 512, 512), 512)
+    for g in range(2):
+        rows = far_ref[:, 16 * g : 16 * g + 16, :].reshape(512, NFIT)
+        got = part_ref[g] + jnp.dot(table_ref[:, at], rows, preferred_element_type=F32)
+        out_ref[:, g] = got.astype(BF16).reshape(32, 2, 16, NFIT)
+
+
+def y_far(core, far, table, part):
+    vmem = pl.BlockSpec(memory_space=pltpu.VMEM)
+    return pl.pallas_call(
+        y_far_kernel,
         out_shape=jax.ShapeDtypeStruct((32, 2, 2, 16, NFIT), BF16),
-        in_specs=[pl.BlockSpec(memory_space=pltpu.SMEM)]
-        + [pl.BlockSpec(memory_space=pltpu.VMEM)] * 3,
-        out_specs=pl.BlockSpec(memory_space=pltpu.VMEM),
-        scratch_shapes=[pltpu.VMEM((1024, NFIT), BF16)],
+        in_specs=[pl.BlockSpec(memory_space=pltpu.SMEM)] + [vmem] * 3,
+        out_specs=vmem,
         compiler_params=pltpu.CompilerParams(vmem_limit_bytes=14 << 20),
-        name="y_transform",
-    )(core, near, far, table)
+        name="y_far",
+    )(core, far, table, part)
 
 
 def gram_kernel(
@@ -453,11 +466,10 @@
     z_table, y_big = expand_yz(core_word, small)
     full = (jnp.max(ranks[0]) >= CHIP_SLOTS) | (jnp.max(ranks[1]) >= LINE_SLOTS)
     full = jnp.where(full, F32(1.0), F32(0.0))[None]
-    slots, z_table, y_big, full = lax.optimization_barrier((slots, z_table, y_big, full))
+    full = full + lax.ppermute(full, "b", [(0, 1), (1, 0)])
+    slots, full = lax.optimization_barrier((slots, full))
     slots = exchange(merge(merge_table, slots), LINES)
-    full = full + lax.ppermute(full, "b", [(0, 1), (1, 0)])
-    x_small = x_table(y_pair == 0)
-    slots, full, x_small, orbitals = lax.optimization_barrier((slots, full, x_small, orbitals))
+    slots, z_table, y_big, orbitals = lax.optimization_barrier((slots, z_table, y_big, orbitals))
     own = order(ranks, slots)
     own = lax.cond(
         full[0] > 0,
@@ -467,10 +479,10 @@
     )
     held = hold(orbitals)
     near, far = fit(core_word, own, sibling(own), z_table, held)
-    x_big = expand_x(x_small)
+    x_big = expand_x(x_table(y_pair == 0))
     screen, mixed = screen_rows(y_pair, z_group * 4)
     screen = pltpu.with_memory_space_constraint(screen, pltpu.HBM)
-    planes = y_transform(core_word, near, sibling(far), y_big)
+    planes = y_far(core_word, sibling(far), y_big, y_near(core_word, near, y_big))
     planes = exchange(planes.reshape(128, 16, NFIT), SAME_CORE).reshape(N, 2, 16, NFIT)
     own, other = gram(core_word, planes, x_big, screen, mixed)
     sums = exchange((own + sibling(other)).reshape(128, 8, 128), SAME_CORE)

time: 123 us -> 124 us (level)
  starting transfers between devices: 41.6 us -> 46.2 us
  waiting for transfers between devices: 51.1 us -> 48 us
    all_to_all x4, starting transfers between devices: 27.8 us -> 30.5 us  [exchange(): return lax.all_to_all(blocks, axes, split_axis=0, concat_axis=0, tiled=True)]
    all_to_all x4, waiting for transfers between devices: 46.1 us -> 43.4 us  [exchange(): return lax.all_to_all(blocks, axes, split_axis=0, concat_axis=0, tiled=True)]
    ppermute x5, starting transfers between devices: 10.4 us -> 11.9 us  [sibling(): return lax.ppermute(block, 'c', [(0, 1), (1, 0)])]
  transfers between devices with their start and end apart: 10 -> 10, of which waited for: 8 -> 9; matrix products, arithmetic and copies ran while one was open for 6% -> 6% of each run, Pallas kernels for 4% -> 5%
where the time goes in v6:
time: 124 us
  waiting for transfers between devices  48 us (39%)
  starting transfers between devices  46.2 us (37%)
  Pallas kernels  17.6 us (14%)
  other arithmetic  9.26 us (7%)
  between operations  2.11 us (2%)
    all_to_all x4, waiting for transfers between devices, exchange(): return lax.all_to_all(blocks, axes, split_axis=0, concat_axis=0, tiled=True)  43.4 us
    all_to_all x4, starting transfers between devices, exchange(): return lax.all_to_all(blocks, axes, split_axis=0, concat_axis=0, tiled=True)  30.5 us
    ppermute x5, starting transfers between devices, sibling(): return lax.ppermute(block, 'c', [(0, 1), (1, 0)])  11.9 us
    pallas_call x1, Pallas kernels, pick(): pl.pallas_call(pick_kernel, out_shape=(half, half, jax.ShapeDtypeStruct((...  4.34 us
    ppermute x5, waiting for transfers between devices, sibling(): return lax.ppermute(block, 'c', [(0, 1), (1, 0)])  4.33 us
    ppermute x1, starting transfers between devices, on_device(): full = full + lax.ppermute(full, 'b', [(0, 1), (1, 0)])  3.72 us
    mul x1, other arithmetic, screen_rows(): return (screen * copies, mixed)  2.93 us
    pallas_call x1, Pallas kernels, gram(): pl.pallas_call(gram_kernel, out_shape=(half, half), in_specs=[pl.BlockSpe...  2.76 us
  transfers between devices with their start and end apart: 10, of which 9 were waited for; matrix products, arithmetic and copies ran while one was open for 6% of the time, Pallas kernels for 5%

profile of v6, /device:TPU:1, one launch (start us, length us, event | category | flops | bytes accessed | tf_op | source)
XLA Modules:
  0.0 123.8 jit_solution(16934828998610961352)
XLA Ops:
  0.0 0.1 pad_add_fusion.place_ref
  0.1 4.3 %pick.1 = (bf16[16,512]{1,0:T(8,128)(2,1)S(1)}, bf16[16,512]{1,0:T(8,128)(2,1)S(1)}, s32[8,256]{1,0:T(8,128)S(1)}, bf16[64,128]{1,0:T(8,128)(2,1)S(1)}) custom-call(s32[3]{0:T(128)S(1)} %pad_add_fusion.place_ref, s32[1,256]{1,0:T(1,128)} %points_ref.1, bf16[1024,2048]{1,0:T(8,128)(2,1)} %orbitals_ref.2), custom_call_target="tpu_custom_call" | custom-call | tf_op jit(solution)/shard_map/pick/pallas_call | solution.py:212
  4.4 3.3 %collective-permute-start.1 = (bf16[16,512]{1,0:T(8,128)(2,1)S(1)}, bf16[16,512]{1,0:T(8,128)(2,1)S(1)}, u32[]{:S(2)}, u32[]{:S(2)}) collective-permute-start(bf16[16,512]{1,0:T(8,128)(2,1)S(1)} %get-tuple-element.38), channel_id=1, source_target_pairs={{0,2},{2,0},{1,3},{3,1},{4,6},{6,4},{5,7},{7,5},{8,10},{10,8},{9,1... | collective-permute-start | bytes 49160 | tf_op jit(solution)/shard_map/ppermute | solution.py:446
  7.7 0.8 collective-permute-done.1
  8.6 0.7 broadcast_in_dim.63
  9.2 6.5 %all-to-all-start.2 = ((bf16[8,16,512]{2,1,0:T(8,128)(2,1)}), bf16[8,16,512]{2,1,0:T(8,128)(2,1)S(1)}, u32[]{:S(2)}, u32[]{:S(2)}) async-start(bf16[8,16,512]{2,1,0:T(8,128)(2,1)} %broadcast_in_dim.63), calls=%async_computation.2 | async-start | bytes 262144 | tf_op jit(solution)/shard_map/all_to_all | solution.py:450
  15.7 0.7 slice_reduce_fusion
  17.7 3.7 %collective-permute-start.2 = (f32[1]{0:T(128)}, f32[1]{0:T(128)}, u32[]{:S(2)}, u32[]{:S(2)}) collective-permute-start(f32[1]{0:T(128)} %bitcast.8), channel_id=1, source_target_pairs={{0,1},{1,0},{2,3},{3,2},{4,5},{5,4},{6,7},{7,6},{8,9},{9,8},{10,11... | collective-permute-start | bytes 20 | tf_op jit(solution)/shard_map/ppermute | solution.py:469
  21.4 0.2 collective-permute-done.2
  22.2 1.4 %all-to-all-done.2.slots_ref = bf16[8,16,512]{2,1,0:T(8,128)(2,1)S(1)} async-done(((bf16[8,16,512]{2,1,0:T(8,128)(2,1)}), bf16[8,16,512]{2,1,0:T(8,128)(2,1)S(1)}, u32[]{:S(2)}, u32[]{:S(2)}) %all-to-all-start.2) | async-done | bytes 131104 | tf_op jit(solution)/shard_map/all_to_all | solution.py:450
  23.6 1.0 merge.1
  24.6 5.0 %all-to-all-start.3 = ((bf16[8,64,512]{2,1,0:T(8,128)(2,1)}), bf16[8,64,512]{2,1,0:T(8,128)(2,1)S(1)}, u32[]{:S(2)}, u32[]{:S(2)}) async-start(bf16[8,64,512]{2,1,0:T(8,128)(2,1)} %merge.1), calls=%async_computation.3 | async-start | bytes 1048576 | tf_op jit(solution)/shard_map/all_to_all | solution.py:450
  29.7 0.3 select_convert_fusion.2.small_ref
  29.9 0.0 copy-start
  29.9 1.4 %expand_yz.1 = (bf16[256,256]{1,0:T(8,128)(2,1)S(1)}, bf16[1024,1024]{1,0:T(8,128)(2,1)S(1)}) custom-call(s32[1]{0:T(128)} %bitcast.5.core_ref, bf16[64,64]{1,0:T(8,128)(2,1)S(1)} %select_convert_fusion.2.small_ref), custom_call_target="tpu_custom_call" | custom-call | flops 1073741824 | bytes 2097152 | tf_op jit(solution)/shard_map/expand_yz/pallas_call | solution.py:120
  31.3 6.3 %all-to-all-done.3.slots_ref = bf16[8,64,512]{2,1,0:T(8,128)(2,1)S(1)} async-done(((bf16[8,64,512]{2,1,0:T(8,128)(2,1)}), bf16[8,64,512]{2,1,0:T(8,128)(2,1)S(1)}, u32[]{:S(2)}, u32[]{:S(2)}) %all-to-all-start.3) | async-done | bytes 524320 | tf_op jit(solution)/shard_map/all_to_all | solution.py:450
  37.7 0.4 order.1
  38.1 0.0 copy-done
  38.1 3.1 %collective-permute-start.3 = (bf16[512,256]{1,0:T(8,128)(2,1)S(1)}, bf16[512,256]{1,0:T(8,128)(2,1)S(1)}, u32[]{:S(2)}, u32[]{:S(2)}) collective-permute-start(bf16[512,256]{1,0:T(8,128)(2,1)S(1)} %get-tuple-element.79.own_ref), channel_id=1, source_target_pairs={{0,2},{2,0},{1,3},{3,1},{4,6},{6,4},{5,7},{7,5},{8,10},{10,8},{9,1... | collective-permute-start | bytes 786440 | tf_op jit(solution)/shard_map/ppermute | solution.py:446
  41.2 2.2 %hold.1.orbitals_ref = bf16[1024,2048]{1,0:T(8,128)(2,1)S(1)} custom-call(bf16[1024,2048]{1,0:T(8,128)(2,1)} %orbitals_ref.2), custom_call_target="tpu_custom_call" | custom-call | bytes 8388608 | tf_op jit(solution)/shard_map/hold/pallas_call | solution.py:293
  43.4 0.0 collective-permute-done.3.other_ref
  43.4 1.8 %fit.1 = (bf16[32,32,256]{2,1,0:T(8,128)(2,1)S(1)}, bf16[32,32,256]{2,1,0:T(8,128)(2,1)S(1)}) custom-call(s32[1]{0:T(128)} %bitcast.5.core_ref, bf16[512,256]{1,0:T(8,128)(2,1)S(1)} %get-tuple-element.79.own_ref, bf16[512,256]{1,0:T(8,128)(2,1)S(1)} %collective-permute-done.3.other_ref, bf16[256,256]{1,0:T(8,128)(2,1)S(1)} %get-tuple-element.47.table_ref, ...), custom_call_target="tpu_custom_call" | custom-call | tf_op jit(solution)/shard_map/fit/pallas_call | solution.py:326
  45.2 0.3 collective-permute-start.4
  45.5 0.7 y_near.1.part_ref
  46.2 1.1 collective-permute-done.4.far_ref
  47.4 1.7 %y_far.1 = bf16[32,2,2,16,256]{4,3,2,1,0:T(8,128)(2,1)} custom-call(s32[1]{0:T(128)} %bitcast.5.core_ref, bf16[32,32,256]{2,1,0:T(8,128)(2,1)S(1)} %collective-permute-done.4.far_ref, bf16[1024,1024]{1,0:T(8,128)(2,1)S(1)} %get-tuple-element.49.table_ref, f32[2,1024,256]{2,1,0:T(8,128)S(1)} %y_near.1.part_ref), custom_call_target="tpu_custom_call" | custom-call | tf_op jit(solution)/shard_map/y_far/pallas_call | solution.py:367
  49.1 10.3 %all-to-all-start.4 = ((bf16[128,16,256]{2,1,0:T(8,128)(2,1)}), bf16[128,16,256]{2,1,0:T(8,128)(2,1)S(1)}, u32[]{:S(2)}, u32[]{:S(2)}) async-start(bf16[128,16,256]{2,1,0:T(8,128)(2,1)} %bitcast.10), calls=%async_computation.4 | async-start | bytes 2097152 | tf_op jit(solution)/shard_map/all_to_all | solution.py:450
  59.5 1.7 %fusion.25.small_ref = bf16[256,256]{1,0:T(8,128)(2,1)S(1)} fusion(s32[256]{0:T(256)S(1)} %get-tuple-element.65, s32[256]{0:T(256)S(1)} %get-tuple-element.66, s32[256]{0:T(256)S(1)} %get-tuple-element.63, s32[256]{0:T(256)S(1)} %get-tuple-element.69, s32[256]{0:T(256)S(1)} %get-tuple-element.64, s32[256]{0:T(256)S(1)} %get-tuple-element.70, ...), kind=kLoop, calls=%fused_computation.76 | loop fusion | flops 5570560 | bytes 137985 | tf_op jit(solution)/shard_map/convert_element_type | solution.py:60
  61.2 1.3 %expand_x.1.table_ref = bf16[1024,1024]{1,0:T(8,128)(2,1)S(1)} custom-call(bf16[256,256]{1,0:T(8,128)(2,1)S(1)} %fusion.25.small_ref), custom_call_target="tpu_custom_call" | custom-call | flops 2147483648 | bytes 2097152 | tf_op jit(solution)/shard_map/expand_x/pallas_call | solution.py:152
  62.6 0.9 fusion.20
  63.4 1.0 compare_and_fusion
  64.4 2.9 %fusion.8.screens_ref = f32[1024,128]{1,0:T(8,128)} fusion(s32[1024]{0:T(1024)S(1)} %get-tuple-element.72, s32[1024]{0:T(1024)S(1)} %get-tuple-element.74, s32[]{:T(128)S(6)} %mul.77, s32[]{:T(128)S(6)} %select_n.283, s32[1024]{0:T(1024)S(1)} %get-tuple-element.73, s32[1024]{0:T(1024)S(1)} %get-tuple-element.77, s32[1024]{0:T(1024)S(1)} %get-tuple-element.71, ...), kind=kLoop, calls=%fused_computation.34 | loop fusion | flops 9175040 | bytes 551945 | tf_op jit(solution)/shard_map/mul | solution.py:82
  67.4 19.3 %all-to-all-done.4 = bf16[128,16,256]{2,1,0:T(8,128)(2,1)S(1)} async-done(((bf16[128,16,256]{2,1,0:T(8,128)(2,1)}), bf16[128,16,256]{2,1,0:T(8,128)(2,1)S(1)}, u32[]{:S(2)}, u32[]{:S(2)}) %all-to-all-start.4) | async-done | bytes 1048608 | tf_op jit(solution)/shard_map/all_to_all | solution.py:450
  86.7 2.8 %gram.1 = (f32[64,2,8,128]{3,2,1,0:T(8,128)S(1)}, f32[64,2,8,128]{3,2,1,0:T(8,128)S(1)}) custom-call(s32[1]{0:T(128)} %bitcast.5.core_ref, bf16[64,2,16,256]{3,2,1,0:T(8,128)(2,1)S(1)} %bitcast.24, bf16[1024,1024]{1,0:T(8,128)(2,1)S(1)} %expand_x.1.table_ref, f32[1024,128]{1,0:T(8,128)} %fusion.8.screens_ref, f32[256,128]{1,0:T(8,128)S(1)} %fusion.40.mixed_ref), custom_call_target="tpu_custom_call" | custom-call | tf_op jit(solution)/shard_map/gram/pallas_call | solution.py:427
  89.5 2.5 %collective-permute-start.5 = (f32[64,2,8,128]{3,2,1,0:T(8,128)S(1)}, f32[64,2,8,128]{3,2,1,0:T(8,128)S(1)}, u32[]{:S(2)}, u32[]{:S(2)}) collective-permute-start(f32[64,2,8,128]{3,2,1,0:T(8,128)S(1)} %get-tuple-element.52), channel_id=1, source_target_pairs={{0,2},{2,0},{1,3},{3,1},{4,6},{6,4},{5,7},{7,5},{8,10},{10,8},{9,1... | collective-permute-start | bytes 1572872 | tf_op jit(solution)/shard_map/ppermute | solution.py:446
  91.9 1.5 %collective-permute-done.5 = f32[64,2,8,128]{3,2,1,0:T(8,128)S(1)} collective-permute-done((f32[64,2,8,128]{3,2,1,0:T(8,128)S(1)}, f32[64,2,8,128]{3,2,1,0:T(8,128)S(1)}, u32[]{:S(2)}, u32[]{:S(2)}) %collective-permute-start.5) | collective-permute-done | bytes 524320 | tf_op jit(solution)/shard_map/ppermute | solution.py:446
  93.5 0.9 add.187
  94.3 8.8 %all-to-all-start.5 = ((f32[128,8,128]{2,1,0:T(8,128)}), f32[128,8,128]{2,1,0:T(8,128)S(1)}, u32[]{:S(2)}, u32[]{:S(2)}) async-start(f32[128,8,128]{2,1,0:T(8,128)} %bitcast.12), calls=%async_computation.5 | async-start | bytes 1048576 | tf_op jit(solution)/shard_map/all_to_all | solution.py:450
  103.1 16.3 %all-to-all-done.5 = f32[128,8,128]{2,1,0:T(8,128)S(1)} async-done(((f32[128,8,128]{2,1,0:T(8,128)}), f32[128,8,128]{2,1,0:T(8,128)S(1)}, u32[]{:S(2)}, u32[]{:S(2)}) %all-to-all-start.5) | async-done | bytes 524320 | tf_op jit(solution)/shard_map/all_to_all | solution.py:450
  119.4 0.1 reduce_sum.21
  119.6 2.8 %collective-permute-start.6 = (f32[4,128]{1,0:T(4,128)S(1)}, f32[4,128]{1,0:T(4,128)S(1)}, u32[]{:S(2)}, u32[]{:S(2)}) collective-permute-start(f32[4,128]{1,0:T(4,128)S(1)} %get-tuple-element.56), channel_id=1, source_target_pairs={{0,2},{2,0},{1,3},{3,1},{4,6},{6,4},{5,7},{7,5},{8,10},{10,8},{9,1... | collective-permute-start | bytes 6152 | tf_op jit(solution)/shard_map/ppermute | solution.py:446
  122.4 0.8 collective-permute-done.6
  123.2 0.6 fusion.55
  (17 shorter events, 0.1 us)
Async XLA Ops:
  4.4 4.1 %collective-permute-start.1 = (bf16[16,512]{1,0:T(8,128)(2,1)S(1)}, bf16[16,512]{1,0:T(8,128)(2,1)S(1)}, u32[]{:S(2)}, u32[]{:S(2)}) collective-permute-start(bf16[16,512]{1,0:T(8,128)(2,1)S(1)} %get-tuple-element.38), channel_id=1, source_target_pairs={{0,2},{2,0},{1,3},{3,1},{4,6},{6,4},{5,7},{7,5},{8,10},{10,8},{9,1... | collective-permute-start | bytes 49160 | tf_op jit(solution)/shard_map/ppermute | solution.py:446
  9.2 14.4 %all-to-all-start.2 = ((bf16[8,16,512]{2,1,0:T(8,128)(2,1)}), bf16[8,16,512]{2,1,0:T(8,128)(2,1)S(1)}, u32[]{:S(2)}, u32[]{:S(2)}) async-start(bf16[8,16,512]{2,1,0:T(8,128)(2,1)} %broadcast_in_dim.63), calls=%async_computation.2 | async-start | bytes 262144 | tf_op jit(solution)/shard_map/all_to_all | solution.py:450
  17.7 4.0 %collective-permute-start.2 = (f32[1]{0:T(128)}, f32[1]{0:T(128)}, u32[]{:S(2)}, u32[]{:S(2)}) collective-permute-start(f32[1]{0:T(128)} %bitcast.8), channel_id=1, source_target_pairs={{0,1},{1,0},{2,3},{3,2},{4,5},{5,4},{6,7},{7,6},{8,9},{9,8},{10,11... | collective-permute-start | bytes 20 | tf_op jit(solution)/shard_map/ppermute | solution.py:469
  24.6 13.1 %all-to-all-start.3 = ((bf16[8,64,512]{2,1,0:T(8,128)(2,1)}), bf16[8,64,512]{2,1,0:T(8,128)(2,1)S(1)}, u32[]{:S(2)}, u32[]{:S(2)}) async-start(bf16[8,64,512]{2,1,0:T(8,128)(2,1)} %merge.1), calls=%async_computation.3 | async-start | bytes 1048576 | tf_op jit(solution)/shard_map/all_to_all | solution.py:450
  29.9 8.1 %copy-start = (s32[1,256]{1,0:T(1,128)S(1)}, s32[1,256]{1,0:T(1,128)}, u32[]{:S(2)}) copy-start(s32[1,256]{1,0:T(1,128)} %points_ref.1) | copy-start | bytes 3076
  38.1 5.3 %collective-permute-start.3 = (bf16[512,256]{1,0:T(8,128)(2,1)S(1)}, bf16[512,256]{1,0:T(8,128)(2,1)S(1)}, u32[]{:S(2)}, u32[]{:S(2)}) collective-permute-start(bf16[512,256]{1,0:T(8,128)(2,1)S(1)} %get-tuple-element.79.own_ref), channel_id=1, source_target_pairs={{0,2},{2,0},{1,3},{3,1},{4,6},{6,4},{5,7},{7,5},{8,10},{10,8},{9,1... | collective-permute-start | bytes 786440 | tf_op jit(solution)/shard_map/ppermute | solution.py:446
  45.2 2.2 %collective-permute-start.4 = (bf16[32,32,256]{2,1,0:T(8,128)(2,1)S(1)}, bf16[32,32,256]{2,1,0:T(8,128)(2,1)S(1)}, u32[]{:S(2)}, u32[]{:S(2)}) collective-permute-start(bf16[32,32,256]{2,1,0:T(8,128)(2,1)S(1)} %get-tuple-element.48), channel_id=1, source_target_pairs={{0,2},{2,0},{1,3},{3,1},{4,6},{6,4},{5,7},{7,5},{8,10},{10,8},{9,1... | collective-permute-start | bytes 1572872 | tf_op jit(solution)/shard_map/ppermute | solution.py:446
  49.1 37.6 %all-to-all-start.4 = ((bf16[128,16,256]{2,1,0:T(8,128)(2,1)}), bf16[128,16,256]{2,1,0:T(8,128)(2,1)S(1)}, u32[]{:S(2)}, u32[]{:S(2)}) async-start(bf16[128,16,256]{2,1,0:T(8,128)(2,1)} %bitcast.10), calls=%async_computation.4 | async-start | bytes 2097152 | tf_op jit(solution)/shard_map/all_to_all | solution.py:450
  89.5 4.0 %collective-permute-start.5 = (f32[64,2,8,128]{3,2,1,0:T(8,128)S(1)}, f32[64,2,8,128]{3,2,1,0:T(8,128)S(1)}, u32[]{:S(2)}, u32[]{:S(2)}) collective-permute-start(f32[64,2,8,128]{3,2,1,0:T(8,128)S(1)} %get-tuple-element.52), channel_id=1, source_target_pairs={{0,2},{2,0},{1,3},{3,1},{4,6},{6,4},{5,7},{7,5},{8,10},{10,8},{9,1... | collective-permute-start | bytes 1572872 | tf_op jit(solution)/shard_map/ppermute | solution.py:446
  94.3 25.1 %all-to-all-start.5 = ((f32[128,8,128]{2,1,0:T(8,128)}), f32[128,8,128]{2,1,0:T(8,128)S(1)}, u32[]{:S(2)}, u32[]{:S(2)}) async-start(f32[128,8,128]{2,1,0:T(8,128)} %bitcast.12), calls=%async_computation.5 | async-start | bytes 1048576 | tf_op jit(solution)/shard_map/all_to_all | solution.py:450
  119.6 3.6 %collective-permute-start.6 = (f32[4,128]{1,0:T(4,128)S(1)}, f32[4,128]{1,0:T(4,128)S(1)}, u32[]{:S(2)}, u32[]{:S(2)}) collective-permute-start(f32[4,128]{1,0:T(4,128)S(1)} %get-tuple-element.56), channel_id=1, source_target_pairs={{0,2},{2,0},{1,3},{3,1},{4,6},{6,4},{5,7},{7,5},{8,10},{10,8},{9,1... | collective-permute-start | bytes 6152 | tf_op jit(solution)/shard_map/ppermute | solution.py:446

commit v7 on v6

--- a/solution.py
+++ b/solution.py
@@ -466,10 +466,11 @@
     z_table, y_big = expand_yz(core_word, small)
     full = (jnp.max(ranks[0]) >= CHIP_SLOTS) | (jnp.max(ranks[1]) >= LINE_SLOTS)
     full = jnp.where(full, F32(1.0), F32(0.0))[None]
+    slots, z_table, y_big, full = lax.optimization_barrier((slots, z_table, y_big, full))
+    slots = exchange(merge(merge_table, slots), LINES)
     full = full + lax.ppermute(full, "b", [(0, 1), (1, 0)])
-    slots, full = lax.optimization_barrier((slots, full))
-    slots = exchange(merge(merge_table, slots), LINES)
-    slots, z_table, y_big, orbitals = lax.optimization_barrier((slots, z_table, y_big, orbitals))
+    x_small = x_table(y_pair == 0)
+    slots, full, x_small, orbitals = lax.optimization_barrier((slots, full, x_small, orbitals))
     own = order(ranks, slots)
     own = lax.cond(
         full[0] > 0,
@@ -479,7 +480,7 @@
     )
     held = hold(orbitals)
     near, far = fit(core_word, own, sibling(own), z_table, held)
-    x_big = expand_x(x_table(y_pair == 0))
+    x_big = expand_x(x_small)
     screen, mixed = screen_rows(y_pair, z_group * 4)
     screen = pltpu.with_memory_space_constraint(screen, pltpu.HBM)
     planes = y_far(core_word, sibling(far), y_big, y_near(core_word, near, y_big))

time: 124 us -> 122 us (0.984)
  starting transfers between devices: 46.2 us -> 41.7 us
  waiting for transfers between devices: 48 us -> 50.3 us
    all_to_all x4, starting transfers between devices: 30.5 us -> 27.8 us  [exchange(): return lax.all_to_all(blocks, axes, split_axis=0, concat_axis=0, tiled=True)]
    all_to_all x4, waiting for transfers between devices: 43.4 us -> 46 us  [exchange(): return lax.all_to_all(blocks, axes, split_axis=0, concat_axis=0, tiled=True)]
    ppermute x5, starting transfers between devices: 11.9 us -> 10.4 us  [sibling(): return lax.ppermute(block, 'c', [(0, 1), (1, 0)])]
  transfers between devices with their start and end apart: 10 -> 10, of which waited for: 9 -> 8; matrix products, arithmetic and copies ran while one was open for 6% -> 6% of each run, Pallas kernels for 5% -> 5%
where the time goes in v7:
time: 122 us
  waiting for transfers between devices  50.3 us (41%)
  starting transfers between devices  41.7 us (34%)
  Pallas kernels  17.5 us (14%)
  other arithmetic  9.26 us (8%)
  between operations  2.24 us (2%)
    all_to_all x4, waiting for transfers between devices, exchange(): return lax.all_to_all(blocks, axes, split_axis=0, concat_axis=0, tiled=True)  46 us
    all_to_all x4, starting transfers between devices, exchange(): return lax.all_to_all(blocks, axes, split_axis=0, concat_axis=0, tiled=True)  27.8 us
    ppermute x5, starting transfers between devices, sibling(): return lax.ppermute(block, 'c', [(0, 1), (1, 0)])  10.4 us
    pallas_call x1, Pallas kernels, pick(): pl.pallas_call(pick_kernel, out_shape=(half, half, jax.ShapeDtypeStruct((...  4.34 us
    ppermute x5, waiting for transfers between devices, sibling(): return lax.ppermute(block, 'c', [(0, 1), (1, 0)])  3.55 us
    ppermute x1, starting transfers between devices, on_device(): full = full + lax.ppermute(full, 'b', [(0, 1), (1, 0)])  3.43 us
    mul x1, other arithmetic, screen_rows(): return (screen * copies, mixed)  2.93 us
    pallas_call x1, Pallas kernels, gram(): pl.pallas_call(gram_kernel, out_shape=(half, half), in_specs=[pl.BlockSpe...  2.75 us
  transfers between devices with their start and end apart: 10, of which 8 were waited for; matrix products, arithmetic and copies ran while one was open for 6% of the time, Pallas kernels for 5%

profile of v7, /device:TPU:1, one launch (start us, length us, event | category | flops | bytes accessed | tf_op | source)
XLA Modules:
  0.0 121.7 jit_solution(18130547391678071279)
XLA Ops:
  0.0 0.1 pad_add_fusion.place_ref
  0.1 4.3 %pick.1 = (bf16[16,512]{1,0:T(8,128)(2,1)S(1)}, bf16[16,512]{1,0:T(8,128)(2,1)S(1)}, s32[8,256]{1,0:T(8,128)S(1)}, bf16[64,128]{1,0:T(8,128)(2,1)S(1)}) custom-call(s32[3]{0:T(128)S(1)} %pad_add_fusion.place_ref, s32[1,256]{1,0:T(1,128)} %points_ref.1, bf16[1024,2048]{1,0:T(8,128)(2,1)} %orbitals_ref.2), custom_call_target="tpu_custom_call" | custom-call | tf_op jit(solution)/shard_map/pick/pallas_call | solution.py:212
  4.4 3.3 %collective-permute-start.1 = (bf16[16,512]{1,0:T(8,128)(2,1)S(1)}, bf16[16,512]{1,0:T(8,128)(2,1)S(1)}, u32[]{:S(2)}, u32[]{:S(2)}) collective-permute-start(bf16[16,512]{1,0:T(8,128)(2,1)S(1)} %get-tuple-element.41), channel_id=1, source_target_pairs={{0,2},{2,0},{1,3},{3,1},{4,6},{6,4},{5,7},{7,5},{8,10},{10,8},{9,1... | collective-permute-start | bytes 49160 | tf_op jit(solution)/shard_map/ppermute | solution.py:446
  7.7 0.7 slice_reduce_fusion
  8.5 0.3 select_convert_fusion.2.small_ref
  8.7 0.0 collective-permute-done.1
  8.8 0.7 broadcast_in_dim.63
  9.4 6.5 %all-to-all-start.2 = ((bf16[8,16,512]{2,1,0:T(8,128)(2,1)}), bf16[8,16,512]{2,1,0:T(8,128)(2,1)S(1)}, u32[]{:S(2)}, u32[]{:S(2)}) async-start(bf16[8,16,512]{2,1,0:T(8,128)(2,1)} %broadcast_in_dim.63), calls=%async_computation.2 | async-start | bytes 262144 | tf_op jit(solution)/shard_map/all_to_all | solution.py:450
  15.9 1.4 %expand_yz.1 = (bf16[256,256]{1,0:T(8,128)(2,1)S(1)}, bf16[1024,1024]{1,0:T(8,128)(2,1)S(1)}) custom-call(s32[1]{0:T(128)} %bitcast.5.core_ref, bf16[64,64]{1,0:T(8,128)(2,1)S(1)} %select_convert_fusion.2.small_ref), custom_call_target="tpu_custom_call" | custom-call | flops 1073741824 | bytes 2097152 | tf_op jit(solution)/shard_map/expand_yz/pallas_call | solution.py:120
  17.3 0.0 copy-start
  18.6 5.7 %all-to-all-done.2.slots_ref = bf16[8,16,512]{2,1,0:T(8,128)(2,1)S(1)} async-done(((bf16[8,16,512]{2,1,0:T(8,128)(2,1)}), bf16[8,16,512]{2,1,0:T(8,128)(2,1)S(1)}, u32[]{:S(2)}, u32[]{:S(2)}) %all-to-all-start.2) | async-done | bytes 131104 | tf_op jit(solution)/shard_map/all_to_all | solution.py:450
  24.2 1.0 merge.1
  25.2 5.0 %all-to-all-start.3 = ((bf16[8,64,512]{2,1,0:T(8,128)(2,1)}), bf16[8,64,512]{2,1,0:T(8,128)(2,1)S(1)}, u32[]{:S(2)}, u32[]{:S(2)}) async-start(bf16[8,64,512]{2,1,0:T(8,128)(2,1)} %merge.1), calls=%async_computation.3 | async-start | bytes 1048576 | tf_op jit(solution)/shard_map/all_to_all | solution.py:450
  30.3 1.7 %fusion.25.small_ref = bf16[256,256]{1,0:T(8,128)(2,1)S(1)} fusion(s32[256]{0:T(256)S(1)} %get-tuple-element.69, s32[256]{0:T(256)S(1)} %get-tuple-element.70, s32[256]{0:T(256)S(1)} %get-tuple-element.67, s32[256]{0:T(256)S(1)} %get-tuple-element.73, s32[256]{0:T(256)S(1)} %get-tuple-element.68, s32[256]{0:T(256)S(1)} %get-tuple-element.74, ...), kind=kLoop, calls=%fused_computation.76 | loop fusion | flops 5570560 | bytes 137985 | tf_op jit(solution)/shard_map/convert_element_type | solution.py:60
  32.0 3.4 %collective-permute-start.2 = (f32[1]{0:T(128)}, f32[1]{0:T(128)}, u32[]{:S(2)}, u32[]{:S(2)}) collective-permute-start(f32[1]{0:T(128)} %bitcast.8), channel_id=1, source_target_pairs={{0,1},{1,0},{2,3},{3,2},{4,5},{5,4},{6,7},{7,6},{8,9},{9,8},{10,11... | collective-permute-start | bytes 20 | tf_op jit(solution)/shard_map/ppermute | solution.py:471
  35.5 0.7 collective-permute-done.2
  36.9 2.9 %all-to-all-done.3.slots_ref = bf16[8,64,512]{2,1,0:T(8,128)(2,1)S(1)} async-done(((bf16[8,64,512]{2,1,0:T(8,128)(2,1)}), bf16[8,64,512]{2,1,0:T(8,128)(2,1)S(1)}, u32[]{:S(2)}, u32[]{:S(2)}) %all-to-all-start.3) | async-done | bytes 524320 | tf_op jit(solution)/shard_map/all_to_all | solution.py:450
  39.8 0.4 order.1
  40.2 0.0 copy-done
  40.2 1.7 %collective-permute-start.3 = (bf16[512,256]{1,0:T(8,128)(2,1)S(1)}, bf16[512,256]{1,0:T(8,128)(2,1)S(1)}, u32[]{:S(2)}, u32[]{:S(2)}) collective-permute-start(bf16[512,256]{1,0:T(8,128)(2,1)S(1)} %get-tuple-element.83.own_ref), channel_id=1, source_target_pairs={{0,2},{2,0},{1,3},{3,1},{4,6},{6,4},{5,7},{7,5},{8,10},{10,8},{9,1... | collective-permute-start | bytes 786440 | tf_op jit(solution)/shard_map/ppermute | solution.py:446
  42.0 2.2 %hold.1.orbitals_ref = bf16[1024,2048]{1,0:T(8,128)(2,1)S(1)} custom-call(bf16[1024,2048]{1,0:T(8,128)(2,1)} %orbitals_ref.2), custom_call_target="tpu_custom_call" | custom-call | bytes 8388608 | tf_op jit(solution)/shard_map/hold/pallas_call | solution.py:293
  44.2 0.0 collective-permute-done.3.other_ref
  44.2 1.8 %fit.1 = (bf16[32,32,256]{2,1,0:T(8,128)(2,1)S(1)}, bf16[32,32,256]{2,1,0:T(8,128)(2,1)S(1)}) custom-call(s32[1]{0:T(128)} %bitcast.5.core_ref, bf16[512,256]{1,0:T(8,128)(2,1)S(1)} %get-tuple-element.83.own_ref, bf16[512,256]{1,0:T(8,128)(2,1)S(1)} %collective-permute-done.3.other_ref, bf16[256,256]{1,0:T(8,128)(2,1)S(1)} %get-tuple-element.50.table_ref, ...), custom_call_target="tpu_custom_call" | custom-call | tf_op jit(solution)/shard_map/fit/pallas_call | solution.py:326
  46.0 0.1 collective-permute-start.4
  46.1 0.7 y_near.1.part_ref
  46.8 1.2 collective-permute-done.4.far_ref
  48.0 1.7 %y_far.1 = bf16[32,2,2,16,256]{4,3,2,1,0:T(8,128)(2,1)} custom-call(s32[1]{0:T(128)} %bitcast.5.core_ref, bf16[32,32,256]{2,1,0:T(8,128)(2,1)S(1)} %collective-permute-done.4.far_ref, bf16[1024,1024]{1,0:T(8,128)(2,1)S(1)} %get-tuple-element.52.table_ref, f32[2,1024,256]{2,1,0:T(8,128)S(1)} %y_near.1.part_ref), custom_call_target="tpu_custom_call" | custom-call | tf_op jit(solution)/shard_map/y_far/pallas_call | solution.py:367
  49.7 7.6 %all-to-all-start.4 = ((bf16[128,16,256]{2,1,0:T(8,128)(2,1)}), bf16[128,16,256]{2,1,0:T(8,128)(2,1)S(1)}, u32[]{:S(2)}, u32[]{:S(2)}) async-start(bf16[128,16,256]{2,1,0:T(8,128)(2,1)} %bitcast.10), calls=%async_computation.4 | async-start | bytes 2097152 | tf_op jit(solution)/shard_map/all_to_all | solution.py:450
  57.3 0.9 fusion.20
  58.2 1.0 compare_and_fusion
  59.2 2.9 %fusion.8.screens_ref = f32[1024,128]{1,0:T(8,128)} fusion(s32[1024]{0:T(1024)S(1)} %get-tuple-element.76, s32[1024]{0:T(1024)S(1)} %get-tuple-element.78, s32[]{:T(128)S(6)} %mul.77, s32[]{:T(128)S(6)} %select_n.283, s32[1024]{0:T(1024)S(1)} %get-tuple-element.77, s32[1024]{0:T(1024)S(1)} %get-tuple-element.81, s32[1024]{0:T(1024)S(1)} %get-tuple-element.75, ...), kind=kLoop, calls=%fused_computation.34 | loop fusion | flops 9175040 | bytes 551945 | tf_op jit(solution)/shard_map/mul | solution.py:82
  62.2 1.3 %expand_x.1.table_ref = bf16[1024,1024]{1,0:T(8,128)(2,1)S(1)} custom-call(bf16[256,256]{1,0:T(8,128)(2,1)S(1)} %fusion.25.small_ref), custom_call_target="tpu_custom_call" | custom-call | flops 2147483648 | bytes 2097152 | tf_op jit(solution)/shard_map/expand_x/pallas_call | solution.py:152
  63.5 21.1 %all-to-all-done.4 = bf16[128,16,256]{2,1,0:T(8,128)(2,1)S(1)} async-done(((bf16[128,16,256]{2,1,0:T(8,128)(2,1)}), bf16[128,16,256]{2,1,0:T(8,128)(2,1)S(1)}, u32[]{:S(2)}, u32[]{:S(2)}) %all-to-all-start.4) | async-done | bytes 1048608 | tf_op jit(solution)/shard_map/all_to_all | solution.py:450
  84.6 2.7 %gram.1 = (f32[64,2,8,128]{3,2,1,0:T(8,128)S(1)}, f32[64,2,8,128]{3,2,1,0:T(8,128)S(1)}) custom-call(s32[1]{0:T(128)} %bitcast.5.core_ref, bf16[64,2,16,256]{3,2,1,0:T(8,128)(2,1)S(1)} %bitcast.24, bf16[1024,1024]{1,0:T(8,128)(2,1)S(1)} %expand_x.1.table_ref, f32[1024,128]{1,0:T(8,128)} %fusion.8.screens_ref, f32[256,128]{1,0:T(8,128)S(1)} %fusion.40.mixed_ref), custom_call_target="tpu_custom_call" | custom-call | tf_op jit(solution)/shard_map/gram/pallas_call | solution.py:427
  87.3 2.5 %collective-permute-start.5 = (f32[64,2,8,128]{3,2,1,0:T(8,128)S(1)}, f32[64,2,8,128]{3,2,1,0:T(8,128)S(1)}, u32[]{:S(2)}, u32[]{:S(2)}) collective-permute-start(f32[64,2,8,128]{3,2,1,0:T(8,128)S(1)} %get-tuple-element.56), channel_id=1, source_target_pairs={{0,2},{2,0},{1,3},{3,1},{4,6},{6,4},{5,7},{7,5},{8,10},{10,8},{9,1... | collective-permute-start | bytes 1572872 | tf_op jit(solution)/shard_map/ppermute | solution.py:446
  89.8 1.5 %collective-permute-done.5 = f32[64,2,8,128]{3,2,1,0:T(8,128)S(1)} collective-permute-done((f32[64,2,8,128]{3,2,1,0:T(8,128)S(1)}, f32[64,2,8,128]{3,2,1,0:T(8,128)S(1)}, u32[]{:S(2)}, u32[]{:S(2)}) %collective-permute-start.5) | collective-permute-done | bytes 524320 | tf_op jit(solution)/shard_map/ppermute | solution.py:446
  91.4 0.9 add.187
  92.2 8.8 %all-to-all-start.5 = ((f32[128,8,128]{2,1,0:T(8,128)}), f32[128,8,128]{2,1,0:T(8,128)S(1)}, u32[]{:S(2)}, u32[]{:S(2)}) async-start(f32[128,8,128]{2,1,0:T(8,128)} %bitcast.12), calls=%async_computation.5 | async-start | bytes 1048576 | tf_op jit(solution)/shard_map/all_to_all | solution.py:450
  101.0 16.3 %all-to-all-done.5 = f32[128,8,128]{2,1,0:T(8,128)S(1)} async-done(((f32[128,8,128]{2,1,0:T(8,128)}), f32[128,8,128]{2,1,0:T(8,128)S(1)}, u32[]{:S(2)}, u32[]{:S(2)}) %all-to-all-start.5) | async-done | bytes 524320 | tf_op jit(solution)/shard_map/all_to_all | solution.py:450
  117.3 0.1 reduce_sum.21
  117.5 2.8 %collective-permute-start.6 = (f32[4,128]{1,0:T(4,128)S(1)}, f32[4,128]{1,0:T(4,128)S(1)}, u32[]{:S(2)}, u32[]{:S(2)}) collective-permute-start(f32[4,128]{1,0:T(4,128)S(1)} %get-tuple-element.60), channel_id=1, source_target_pairs={{0,2},{2,0},{1,3},{3,1},{4,6},{6,4},{5,7},{7,5},{8,10},{10,8},{9,1... | collective-permute-start | bytes 6152 | tf_op jit(solution)/shard_map/ppermute | solution.py:446
  120.3 0.8 collective-permute-done.6
  121.1 0.6 fusion.55
  (17 shorter events, 0.1 us)
Async XLA Ops:
  4.4 4.3 %collective-permute-start.1 = (bf16[16,512]{1,0:T(8,128)(2,1)S(1)}, bf16[16,512]{1,0:T(8,128)(2,1)S(1)}, u32[]{:S(2)}, u32[]{:S(2)}) collective-permute-start(bf16[16,512]{1,0:T(8,128)(2,1)S(1)} %get-tuple-element.41), channel_id=1, source_target_pairs={{0,2},{2,0},{1,3},{3,1},{4,6},{6,4},{5,7},{7,5},{8,10},{10,8},{9,1... | collective-permute-start | bytes 49160 | tf_op jit(solution)/shard_map/ppermute | solution.py:446
  9.4 14.8 %all-to-all-start.2 = ((bf16[8,16,512]{2,1,0:T(8,128)(2,1)}), bf16[8,16,512]{2,1,0:T(8,128)(2,1)S(1)}, u32[]{:S(2)}, u32[]{:S(2)}) async-start(bf16[8,16,512]{2,1,0:T(8,128)(2,1)} %broadcast_in_dim.63), calls=%async_computation.2 | async-start | bytes 262144 | tf_op jit(solution)/shard_map/all_to_all | solution.py:450
  17.3 22.9 %copy-start = (s32[1,256]{1,0:T(1,128)S(1)}, s32[1,256]{1,0:T(1,128)}, u32[]{:S(2)}) copy-start(s32[1,256]{1,0:T(1,128)} %points_ref.1) | copy-start | bytes 3076
  25.2 14.6 %all-to-all-start.3 = ((bf16[8,64,512]{2,1,0:T(8,128)(2,1)}), bf16[8,64,512]{2,1,0:T(8,128)(2,1)S(1)}, u32[]{:S(2)}, u32[]{:S(2)}) async-start(bf16[8,64,512]{2,1,0:T(8,128)(2,1)} %merge.1), calls=%async_computation.3 | async-start | bytes 1048576 | tf_op jit(solution)/shard_map/all_to_all | solution.py:450
  32.0 4.2 %collective-permute-start.2 = (f32[1]{0:T(128)}, f32[1]{0:T(128)}, u32[]{:S(2)}, u32[]{:S(2)}) collective-permute-start(f32[1]{0:T(128)} %bitcast.8), channel_id=1, source_target_pairs={{0,1},{1,0},{2,3},{3,2},{4,5},{5,4},{6,7},{7,6},{8,9},{9,8},{10,11... | collective-permute-start | bytes 20 | tf_op jit(solution)/shard_map/ppermute | solution.py:471
  40.2 3.9 %collective-permute-start.3 = (bf16[512,256]{1,0:T(8,128)(2,1)S(1)}, bf16[512,256]{1,0:T(8,128)(2,1)S(1)}, u32[]{:S(2)}, u32[]{:S(2)}) collective-permute-start(bf16[512,256]{1,0:T(8,128)(2,1)S(1)} %get-tuple-element.83.own_ref), channel_id=1, source_target_pairs={{0,2},{2,0},{1,3},{3,1},{4,6},{6,4},{5,7},{7,5},{8,10},{10,8},{9,1... | collective-permute-start | bytes 786440 | tf_op jit(solution)/shard_map/ppermute | solution.py:446
  46.0 2.0 %collective-permute-start.4 = (bf16[32,32,256]{2,1,0:T(8,128)(2,1)S(1)}, bf16[32,32,256]{2,1,0:T(8,128)(2,1)S(1)}, u32[]{:S(2)}, u32[]{:S(2)}) collective-permute-start(bf16[32,32,256]{2,1,0:T(8,128)(2,1)S(1)} %get-tuple-element.51), channel_id=1, source_target_pairs={{0,2},{2,0},{1,3},{3,1},{4,6},{6,4},{5,7},{7,5},{8,10},{10,8},{9,1... | collective-permute-start | bytes 1572872 | tf_op jit(solution)/shard_map/ppermute | solution.py:446
  49.7 34.9 %all-to-all-start.4 = ((bf16[128,16,256]{2,1,0:T(8,128)(2,1)}), bf16[128,16,256]{2,1,0:T(8,128)(2,1)S(1)}, u32[]{:S(2)}, u32[]{:S(2)}) async-start(bf16[128,16,256]{2,1,0:T(8,128)(2,1)} %bitcast.10), calls=%async_computation.4 | async-start | bytes 2097152 | tf_op jit(solution)/shard_map/all_to_all | solution.py:450
  87.3 4.0 %collective-permute-start.5 = (f32[64,2,8,128]{3,2,1,0:T(8,128)S(1)}, f32[64,2,8,128]{3,2,1,0:T(8,128)S(1)}, u32[]{:S(2)}, u32[]{:S(2)}) collective-permute-start(f32[64,2,8,128]{3,2,1,0:T(8,128)S(1)} %get-tuple-element.56), channel_id=1, source_target_pairs={{0,2},{2,0},{1,3},{3,1},{4,6},{6,4},{5,7},{7,5},{8,10},{10,8},{9,1... | collective-permute-start | bytes 1572872 | tf_op jit(solution)/shard_map/ppermute | solution.py:446
  92.2 25.1 %all-to-all-start.5 = ((f32[128,8,128]{2,1,0:T(8,128)}), f32[128,8,128]{2,1,0:T(8,128)S(1)}, u32[]{:S(2)}, u32[]{:S(2)}) async-start(f32[128,8,128]{2,1,0:T(8,128)} %bitcast.12), calls=%async_computation.5 | async-start | bytes 1048576 | tf_op jit(solution)/shard_map/all_to_all | solution.py:450
  117.5 3.6 %collective-permute-start.6 = (f32[4,128]{1,0:T(4,128)S(1)}, f32[4,128]{1,0:T(4,128)S(1)}, u32[]{:S(2)}, u32[]{:S(2)}) collective-permute-start(f32[4,128]{1,0:T(4,128)S(1)} %get-tuple-element.60), channel_id=1, source_target_pairs={{0,2},{2,0},{1,3},{3,1},{4,6},{6,4},{5,7},{7,5},{8,10},{10,8},{9,1... | collective-permute-start | bytes 6152 | tf_op jit(solution)/shard_map/ppermute | solution.py:446

commit v8 on v7

--- a/solution.py
+++ b/solution.py
@@ -469,8 +469,7 @@
     slots, z_table, y_big, full = lax.optimization_barrier((slots, z_table, y_big, full))
     slots = exchange(merge(merge_table, slots), LINES)
     full = full + lax.ppermute(full, "b", [(0, 1), (1, 0)])
-    x_small = x_table(y_pair == 0)
-    slots, full, x_small, orbitals = lax.optimization_barrier((slots, full, x_small, orbitals))
+    slots, full, orbitals = lax.optimization_barrier((slots, full, orbitals))
     own = order(ranks, slots)
     own = lax.cond(
         full[0] > 0,
@@ -480,7 +479,7 @@
     )
     held = hold(orbitals)
     near, far = fit(core_word, own, sibling(own), z_table, held)
-    x_big = expand_x(x_small)
+    x_big = expand_x(x_table(y_pair == 0))
     screen, mixed = screen_rows(y_pair, z_group * 4)
     screen = pltpu.with_memory_space_constraint(screen, pltpu.HBM)
     planes = y_far(core_word, sibling(far), y_big, y_near(core_word, near, y_big))

time: 122 us -> 123 us (level)
  no operation moved by 1% of the time
where the time goes in v8:
time: 123 us
  waiting for transfers between devices  51.4 us (42%)
  starting transfers between devices  41.6 us (34%)
  Pallas kernels  17.6 us (14%)
  other arithmetic  9.24 us (8%)
  between operations  2.21 us (2%)
    all_to_all x4, waiting for transfers between devices, exchange(): return lax.all_to_all(blocks, axes, split_axis=0, concat_axis=0, tiled=True)  46.8 us
    all_to_all x4, starting transfers between devices, exchange(): return lax.all_to_all(blocks, axes, split_axis=0, concat_axis=0, tiled=True)  27.7 us
    ppermute x5, starting transfers between devices, sibling(): return lax.ppermute(block, 'c', [(0, 1), (1, 0)])  10.4 us
    pallas_call x1, Pallas kernels, pick(): pl.pallas_call(pick_kernel, out_shape=(half, half, jax.ShapeDtypeStruct((...  4.34 us
    ppermute x5, waiting for transfers between devices, sibling(): return lax.ppermute(block, 'c', [(0, 1), (1, 0)])  3.49 us
    ppermute x1, starting transfers between devices, on_device(): full = full + lax.ppermute(full, 'b', [(0, 1), (1, 0)])  3.42 us
    mul x1, other arithmetic, screen_rows(): return (screen * copies, mixed)  2.93 us
    pallas_call x1, Pallas kernels, gram(): pl.pallas_call(gram_kernel, out_shape=(half, half), in_specs=[pl.BlockSpe...  2.76 us
  transfers between devices with their start and end apart: 10, of which 8 were waited for; matrix products, arithmetic and copies ran while one was open for 6% of the time, Pallas kernels for 5%

profile of v8, /device:TPU:1, one launch (start us, length us, event | category | flops | bytes accessed | tf_op | source)
XLA Modules:
  0.0 122.7 jit_solution(12737463140227168462)
XLA Ops:
  0.0 0.1 pad_add_fusion.place_ref
  0.1 4.3 %pick.1 = (bf16[16,512]{1,0:T(8,128)(2,1)S(1)}, bf16[16,512]{1,0:T(8,128)(2,1)S(1)}, s32[8,256]{1,0:T(8,128)S(1)}, bf16[64,128]{1,0:T(8,128)(2,1)S(1)}) custom-call(s32[3]{0:T(128)S(1)} %pad_add_fusion.place_ref, s32[1,256]{1,0:T(1,128)} %points_ref.1, bf16[1024,2048]{1,0:T(8,128)(2,1)} %orbitals_ref.2), custom_call_target="tpu_custom_call" | custom-call | tf_op jit(solution)/shard_map/pick/pallas_call | solution.py:212
  4.4 3.3 %collective-permute-start.1 = (bf16[16,512]{1,0:T(8,128)(2,1)S(1)}, bf16[16,512]{1,0:T(8,128)(2,1)S(1)}, u32[]{:S(2)}, u32[]{:S(2)}) collective-permute-start(bf16[16,512]{1,0:T(8,128)(2,1)S(1)} %get-tuple-element.40), channel_id=1, source_target_pairs={{0,2},{2,0},{1,3},{3,1},{4,6},{6,4},{5,7},{7,5},{8,10},{10,8},{9,1... | collective-permute-start | bytes 49160 | tf_op jit(solution)/shard_map/ppermute | solution.py:446
  7.7 0.7 slice_reduce_fusion
  9.7 0.0 collective-permute-done.1
  9.8 0.7 broadcast_in_dim.63
  10.4 6.5 %all-to-all-start.2 = ((bf16[8,16,512]{2,1,0:T(8,128)(2,1)}), bf16[8,16,512]{2,1,0:T(8,128)(2,1)S(1)}, u32[]{:S(2)}, u32[]{:S(2)}) async-start(bf16[8,16,512]{2,1,0:T(8,128)(2,1)} %broadcast_in_dim.63), calls=%async_computation.2 | async-start | bytes 262144 | tf_op jit(solution)/shard_map/all_to_all | solution.py:450
  16.9 0.3 select_convert_fusion.2.small_ref
  17.2 1.4 %expand_yz.1 = (bf16[256,256]{1,0:T(8,128)(2,1)S(1)}, bf16[1024,1024]{1,0:T(8,128)(2,1)S(1)}) custom-call(s32[1]{0:T(128)} %bitcast.5.core_ref, bf16[64,64]{1,0:T(8,128)(2,1)S(1)} %select_convert_fusion.2.small_ref), custom_call_target="tpu_custom_call" | custom-call | flops 1073741824 | bytes 2097152 | tf_op jit(solution)/shard_map/expand_yz/pallas_call | solution.py:120
  18.6 0.0 copy-start
  18.6 6.8 %all-to-all-done.2.slots_ref = bf16[8,16,512]{2,1,0:T(8,128)(2,1)S(1)} async-done(((bf16[8,16,512]{2,1,0:T(8,128)(2,1)}), bf16[8,16,512]{2,1,0:T(8,128)(2,1)S(1)}, u32[]{:S(2)}, u32[]{:S(2)}) %all-to-all-start.2) | async-done | bytes 131104 | tf_op jit(solution)/shard_map/all_to_all | solution.py:450
  25.3 1.0 merge.1
  26.3 5.0 %all-to-all-start.3 = ((bf16[8,64,512]{2,1,0:T(8,128)(2,1)}), bf16[8,64,512]{2,1,0:T(8,128)(2,1)S(1)}, u32[]{:S(2)}, u32[]{:S(2)}) async-start(bf16[8,64,512]{2,1,0:T(8,128)(2,1)} %merge.1), calls=%async_computation.3 | async-start | bytes 1048576 | tf_op jit(solution)/shard_map/all_to_all | solution.py:450
  31.4 3.4 %collective-permute-start.2 = (f32[1]{0:T(128)}, f32[1]{0:T(128)}, u32[]{:S(2)}, u32[]{:S(2)}) collective-permute-start(f32[1]{0:T(128)} %bitcast.8), channel_id=1, source_target_pairs={{0,1},{1,0},{2,3},{3,2},{4,5},{5,4},{6,7},{7,6},{8,9},{9,8},{10,11... | collective-permute-start | bytes 20 | tf_op jit(solution)/shard_map/ppermute | solution.py:471
  34.8 1.2 collective-permute-done.2
  36.6 4.4 %all-to-all-done.3.slots_ref = bf16[8,64,512]{2,1,0:T(8,128)(2,1)S(1)} async-done(((bf16[8,64,512]{2,1,0:T(8,128)(2,1)}), bf16[8,64,512]{2,1,0:T(8,128)(2,1)S(1)}, u32[]{:S(2)}, u32[]{:S(2)}) %all-to-all-start.3) | async-done | bytes 524320 | tf_op jit(solution)/shard_map/all_to_all | solution.py:450
  40.9 0.4 order.1
  41.3 0.0 copy-done
  41.3 1.5 %collective-permute-start.3 = (bf16[512,256]{1,0:T(8,128)(2,1)S(1)}, bf16[512,256]{1,0:T(8,128)(2,1)S(1)}, u32[]{:S(2)}, u32[]{:S(2)}) collective-permute-start(bf16[512,256]{1,0:T(8,128)(2,1)S(1)} %get-tuple-element.81.own_ref), channel_id=1, source_target_pairs={{0,2},{2,0},{1,3},{3,1},{4,6},{6,4},{5,7},{7,5},{8,10},{10,8},{9,1... | collective-permute-start | bytes 786440 | tf_op jit(solution)/shard_map/ppermute | solution.py:446
  42.9 2.2 %hold.1.orbitals_ref = bf16[1024,2048]{1,0:T(8,128)(2,1)S(1)} custom-call(bf16[1024,2048]{1,0:T(8,128)(2,1)} %orbitals_ref.2), custom_call_target="tpu_custom_call" | custom-call | bytes 8388608 | tf_op jit(solution)/shard_map/hold/pallas_call | solution.py:293
  45.1 0.0 collective-permute-done.3.other_ref
  45.1 1.8 %fit.1 = (bf16[32,32,256]{2,1,0:T(8,128)(2,1)S(1)}, bf16[32,32,256]{2,1,0:T(8,128)(2,1)S(1)}) custom-call(s32[1]{0:T(128)} %bitcast.5.core_ref, bf16[512,256]{1,0:T(8,128)(2,1)S(1)} %get-tuple-element.81.own_ref, bf16[512,256]{1,0:T(8,128)(2,1)S(1)} %collective-permute-done.3.other_ref, bf16[256,256]{1,0:T(8,128)(2,1)S(1)} %get-tuple-element.49.table_ref, ...), custom_call_target="tpu_custom_call" | custom-call | tf_op jit(solution)/shard_map/fit/pallas_call | solution.py:326
  46.9 0.3 collective-permute-start.4
  47.2 0.7 y_near.1.part_ref
  47.9 1.1 collective-permute-done.4.far_ref
  49.1 1.7 %y_far.1 = bf16[32,2,2,16,256]{4,3,2,1,0:T(8,128)(2,1)} custom-call(s32[1]{0:T(128)} %bitcast.5.core_ref, bf16[32,32,256]{2,1,0:T(8,128)(2,1)S(1)} %collective-permute-done.4.far_ref, bf16[1024,1024]{1,0:T(8,128)(2,1)S(1)} %get-tuple-element.51.table_ref, f32[2,1024,256]{2,1,0:T(8,128)S(1)} %y_near.1.part_ref), custom_call_target="tpu_custom_call" | custom-call | tf_op jit(solution)/shard_map/y_far/pallas_call | solution.py:367
  50.8 7.5 %all-to-all-start.4 = ((bf16[128,16,256]{2,1,0:T(8,128)(2,1)}), bf16[128,16,256]{2,1,0:T(8,128)(2,1)S(1)}, u32[]{:S(2)}, u32[]{:S(2)}) async-start(bf16[128,16,256]{2,1,0:T(8,128)(2,1)} %bitcast.10), calls=%async_computation.4 | async-start | bytes 2097152 | tf_op jit(solution)/shard_map/all_to_all | solution.py:450
  58.3 1.7 %fusion.25.small_ref = bf16[256,256]{1,0:T(8,128)(2,1)S(1)} fusion(s32[256]{0:T(256)S(1)} %get-tuple-element.67, s32[256]{0:T(256)S(1)} %get-tuple-element.68, s32[256]{0:T(256)S(1)} %get-tuple-element.65, s32[256]{0:T(256)S(1)} %get-tuple-element.71, s32[256]{0:T(256)S(1)} %get-tuple-element.66, s32[256]{0:T(256)S(1)} %get-tuple-element.72, ...), kind=kLoop, calls=%fused_computation.76 | loop fusion | flops 5570560 | bytes 137985 | tf_op jit(solution)/shard_map/convert_element_type | solution.py:60
  60.1 1.3 %expand_x.1.table_ref = bf16[1024,1024]{1,0:T(8,128)(2,1)S(1)} custom-call(bf16[256,256]{1,0:T(8,128)(2,1)S(1)} %fusion.25.small_ref), custom_call_target="tpu_custom_call" | custom-call | flops 2147483648 | bytes 2097152 | tf_op jit(solution)/shard_map/expand_x/pallas_call | solution.py:152
  61.4 0.9 fusion.20
  62.3 1.0 compare_and_fusion
  63.3 2.9 %fusion.8.screens_ref = f32[1024,128]{1,0:T(8,128)} fusion(s32[1024]{0:T(1024)S(1)} %get-tuple-element.74, s32[1024]{0:T(1024)S(1)} %get-tuple-element.76, s32[]{:T(128)S(6)} %mul.77, s32[]{:T(128)S(6)} %select_n.283, s32[1024]{0:T(1024)S(1)} %get-tuple-element.75, s32[1024]{0:T(1024)S(1)} %get-tuple-element.79, s32[1024]{0:T(1024)S(1)} %get-tuple-element.73, ...), kind=kLoop, calls=%fused_computation.34 | loop fusion | flops 9175040 | bytes 551945 | tf_op jit(solution)/shard_map/mul | solution.py:82
  66.3 19.3 %all-to-all-done.4 = bf16[128,16,256]{2,1,0:T(8,128)(2,1)S(1)} async-done(((bf16[128,16,256]{2,1,0:T(8,128)(2,1)}), bf16[128,16,256]{2,1,0:T(8,128)(2,1)S(1)}, u32[]{:S(2)}, u32[]{:S(2)}) %all-to-all-start.4) | async-done | bytes 1048608 | tf_op jit(solution)/shard_map/all_to_all | solution.py:450
  85.6 2.8 %gram.1 = (f32[64,2,8,128]{3,2,1,0:T(8,128)S(1)}, f32[64,2,8,128]{3,2,1,0:T(8,128)S(1)}) custom-call(s32[1]{0:T(128)} %bitcast.5.core_ref, bf16[64,2,16,256]{3,2,1,0:T(8,128)(2,1)S(1)} %bitcast.24, bf16[1024,1024]{1,0:T(8,128)(2,1)S(1)} %expand_x.1.table_ref, f32[1024,128]{1,0:T(8,128)} %fusion.8.screens_ref, f32[256,128]{1,0:T(8,128)S(1)} %fusion.40.mixed_ref), custom_call_target="tpu_custom_call" | custom-call | tf_op jit(solution)/shard_map/gram/pallas_call | solution.py:427
  88.3 2.5 %collective-permute-start.5 = (f32[64,2,8,128]{3,2,1,0:T(8,128)S(1)}, f32[64,2,8,128]{3,2,1,0:T(8,128)S(1)}, u32[]{:S(2)}, u32[]{:S(2)}) collective-permute-start(f32[64,2,8,128]{3,2,1,0:T(8,128)S(1)} %get-tuple-element.54), channel_id=1, source_target_pairs={{0,2},{2,0},{1,3},{3,1},{4,6},{6,4},{5,7},{7,5},{8,10},{10,8},{9,1... | collective-permute-start | bytes 1572872 | tf_op jit(solution)/shard_map/ppermute | solution.py:446
  90.8 1.5 %collective-permute-done.5 = f32[64,2,8,128]{3,2,1,0:T(8,128)S(1)} collective-permute-done((f32[64,2,8,128]{3,2,1,0:T(8,128)S(1)}, f32[64,2,8,128]{3,2,1,0:T(8,128)S(1)}, u32[]{:S(2)}, u32[]{:S(2)}) %collective-permute-start.5) | collective-permute-done | bytes 524320 | tf_op jit(solution)/shard_map/ppermute | solution.py:446
  92.4 0.9 add.187
  93.2 8.8 %all-to-all-start.5 = ((f32[128,8,128]{2,1,0:T(8,128)}), f32[128,8,128]{2,1,0:T(8,128)S(1)}, u32[]{:S(2)}, u32[]{:S(2)}) async-start(f32[128,8,128]{2,1,0:T(8,128)} %bitcast.12), calls=%async_computation.5 | async-start | bytes 1048576 | tf_op jit(solution)/shard_map/all_to_all | solution.py:450
  102.0 16.3 %all-to-all-done.5 = f32[128,8,128]{2,1,0:T(8,128)S(1)} async-done(((f32[128,8,128]{2,1,0:T(8,128)}), f32[128,8,128]{2,1,0:T(8,128)S(1)}, u32[]{:S(2)}, u32[]{:S(2)}) %all-to-all-start.5) | async-done | bytes 524320 | tf_op jit(solution)/shard_map/all_to_all | solution.py:450
  118.3 0.1 reduce_sum.21
  118.5 2.8 %collective-permute-start.6 = (f32[4,128]{1,0:T(4,128)S(1)}, f32[4,128]{1,0:T(4,128)S(1)}, u32[]{:S(2)}, u32[]{:S(2)}) collective-permute-start(f32[4,128]{1,0:T(4,128)S(1)} %get-tuple-element.58), channel_id=1, source_target_pairs={{0,2},{2,0},{1,3},{3,1},{4,6},{6,4},{5,7},{7,5},{8,10},{10,8},{9,1... | collective-permute-start | bytes 6152 | tf_op jit(solution)/shard_map/ppermute | solution.py:446
  121.3 0.8 collective-permute-done.6
  122.1 0.6 fusion.55
  (17 shorter events, 0.1 us)
Async XLA Ops:
  4.4 5.3 %collective-permute-start.1 = (bf16[16,512]{1,0:T(8,128)(2,1)S(1)}, bf16[16,512]{1,0:T(8,128)(2,1)S(1)}, u32[]{:S(2)}, u32[]{:S(2)}) collective-permute-start(bf16[16,512]{1,0:T(8,128)(2,1)S(1)} %get-tuple-element.40), channel_id=1, source_target_pairs={{0,2},{2,0},{1,3},{3,1},{4,6},{6,4},{5,7},{7,5},{8,10},{10,8},{9,1... | collective-permute-start | bytes 49160 | tf_op jit(solution)/shard_map/ppermute | solution.py:446
  10.4 14.9 %all-to-all-start.2 = ((bf16[8,16,512]{2,1,0:T(8,128)(2,1)}), bf16[8,16,512]{2,1,0:T(8,128)(2,1)S(1)}, u32[]{:S(2)}, u32[]{:S(2)}) async-start(bf16[8,16,512]{2,1,0:T(8,128)(2,1)} %broadcast_in_dim.63), calls=%async_computation.2 | async-start | bytes 262144 | tf_op jit(solution)/shard_map/all_to_all | solution.py:450
  18.6 22.7 %copy-start = (s32[1,256]{1,0:T(1,128)S(1)}, s32[1,256]{1,0:T(1,128)}, u32[]{:S(2)}) copy-start(s32[1,256]{1,0:T(1,128)} %points_ref.1) | copy-start | bytes 3076
  26.3 14.6 %all-to-all-start.3 = ((bf16[8,64,512]{2,1,0:T(8,128)(2,1)}), bf16[8,64,512]{2,1,0:T(8,128)(2,1)S(1)}, u32[]{:S(2)}, u32[]{:S(2)}) async-start(bf16[8,64,512]{2,1,0:T(8,128)(2,1)} %merge.1), calls=%async_computation.3 | async-start | bytes 1048576 | tf_op jit(solution)/shard_map/all_to_all | solution.py:450
  31.4 4.6 %collective-permute-start.2 = (f32[1]{0:T(128)}, f32[1]{0:T(128)}, u32[]{:S(2)}, u32[]{:S(2)}) collective-permute-start(f32[1]{0:T(128)} %bitcast.8), channel_id=1, source_target_pairs={{0,1},{1,0},{2,3},{3,2},{4,5},{5,4},{6,7},{7,6},{8,9},{9,8},{10,11... | collective-permute-start | bytes 20 | tf_op jit(solution)/shard_map/ppermute | solution.py:471
  41.3 3.8 %collective-permute-start.3 = (bf16[512,256]{1,0:T(8,128)(2,1)S(1)}, bf16[512,256]{1,0:T(8,128)(2,1)S(1)}, u32[]{:S(2)}, u32[]{:S(2)}) collective-permute-start(bf16[512,256]{1,0:T(8,128)(2,1)S(1)} %get-tuple-element.81.own_ref), channel_id=1, source_target_pairs={{0,2},{2,0},{1,3},{3,1},{4,6},{6,4},{5,7},{7,5},{8,10},{10,8},{9,1... | collective-permute-start | bytes 786440 | tf_op jit(solution)/shard_map/ppermute | solution.py:446
  46.9 2.2 %collective-permute-start.4 = (bf16[32,32,256]{2,1,0:T(8,128)(2,1)S(1)}, bf16[32,32,256]{2,1,0:T(8,128)(2,1)S(1)}, u32[]{:S(2)}, u32[]{:S(2)}) collective-permute-start(bf16[32,32,256]{2,1,0:T(8,128)(2,1)S(1)} %get-tuple-element.50), channel_id=1, source_target_pairs={{0,2},{2,0},{1,3},{3,1},{4,6},{6,4},{5,7},{7,5},{8,10},{10,8},{9,1... | collective-permute-start | bytes 1572872 | tf_op jit(solution)/shard_map/ppermute | solution.py:446
  50.8 34.8 %all-to-all-start.4 = ((bf16[128,16,256]{2,1,0:T(8,128)(2,1)}), bf16[128,16,256]{2,1,0:T(8,128)(2,1)S(1)}, u32[]{:S(2)}, u32[]{:S(2)}) async-start(bf16[128,16,256]{2,1,0:T(8,128)(2,1)} %bitcast.10), calls=%async_computation.4 | async-start | bytes 2097152 | tf_op jit(solution)/shard_map/all_to_all | solution.py:450
  88.3 4.0 %collective-permute-start.5 = (f32[64,2,8,128]{3,2,1,0:T(8,128)S(1)}, f32[64,2,8,128]{3,2,1,0:T(8,128)S(1)}, u32[]{:S(2)}, u32[]{:S(2)}) collective-permute-start(f32[64,2,8,128]{3,2,1,0:T(8,128)S(1)} %get-tuple-element.54), channel_id=1, source_target_pairs={{0,2},{2,0},{1,3},{3,1},{4,6},{6,4},{5,7},{7,5},{8,10},{10,8},{9,1... | collective-permute-start | bytes 1572872 | tf_op jit(solution)/shard_map/ppermute | solution.py:446
  93.2 25.1 %all-to-all-start.5 = ((f32[128,8,128]{2,1,0:T(8,128)}), f32[128,8,128]{2,1,0:T(8,128)S(1)}, u32[]{:S(2)}, u32[]{:S(2)}) async-start(f32[128,8,128]{2,1,0:T(8,128)} %bitcast.12), calls=%async_computation.5 | async-start | bytes 1048576 | tf_op jit(solution)/shard_map/all_to_all | solution.py:450
  118.5 3.6 %collective-permute-start.6 = (f32[4,128]{1,0:T(4,128)S(1)}, f32[4,128]{1,0:T(4,128)S(1)}, u32[]{:S(2)}, u32[]{:S(2)}) collective-permute-start(f32[4,128]{1,0:T(4,128)S(1)} %get-tuple-element.58), channel_id=1, source_target_pairs={{0,2},{2,0},{1,3},{3,1},{4,6},{6,4},{5,7},{7,5},{8,10},{10,8},{9,1... | collective-permute-start | bytes 6152 | tf_op jit(solution)/shard_map/ppermute | solution.py:446
